TPU v7x, 32 devices: a whole 2x2x4 slice. The times are simulated.
32 devices in a mesh: section: 2 (over x), frame: 4 (over z), head: 4 (over y, core).
Axes of the slice: x: 2, y: 2, z: 4, core: 2. Of those that a mesh axis runs over, the one named last changes fastest.
Arguments:
- inputs: bfloat16 [2, 2, 16, 128, 3072], P('section', None, 'frame'), may hold values from -45 to 45
- upstream: bfloat16 [2, 16, 128, 3072], P(None, 'frame'), may hold values from -6 to 6
- norm_gain: float32 [2, 3072], P('section'), may hold values from 0.5 to 2
- head_gain: float32 [2, 2, 128], P('section'), may hold values from 0.5 to 2
- w_query: bfloat16 [2, 3072, 3072], P('section', 'frame', 'head'), may hold values from -0.109375 to 0.109375
- w_key: bfloat16 [2, 3072, 3072], P('section', 'frame', 'head'), may hold values from -0.109375 to 0.109375
- w_value: bfloat16 [2, 3072, 3072], P('section', 'frame', 'head'), may hold values from -0.109375 to 0.109375
- w_out: bfloat16 [2, 3072, 3072], P('section', 'head', 'frame'), may hold values from -0.109375 to 0.109375
Outputs:
- input_grads: bfloat16 [2, 2, 16, 128, 3072], P('section', None, 'frame', None, 'head')
All inputs are finite; a program needn't handle non-finite values.
Results may differ from a plain program's by a relative error of at most 0.014.
Values may be sent and summed in bfloat16 or wider, within the bound.
No kernel may reach another device: no remote copies, remote signals or barrier semaphores. Data moves between devices by JAX's collectives and lax.ppermute only.
A program may use at most 192 MiB of HBM per device.

v0:
```python
import jax
import jax.numpy as jnp
from jax import lax
from jax.sharding import PartitionSpec as P

FRAMES = 16


EPS = 1e-06


def from_behind(value, axis, steps):
    count = lax.axis_size(axis)
    initial, last = (max(0, -steps), min(count, count - steps))
    return lax.ppermute(value, axis, [(source, source + steps) for source in range(initial, last)])


def attend_back(query_low, key_rows, value_low, grad_out):
    scores = jnp.einsum("blhd,bmhd->bhlm", query_low, key_rows, preferred_element_type=jnp.float32)
    expo_scores = jnp.exp(scores)
    probs_full = expo_scores / jnp.sum(expo_scores, axis=-1, keepdims=True)
    probs_low = probs_full.astype(jnp.bfloat16)
    grad_probs = jnp.einsum(
        "blhd,bmhd->bhlm", grad_out, value_low, preferred_element_type=jnp.float32
    )
    inner_sum = jnp.sum(probs_full * grad_probs, axis=-1, keepdims=True)
    dscore = (probs_full * (grad_probs - inner_sum)).astype(jnp.bfloat16)
    dquery = jnp.einsum("bhlm,bmhd->blhd", dscore, key_rows, preferred_element_type=jnp.float32)
    grad_key = jnp.einsum("bhlm,blhd->bmhd", dscore, query_low, preferred_element_type=jnp.float32)
    dvalue = jnp.einsum("bhlm,blhd->bmhd", probs_low, grad_out, preferred_element_type=jnp.float32)
    return (dquery.astype(jnp.bfloat16), grad_key.astype(jnp.bfloat16), dvalue.astype(jnp.bfloat16))


def head_norm(raw_rows):
    scale_rows = lax.rsqrt(jnp.mean(raw_rows * raw_rows, axis=-1, keepdims=True) + EPS)
    return (raw_rows * scale_rows, scale_rows)


def norm_back(grad_low, normal_hat, scale_rows, gain_vec):
    grad_hat = grad_low.astype(jnp.float32) * gain_vec
    inner_mean = jnp.mean(grad_hat * normal_hat, axis=-1, keepdims=True)
    return (scale_rows * (grad_hat - normal_hat * inner_mean)).astype(jnp.bfloat16)


def contract_last(left, right):
    return lax.dot_general(
        left, right, (((1,), (1,)), ((), ())), preferred_element_type=jnp.float32
    )


def on_device(inputs, upstream, norm_gain, head_gain, w_query, w_key, w_value, w_out):
    section_index = lax.axis_index("section")
    on_last = section_index == 1
    query_full, key_full, value_full = (
        lax.all_gather(w_query[0], "frame", axis=0, tiled=True),
        lax.all_gather(w_key[0], "frame", axis=0, tiled=True),
        lax.all_gather(w_value[0], "frame", axis=0, tiled=True),
    )
    out_full = lax.all_gather(w_out[0], "frame", axis=1, tiled=True)
    gain_row = norm_gain[0]
    head_gains = head_gain[0]
    head_dim = head_gains.shape[-1]
    local_width = query_full.shape[1]
    local_heads = local_width // head_dim
    batches = inputs.shape[1]
    frames = inputs.shape[2]
    patches = inputs.shape[3]
    feat_width = inputs.shape[4]
    row_count = frames * patches
    share_width = feat_width // lax.axis_size("head")
    my_head = lax.axis_index("head")
    query_gain = head_gains[0] * head_dim ** (-0.5)

    def forward_state(saved_rows):
        flat_rows = saved_rows.reshape(row_count, feat_width).astype(jnp.float32)
        inv_rms = lax.rsqrt(jnp.mean(flat_rows * flat_rows, axis=-1, keepdims=True) + EPS)
        normed = flat_rows * inv_rms
        normed_low = (normed * gain_row).astype(jnp.bfloat16)

        def project(weight):
            return jnp.dot(normed_low, weight, preferred_element_type=jnp.float32).reshape(
                frames, patches, local_heads, head_dim
            )

        query_hat, query_scale = head_norm(project(query_full))
        key_hat, key_scale = head_norm(project(key_full))
        value_low = project(value_full).astype(jnp.bfloat16)
        query_low = (query_hat * query_gain).astype(jnp.bfloat16)
        key_low = (key_hat * head_gains[1]).astype(jnp.bfloat16)
        return (
            normed,
            inv_rms,
            query_hat,
            query_scale,
            key_hat,
            key_scale,
            query_low,
            key_low,
            value_low,
        )

    def attn_grad(grad_in):
        grad_attn = contract_last(grad_in.reshape(row_count, feat_width), out_full)
        return grad_attn.astype(jnp.bfloat16).reshape(frames, patches, local_heads, head_dim)

    def finish(state, grad_in, dquery, grad_key, dvalue):
        normed, inv_rms, query_hat, query_scale, key_hat, key_scale = state[:6]
        dquery_raw = norm_back(dquery, query_hat, query_scale, query_gain).reshape(
            row_count, local_width
        )
        dkey_raw = norm_back(grad_key, key_hat, key_scale, head_gains[1]).reshape(
            row_count, local_width
        )
        dvalue_rows = dvalue.reshape(row_count, local_width)
        dnorm = (
            contract_last(dquery_raw, query_full)
            + contract_last(dkey_raw, key_full)
            + contract_last(dvalue_rows, value_full)
        )
        grad_hat = dnorm * gain_row
        term_rows = inv_rms * (
            grad_hat - normed * jnp.mean(grad_hat * normed, axis=-1, keepdims=True)
        )
        term_low = term_rows.astype(jnp.bfloat16).astype(jnp.float32)
        grad_rows = grad_in.reshape(row_count, feat_width)
        summed = lax.psum(term_low.astype(jnp.bfloat16), "head").astype(jnp.float32)
        full_rows = (grad_rows.astype(jnp.float32) + summed).astype(jnp.bfloat16)
        own_part = lax.dynamic_slice_in_dim(full_rows, my_head * share_width, share_width, 1)
        return (
            own_part.reshape(frames, patches, share_width),
            full_rows.reshape(frames, patches, full_rows.shape[-1]),
        )

    def spatial_branch(saved_rows, fresh_grad, received):
        state = forward_state(saved_rows)
        grad_attn = attn_grad(fresh_grad)
        dquery, grad_key, dvalue = attend_back(state[6], state[7], state[8], grad_attn)
        return finish(state, fresh_grad, dquery, grad_key, dvalue)

    def temporal_branch(saved_rows, fresh_grad, received):
        state = forward_state(saved_rows)
        grad_attn = attn_grad(received)
        query_low = lax.all_to_all(state[6], "frame", split_axis=1, concat_axis=0, tiled=True)
        key_low = lax.all_to_all(state[7], "frame", split_axis=1, concat_axis=0, tiled=True)
        value_low = lax.all_to_all(state[8], "frame", split_axis=1, concat_axis=0, tiled=True)
        grad_out = lax.all_to_all(grad_attn, "frame", split_axis=1, concat_axis=0, tiled=True)
        total_frames = query_low.shape[0]
        few_patches = query_low.shape[1]
        item_count = query_low.shape[2]
        clip_count = total_frames // FRAMES

        def into_time(array_in):
            shaped = array_in.reshape(clip_count, FRAMES, few_patches, item_count, head_dim)
            return shaped.transpose(0, 2, 1, 3, 4).reshape(
                clip_count * few_patches, FRAMES, item_count, head_dim
            )

        def out_time(array_in):
            shaped = array_in.reshape(clip_count, few_patches, FRAMES, item_count, head_dim)
            return shaped.transpose(0, 2, 1, 3, 4).reshape(
                total_frames, few_patches, item_count, head_dim
            )

        dquery, grad_key, dvalue = attend_back(
            into_time(query_low), into_time(key_low), into_time(value_low), into_time(grad_out)
        )
        dquery, grad_key, dvalue = (
            lax.all_to_all(out_time(dquery), "frame", split_axis=0, concat_axis=1, tiled=True),
            lax.all_to_all(out_time(grad_key), "frame", split_axis=0, concat_axis=1, tiled=True),
            lax.all_to_all(out_time(dvalue), "frame", split_axis=0, concat_axis=1, tiled=True),
        )
        return finish(state, received, dquery, grad_key, dvalue)

    received = jnp.zeros((frames, patches, feat_width), jnp.bfloat16)
    results = []
    for tick_index in range(batches + 1):
        fresh_grad = upstream[min(tick_index, batches - 1)]
        slot_index = jnp.clip(tick_index - 1 + section_index, 0, batches - 1)
        saved_rows = lax.dynamic_index_in_dim(inputs[0], slot_index, 0, keepdims=False)
        own_part, passed = lax.cond(
            on_last, spatial_branch, temporal_branch, saved_rows, fresh_grad, received
        )
        results.append(own_part)
        if tick_index < batches:
            received = from_behind(passed, "section", -1)
    late_part = jnp.stack(results[:batches])
    early_part = jnp.stack(results[1:])
    return jnp.where(on_last, late_part, early_part)[None]


def solution(mesh):
    in_specs = (
        P("section", None, "frame", None, None),
        P(None, "frame", None, None),
        P("section", None),
        P("section", None, None),
        P("section", "frame", "head"),
        P("section", "frame", "head"),
        P("section", "frame", "head"),
        P("section", "head", "frame"),
    )
    out_specs = P("section", None, "frame", None, "head")
    return jax.shard_map(
        on_device, mesh=mesh, in_specs=in_specs, out_specs=out_specs, check_vma=False
    )
```

profile of v0, /device:TPU:0, one launch (start us, length us, event | category | flops | bytes accessed | tf_op | source)
XLA Modules:
  0.0 1428.0 jit_solution(9958134378283620044)
XLA Ops:
  12.9 7.4 dynamic-slice_bitcast_fusion
  20.4 80.7 %all-gather.13.cloned.1.call-done = bf16[1,768,3072]{2,1,0:T(8,128)(2,1)} async-done(((bf16[1,768,768]{2,1,0:T(8,128)(2,1)}), bf16[1,768,3072]{2,1,0:T(8,128)(2,1)}) %all-gather.13.cloned.1.call-update) | async-done | bytes 4718608 | tf_op jit(solution)/shard_map/all_gather | solution.py:59
  101.1 89.4 %all-gather.9.cloned.1.call-done = bf16[1,3072,768]{1,2,0:T(8,128)(2,1)} async-done(((bf16[1,768,768]{1,2,0:T(8,128)(2,1)}), bf16[1,3072,768]{1,2,0:T(8,128)(2,1)}) %all-gather.9.cloned.1.call-update) | async-done | bytes 4718608 | tf_op jit(solution)/shard_map/all_gather | solution.py:55
  190.5 89.4 %all-gather.11.cloned.1.call-done = bf16[1,3072,768]{1,2,0:T(8,128)(2,1)} async-done(((bf16[1,768,768]{1,2,0:T(8,128)(2,1)}), bf16[1,3072,768]{1,2,0:T(8,128)(2,1)}) %all-gather.11.cloned.1.call-update) | async-done | bytes 4718608 | tf_op jit(solution)/shard_map/all_gather | solution.py:56
  279.9 89.3 %all-gather.15.cloned.1.call-done = bf16[1,3072,768]{1,2,0:T(8,128)(2,1)} async-done(((bf16[1,768,768]{1,2,0:T(8,128)(2,1)}), bf16[1,3072,768]{1,2,0:T(8,128)(2,1)}) %all-gather.15.cloned.1.call-update) | async-done | bytes 4718608 | tf_op jit(solution)/shard_map/all_gather | solution.py:57
  369.2 306.5 %conditional.3 = (bf16[512,3072]{1,0:T(8,128)(2,1)}, bf16[512,3072]{1,0:T(8,128)(2,1)}, s32[]{:T(128)}, s32[]{:T(128)}, s32[]{:T(128)}, /*index=5*/s32[]{:T(128)}, s32[]{:T(128)}) conditional(s32[]{:T(128)} %convert_element_type.528, (bf16[4,128,3072]{2,1,0:T(8,128)(2,1)}, f32[1,3072]{1,0:T(1,128)S(1)}, bf16[3072,768]{0,1:T(8,128)(2,1)}, ...), branch_computations={%region_0.10_spmd, %region_10.20_spmd} | conditional | flops 17487505408 | bytes 333823616 | solution.py:180
  372.1 5.4 convolution_convert_fusion.3
  383.1 5.9 fusion.3
  394.9 8.8 all-to-all-done.3
  407.8 5.7 multiply_reduce_fusion.6
  418.1 9.5 all-to-all-done.2
  427.6 4.4 all-to-all-start.1
  432.0 5.7 multiply_reduce_fusion.5
  442.3 9.3 all-to-all-done.1
  463.8 11.7 all-to-all-done
  496.4 16.3 %all-to-all-done.4 = bf16[16,32,6,128]{3,1,2,0:T(8,128)(2,1)} async-done(((bf16[16,32,6,128]{3,1,2,0:T(8,128)(2,1)}), bf16[16,32,6,128]{3,1,2,0:T(8,128)(2,1)}, u32[]{:S(2)}, u32[]{:S(2)}) %all-to-all-start.4) | async-done | bytes 786464 | tf_op jit(solution)/shard_map/cond/branch_0_fun/all_to_all | solution.py:168
  525.7 10.9 all-to-all-done.6
  547.2 6.9 fusion.14
  554.1 6.3 all-to-all-done.5
  570.1 7.2 fusion.11
  577.3 7.7 multiply_reduce_fusion
  588.7 66.7 %all-reduce.7.cloned.1.call-done = bf16[512,3072]{1,0:T(8,128)(2,1)} async-done(((bf16[512,3072]{1,0:T(8,128)(2,1)}), bf16[512,3072]{1,0:T(8,128)(2,1)}) %all-reduce.7.cloned.1.call-update) | async-done | bytes 3145744 | tf_op jit(solution)/shard_map/cond/branch_0_fun/psum | solution.py:126
  680.8 66.7 %collective-permute-done = bf16[4,128,3072]{2,1,0:T(8,128)(2,1)S(1)} collective-permute-done((bf16[4,128,3072]{2,1,0:T(8,128)(2,1)}, bf16[4,128,3072]{2,1,0:T(8,128)(2,1)S(1)}, u32[]{:S(2)}, u32[]{:S(2)}) %collective-permute-start) | collective-permute-done | bytes 3145760 | tf_op jit(solution)/shard_map/ppermute | solution.py:15
  747.5 303.8 %conditional.4 = (bf16[512,3072]{1,0:T(8,128)(2,1)}, bf16[512,3072]{1,0:T(8,128)(2,1)}, s32[]{:T(128)}, s32[]{:T(128)}, s32[]{:T(128)}, /*index=5*/s32[]{:T(128)}, s32[]{:T(128)}) conditional(s32[]{:T(128)} %convert_element_type.528, (bf16[4,128,3072]{2,1,0:T(8,128)(2,1)S(1)}, bf16[4,128,3072]{2,1,0:T(8,128)(2,1)S(1)}, f32[1,3072]{1,0:T(1,128)S(1)}, ...), branch_computations={%region_20.30_spmd, %region_30.40_spmd} | conditional | flops 17487505408 | bytes 323083040 | solution.py:180
  750.0 5.4 convolution_convert_fusion.12
  756.9 4.6 all-to-all-start.10
  761.5 6.8 convolution_convert_fusion.13
  774.2 6.5 all-to-all-done.10
  784.9 4.7 multiply_reduce_fusion.18
  794.2 10.4 all-to-all-done.9
  808.7 4.7 multiply_reduce_fusion.17
  818.0 10.4 all-to-all-done.8
  828.4 4.4 all-to-all-start.7
  840.7 11.8 all-to-all-done.7
  873.4 16.3 %all-to-all-done.11 = bf16[16,32,6,128]{3,1,2,0:T(8,128)(2,1)} async-done(((bf16[16,32,6,128]{3,1,2,0:T(8,128)(2,1)}), bf16[16,32,6,128]{3,1,2,0:T(8,128)(2,1)}, u32[]{:S(2)}, u32[]{:S(2)}) %all-to-all-start.11) | async-done | bytes 786464 | tf_op jit(solution)/shard_map/cond/branch_0_fun/all_to_all | solution.py:168
  889.7 4.2 all-to-all-start.13
  902.7 10.8 all-to-all-done.13
  924.0 6.9 fusion.64
  930.9 6.5 all-to-all-done.12
  947.0 4.7 fusion.61
  951.8 5.0 multiply_reduce_fusion.12
  960.2 66.4 %all-reduce.11.cloned.1.call-done = bf16[512,3072]{1,0:T(8,128)(2,1)} async-done(((bf16[512,3072]{1,0:T(8,128)(2,1)}), bf16[512,3072]{1,0:T(8,128)(2,1)}) %all-reduce.11.cloned.1.call-update) | async-done | bytes 3145744 | tf_op jit(solution)/shard_map/cond/branch_0_fun/psum | solution.py:126
  1026.6 4.7 add_convert_fusion.1
  1058.0 65.6 %collective-permute-done.1 = bf16[4,128,3072]{2,1,0:T(8,128)(2,1)} collective-permute-done((bf16[4,128,3072]{2,1,0:T(8,128)(2,1)}, bf16[4,128,3072]{2,1,0:T(8,128)(2,1)}, u32[]{:S(2)}, u32[]{:S(2)}) %collective-permute-start.1) | collective-permute-done | bytes 3145760 | tf_op jit(solution)/shard_map/ppermute | solution.py:15
  1123.6 294.0 %conditional.5 = (bf16[1,1,4,128,768]{4,3,2,1,0:T(8,128)(2,1)S(1)}) conditional(s32[]{:T(128)} %convert_element_type.528, (bf16[4,128,3072]{2,1,0:T(8,128)(2,1)}, bf16[4,128,3072]{2,1,0:T(8,128)(2,1)S(1)}, f32[1,3072]{1,0:T(1,128)S(1)}, bf16[3072,768]{0,1:T(8,128)(2,1)}, bf16[3072,768]{0,1:T(8,128)(2,1)}, /*index=5*/f32[2,128]{1,0:T(2,128)S(1)}, ...), branch_computations={%region_40.50_spmd, %region_50.60_spmd} | conditional | flops 17482786816 | bytes 284547776 | solution.py:180
  1123.6 6.9 convolution_convert_fusion.23
  1136.3 4.6 all-to-all-start.16
  1141.6 5.4 convolution_convert_fusion.22
  1148.5 11.6 all-to-all-done.16
  1160.1 4.2 all-to-all-start.17
  1164.3 4.7 multiply_reduce_fusion.30
  1173.6 10.3 all-to-all-done.17
  1184.0 4.6 all-to-all-start.15
  1188.6 4.7 multiply_reduce_fusion.29
  1197.8 10.4 all-to-all-done.15
  1220.3 11.7 all-to-all-done.14
  1253.0 16.3 %all-to-all-done.18 = bf16[16,32,6,128]{3,1,2,0:T(8,128)(2,1)} async-done(((bf16[16,32,6,128]{3,1,2,0:T(8,128)(2,1)}), bf16[16,32,6,128]{3,1,2,0:T(8,128)(2,1)}, u32[]{:S(2)}, u32[]{:S(2)}) %all-to-all-start.18) | async-done | bytes 786464 | tf_op jit(solution)/shard_map/cond/branch_0_fun/all_to_all | solution.py:168
  1269.3 4.2 all-to-all-start.20
  1282.3 10.8 all-to-all-done.20
  1303.5 6.9 fusion.113
  1310.5 6.5 all-to-all-done.19
  1326.6 4.7 fusion.110
  1331.4 5.0 multiply_reduce_fusion.24
  1339.8 66.4 %all-reduce.15.cloned.1.call-done = bf16[512,3072]{1,0:T(8,128)(2,1)} async-done(((bf16[512,3072]{1,0:T(8,128)(2,1)}), bf16[512,3072]{1,0:T(8,128)(2,1)}) %all-reduce.15.cloned.1.call-update) | async-done | bytes 3145744 | tf_op jit(solution)/shard_map/cond/branch_0_fun/psum | solution.py:126
  (274 shorter events, 298.1 us)
Async XLA Ops:
  6.5 3.3 copy-start.55
  6.5 94.5 %all-gather.13.cloned.1.call-start = ((), (), s32[]{:S(2)}) async-start(), calls=%async_computation.29 | async-start | bytes 5898240 | tf_op jit(solution)/shard_map/all_gather | solution.py:59
  7.3 4.1 copy-start.56
  7.3 183.2 %all-gather.9.cloned.1.call-start = ((), (), s32[]{:S(2)}) async-start(), calls=%async_computation.27 | async-start | bytes 5898240 | tf_op jit(solution)/shard_map/all_gather | solution.py:55
  9.8 3.1 copy-start.60
  9.8 270.1 %all-gather.11.cloned.1.call-start = ((), (), s32[]{:S(2)}) async-start(), calls=%async_computation.28 | async-start | bytes 5898240 | tf_op jit(solution)/shard_map/all_gather | solution.py:56
  11.4 357.9 %all-gather.15.cloned.1.call-start = ((), (), s32[]{:S(2)}) async-start(), calls=%async_computation.30 | async-start | bytes 5898240 | tf_op jit(solution)/shard_map/all_gather | solution.py:57
  12.9 356.3 %copy-start.51 = (f32[1,3072]{1,0:T(1,128)S(1)}, f32[1,3072]{1,0:T(1,128)}, u32[]{:S(2)}) copy-start(f32[1,3072]{1,0:T(1,128)} %param.16) | copy-start | bytes 36868
  369.2 2.8 copy-start.1
  378.9 24.7 %all-to-all-start.3 = ((bf16[4,128,6,128]{3,0,2,1:T(4,128)(2,1)}), bf16[4,128,6,128]{3,0,2,1:T(4,128)(2,1)}, u32[]{:S(2)}, u32[]{:S(2)}) async-start(bf16[4,128,6,128]{3,0,2,1:T(4,128)(2,1)} %copy.441), calls=%async_computation.3 | async-start | bytes 1572864 | tf_op jit(solution)/shard_map/cond/branch_0_fun/all_to_all | solution.py:145
  403.6 23.9 %all-to-all-start.2 = ((bf16[4,128,6,128]{3,0,2,1:T(4,128)(2,1)}), bf16[4,128,6,128]{3,0,2,1:T(4,128)(2,1)}, u32[]{:S(2)}, u32[]{:S(2)}) async-start(bf16[4,128,6,128]{3,0,2,1:T(4,128)(2,1)} %copy.438), calls=%async_computation.2 | async-start | bytes 1572864 | tf_op jit(solution)/shard_map/cond/branch_0_fun/all_to_all | solution.py:146
  427.6 24.1 %all-to-all-start.1 = ((bf16[4,128,6,128]{3,0,2,1:T(4,128)(2,1)}), bf16[4,128,6,128]{3,0,2,1:T(4,128)(2,1)}, u32[]{:S(2)}, u32[]{:S(2)}) async-start(bf16[4,128,6,128]{3,0,2,1:T(4,128)(2,1)} %copy.434), calls=%async_computation.1 | async-start | bytes 1572864 | tf_op jit(solution)/shard_map/cond/branch_0_fun/all_to_all | solution.py:143
  451.6 23.9 %all-to-all-start = ((bf16[4,128,6,128]{3,0,2,1:T(4,128)(2,1)}), bf16[4,128,6,128]{3,0,2,1:T(4,128)(2,1)}, u32[]{:S(2)}, u32[]{:S(2)}) async-start(bf16[4,128,6,128]{3,0,2,1:T(4,128)(2,1)} %copy.431), calls=%async_computation | async-start | bytes 1572864 | tf_op jit(solution)/shard_map/cond/branch_0_fun/all_to_all | solution.py:144
  475.5 3.0 copy-start.35
  475.5 3.0 copy-start.43
  484.1 3.2 copy-start.46
  488.9 23.9 %all-to-all-start.4 = ((bf16[16,32,6,128]{3,1,2,0:T(8,128)(2,1)}), bf16[16,32,6,128]{3,1,2,0:T(8,128)(2,1)}, u32[]{:S(2)}, u32[]{:S(2)}) async-start(bf16[16,32,6,128]{3,1,2,0:T(8,128)(2,1)} %copy.444), calls=%async_computation.4 | async-start | bytes 1572864 | tf_op jit(solution)/shard_map/cond/branch_0_fun/all_to_all | solution.py:168
  512.7 23.9 %all-to-all-start.6 = ((bf16[16,32,6,128]{3,1,2,0:T(8,128)(2,1)}), bf16[16,32,6,128]{3,1,2,0:T(8,128)(2,1)}, u32[]{:S(2)}, u32[]{:S(2)}) async-start(bf16[16,32,6,128]{3,1,2,0:T(8,128)(2,1)} %copy.452), calls=%async_computation.6 | async-start | bytes 1572864 | tf_op jit(solution)/shard_map/cond/branch_0_fun/all_to_all | solution.py:170
  536.6 23.9 %all-to-all-start.5 = ((bf16[16,32,6,128]{3,1,2,0:T(8,128)(2,1)}), bf16[16,32,6,128]{3,1,2,0:T(8,128)(2,1)}, u32[]{:S(2)}, u32[]{:S(2)}) async-start(bf16[16,32,6,128]{3,1,2,0:T(8,128)(2,1)} %copy.448), calls=%async_computation.5 | async-start | bytes 1572864 | tf_op jit(solution)/shard_map/cond/branch_0_fun/all_to_all | solution.py:169
  540.8 114.7 %all-reduce.7.cloned.1.call-start = ((), (), s32[]{:S(2)}) async-start(), calls=%async_computation.21 | async-start | bytes 6291456 | tf_op jit(solution)/shard_map/cond/branch_0_fun/psum | solution.py:126
  541.2 4.9 copy-start.14
  541.2 4.9 copy-start.27
  566.2 2.8 copy-start.21
  569.0 8.3 slice-start.14
  570.1 7.3 copy-start.2
  570.1 7.2 slice-start.15
  570.1 7.2 copy-start.40
  675.7 71.8 %collective-permute-start = (bf16[4,128,3072]{2,1,0:T(8,128)(2,1)}, bf16[4,128,3072]{2,1,0:T(8,128)(2,1)S(1)}, u32[]{:S(2)}, u32[]{:S(2)}) collective-permute-start(bf16[4,128,3072]{2,1,0:T(8,128)(2,1)} %bitcast.802), channel_id=1, source_target_pairs={{16,0},{17,1},{18,2},{19,3},{20,4},{21,5},{22,6},{23,7},{24,8},{25... | collective-permute-start | bytes 9437192 | tf_op jit(solution)/shard_map/ppermute | solution.py:15
  756.9 23.8 %all-to-all-start.10 = ((bf16[4,128,6,128]{3,0,2,1:T(4,128)(2,1)}), bf16[4,128,6,128]{3,0,2,1:T(4,128)(2,1)}, u32[]{:S(2)}, u32[]{:S(2)}) async-start(bf16[4,128,6,128]{3,0,2,1:T(4,128)(2,1)} %copy.475), calls=%async_computation.10 | async-start | bytes 1572864 | tf_op jit(solution)/shard_map/cond/branch_0_fun/all_to_all | solution.py:145
  780.7 23.9 %all-to-all-start.9 = ((bf16[4,128,6,128]{3,0,2,1:T(4,128)(2,1)}), bf16[4,128,6,128]{3,0,2,1:T(4,128)(2,1)}, u32[]{:S(2)}, u32[]{:S(2)}) async-start(bf16[4,128,6,128]{3,0,2,1:T(4,128)(2,1)} %copy.472), calls=%async_computation.9 | async-start | bytes 1572864 | tf_op jit(solution)/shard_map/cond/branch_0_fun/all_to_all | solution.py:146
  804.5 23.8 %all-to-all-start.8 = ((bf16[4,128,6,128]{3,0,2,1:T(4,128)(2,1)}), bf16[4,128,6,128]{3,0,2,1:T(4,128)(2,1)}, u32[]{:S(2)}, u32[]{:S(2)}) async-start(bf16[4,128,6,128]{3,0,2,1:T(4,128)(2,1)} %copy.468), calls=%async_computation.8 | async-start | bytes 1572864 | tf_op jit(solution)/shard_map/cond/branch_0_fun/all_to_all | solution.py:143
  828.4 24.0 %all-to-all-start.7 = ((bf16[4,128,6,128]{3,0,2,1:T(4,128)(2,1)}), bf16[4,128,6,128]{3,0,2,1:T(4,128)(2,1)}, u32[]{:S(2)}, u32[]{:S(2)}) async-start(bf16[4,128,6,128]{3,0,2,1:T(4,128)(2,1)} %copy.465), calls=%async_computation.7 | async-start | bytes 1572864 | tf_op jit(solution)/shard_map/cond/branch_0_fun/all_to_all | solution.py:144
  852.4 2.9 copy-start.36
  852.4 2.9 copy-start.44
  861.0 3.2 copy-start.47
  865.8 23.9 %all-to-all-start.11 = ((bf16[16,32,6,128]{3,1,2,0:T(8,128)(2,1)}), bf16[16,32,6,128]{3,1,2,0:T(8,128)(2,1)}, u32[]{:S(2)}, u32[]{:S(2)}) async-start(bf16[16,32,6,128]{3,1,2,0:T(8,128)(2,1)} %copy.478), calls=%async_computation.11 | async-start | bytes 1572864 | tf_op jit(solution)/shard_map/cond/branch_0_fun/all_to_all | solution.py:168
  889.7 23.9 %all-to-all-start.13 = ((bf16[16,32,6,128]{3,1,2,0:T(8,128)(2,1)}), bf16[16,32,6,128]{3,1,2,0:T(8,128)(2,1)}, u32[]{:S(2)}, u32[]{:S(2)}) async-start(bf16[16,32,6,128]{3,1,2,0:T(8,128)(2,1)} %copy.486), calls=%async_computation.13 | async-start | bytes 1572864 | tf_op jit(solution)/shard_map/cond/branch_0_fun/all_to_all | solution.py:170
  913.5 23.9 %all-to-all-start.12 = ((bf16[16,32,6,128]{3,1,2,0:T(8,128)(2,1)}), bf16[16,32,6,128]{3,1,2,0:T(8,128)(2,1)}, u32[]{:S(2)}, u32[]{:S(2)}) async-start(bf16[16,32,6,128]{3,1,2,0:T(8,128)(2,1)} %copy.482), calls=%async_computation.12 | async-start | bytes 1572864 | tf_op jit(solution)/shard_map/cond/branch_0_fun/all_to_all | solution.py:169
  917.7 108.9 %all-reduce.11.cloned.1.call-start = ((), (), s32[]{:S(2)}) async-start(), calls=%async_computation.23 | async-start | bytes 6291456 | tf_op jit(solution)/shard_map/cond/branch_0_fun/psum | solution.py:126
  918.0 4.9 copy-start.15
  918.0 4.9 copy-start.29
  943.1 2.8 copy-start.23
  947.0 4.7 slice-start.16
  947.0 4.7 slice-start.17
  947.0 4.7 copy-start.41
  960.2 66.4 %copy-start.50 = (bf16[4,128,3072]{2,1,0:T(8,128)(2,1)S(1)}, bf16[4,128,3072]{2,1,0:T(8,128)(2,1)}, u32[]{:S(2)}) copy-start(bf16[4,128,3072]{2,1,0:T(8,128)(2,1)} %copy-done.49) | copy-start | bytes 9437188 | tf_op jit(solution)/shard_map/cond
  1051.3 72.2 %copy-start = (bf16[4,128,3072]{2,1,0:T(8,128)(2,1)S(1)}, bf16[4,128,3072]{2,1,0:T(8,128)(2,1)}, u32[]{:S(2)}) copy-start(bf16[4,128,3072]{2,1,0:T(8,128)(2,1)} %get-tuple-element.325) | copy-start | bytes 9437188
  1051.4 72.2 %collective-permute-start.1 = (bf16[4,128,3072]{2,1,0:T(8,128)(2,1)}, bf16[4,128,3072]{2,1,0:T(8,128)(2,1)}, u32[]{:S(2)}, u32[]{:S(2)}) collective-permute-start(bf16[4,128,3072]{2,1,0:T(8,128)(2,1)} %bitcast.261), channel_id=1, source_target_pairs={{16,0},{17,1},{18,2},{19,3},{20,4},{21,5},{22,6},{23,7},{24,8},{25... | collective-permute-start | bytes 9437192 | tf_op jit(solution)/shard_map/ppermute | solution.py:15
  1136.3 23.8 %all-to-all-start.16 = ((bf16[4,128,6,128]{3,0,2,1:T(4,128)(2,1)}), bf16[4,128,6,128]{3,0,2,1:T(4,128)(2,1)}, u32[]{:S(2)}, u32[]{:S(2)}) async-start(bf16[4,128,6,128]{3,0,2,1:T(4,128)(2,1)} %copy.506), calls=%async_computation.16 | async-start | bytes 1572864 | tf_op jit(solution)/shard_map/cond/branch_0_fun/all_to_all | solution.py:146
  1160.1 23.9 %all-to-all-start.17 = ((bf16[4,128,6,128]{3,0,2,1:T(4,128)(2,1)}), bf16[4,128,6,128]{3,0,2,1:T(4,128)(2,1)}, u32[]{:S(2)}, u32[]{:S(2)}) async-start(bf16[4,128,6,128]{3,0,2,1:T(4,128)(2,1)} %copy.509), calls=%async_computation.17 | async-start | bytes 1572864 | tf_op jit(solution)/shard_map/cond/branch_0_fun/all_to_all | solution.py:145
  1184.0 24.2 %all-to-all-start.15 = ((bf16[4,128,6,128]{3,0,2,1:T(4,128)(2,1)}), bf16[4,128,6,128]{3,0,2,1:T(4,128)(2,1)}, u32[]{:S(2)}, u32[]{:S(2)}) async-start(bf16[4,128,6,128]{3,0,2,1:T(4,128)(2,1)} %copy.502), calls=%async_computation.15 | async-start | bytes 1572864 | tf_op jit(solution)/shard_map/cond/branch_0_fun/all_to_all | solution.py:143
  1208.2 23.9 %all-to-all-start.14 = ((bf16[4,128,6,128]{3,0,2,1:T(4,128)(2,1)}), bf16[4,128,6,128]{3,0,2,1:T(4,128)(2,1)}, u32[]{:S(2)}, u32[]{:S(2)}) async-start(bf16[4,128,6,128]{3,0,2,1:T(4,128)(2,1)} %copy.499), calls=%async_computation.14 | async-start | bytes 1572864 | tf_op jit(solution)/shard_map/cond/branch_0_fun/all_to_all | solution.py:144
  1232.1 2.9 copy-start.34
  1232.1 2.9 copy-start.45
  1240.6 3.2 copy-start.48
  1245.4 23.8 %all-to-all-start.18 = ((bf16[16,32,6,128]{3,1,2,0:T(8,128)(2,1)}), bf16[16,32,6,128]{3,1,2,0:T(8,128)(2,1)}, u32[]{:S(2)}, u32[]{:S(2)}) async-start(bf16[16,32,6,128]{3,1,2,0:T(8,128)(2,1)} %copy.512), calls=%async_computation.18 | async-start | bytes 1572864 | tf_op jit(solution)/shard_map/cond/branch_0_fun/all_to_all | solution.py:168
  1269.3 23.9 %all-to-all-start.20 = ((bf16[16,32,6,128]{3,1,2,0:T(8,128)(2,1)}), bf16[16,32,6,128]{3,1,2,0:T(8,128)(2,1)}, u32[]{:S(2)}, u32[]{:S(2)}) async-start(bf16[16,32,6,128]{3,1,2,0:T(8,128)(2,1)} %copy.520), calls=%async_computation.20 | async-start | bytes 1572864 | tf_op jit(solution)/shard_map/cond/branch_0_fun/all_to_all | solution.py:170
  1293.1 23.8 %all-to-all-start.19 = ((bf16[16,32,6,128]{3,1,2,0:T(8,128)(2,1)}), bf16[16,32,6,128]{3,1,2,0:T(8,128)(2,1)}, u32[]{:S(2)}, u32[]{:S(2)}) async-start(bf16[16,32,6,128]{3,1,2,0:T(8,128)(2,1)} %copy.516), calls=%async_computation.19 | async-start | bytes 1572864 | tf_op jit(solution)/shard_map/cond/branch_0_fun/all_to_all | solution.py:169
  1297.3 108.8 %all-reduce.15.cloned.1.call-start = ((), (), s32[]{:S(2)}) async-start(), calls=%async_computation.25 | async-start | bytes 6291456 | tf_op jit(solution)/shard_map/cond/branch_0_fun/psum | solution.py:126
  1297.6 4.9 copy-start.16
  1297.6 4.9 copy-start.31
  1326.6 4.7 slice-start.18
  1326.6 4.7 slice-start.19
  1326.6 4.7 copy-start.42
  (14 other events, 21.6 us)
Sparse Core Ops, SparseCore 0:
  8.9 92.0 all-gather.12
  102.6 87.8 all-gather.8
  192.1 87.8 all-gather.10
  281.4 87.8 all-gather.14
  588.8 66.5 all-reduce.6
  960.3 66.2 all-reduce.10
  1339.9 66.2 all-reduce.14
where the time goes:
time: 1440 us; the launch traced here: 1430 us
  waiting for transfers between devices  905 us (63%)
  local copies, waits for them, and re-layouts  158 us (11%)
  matrix products  151 us (10%)
  starting transfers between devices  93.4 us (6%)
  other arithmetic  63.1 us (4%)
  loops' own time  43.8 us (3%)
    psum x3, waiting for transfers between devices, finish(): summed = lax.psum(term_low.astype(jnp.bfloat16), 'head').astype(jnp.float32)  200 us
    ppermute x2, waiting for transfers between devices, from_behind(): lax.ppermute(value, axis, [(source, source + steps) for source in range(i...  132 us
    all_gather x1, waiting for transfers between devices, on_device(): lax.all_gather(w_key[0], 'frame', axis=0, tiled=True)  89.4 us
    all_gather x1, waiting for transfers between devices, on_device(): lax.all_gather(w_query[0], 'frame', axis=0, tiled=True)  89.4 us
    all_gather x1, waiting for transfers between devices, on_device(): lax.all_gather(w_value[0], 'frame', axis=0, tiled=True)  89.3 us
    all_gather x1, waiting for transfers between devices, on_device(): out_full = lax.all_gather(w_out[0], 'frame', axis=1, tiled=True)  80.7 us
    dot_general x12, matrix products, contract_last(): lax.dot_general(left, right, (((1,), (1,)), ((), ())), preferred_element_...  74.6 us
    all_to_all x3, waiting for transfers between devices, temporal_branch(): lax.all_to_all(out_time(dquery), 'frame', split_axis=0, concat_axis=1, ti...  48.9 us
  transfers between devices with their start and end apart: 30, of which 30 were waited for; matrix products, arithmetic and copies ran while one was open for 14% of the time, Pallas kernels for 0%

commit v1 on v0

v1 whole, which is shorter than its diff:
```python
import functools

import jax
import jax.numpy as jnp
from jax import lax
from jax.experimental import pallas as pl
from jax.experimental.pallas import tpu as pltpu
from jax.sharding import PartitionSpec as P

FRAMES = 16
EPS = 1e-06


def dot_nn(left, right):
    return lax.dot_general(left, right, (((1,), (0,)), ((), ())), preferred_element_type=jnp.float32)


def dot_nt(left, right):
    return lax.dot_general(left, right, (((1,), (1,)), ((), ())), preferred_element_type=jnp.float32)


def dot_tn(left, right):
    return lax.dot_general(left, right, (((0,), (0,)), ((), ())), preferred_element_type=jnp.float32)


def head_norm(raw_rows):
    scale_rows = lax.rsqrt(jnp.mean(raw_rows * raw_rows, axis=-1, keepdims=True) + EPS)
    return raw_rows * scale_rows, scale_rows


def norm_back(grad_low, normal_hat, scale_rows, gain_vec):
    grad_hat = grad_low.astype(jnp.float32) * gain_vec
    inner_mean = jnp.mean(grad_hat * normal_hat, axis=-1, keepdims=True)
    return (scale_rows * (grad_hat - normal_hat * inner_mean)).astype(jnp.bfloat16)


def attend_back(query_low, key_low, value_low, grad_attn, mask):
    expo = jnp.exp(dot_nt(query_low, key_low)) * mask
    probs = expo / jnp.sum(expo, axis=-1, keepdims=True)
    dprob = dot_nt(grad_attn, value_low)
    dscore = (probs * (dprob - jnp.sum(probs * dprob, axis=-1, keepdims=True))).astype(jnp.bfloat16)
    dquery = dot_nn(dscore, key_low).astype(jnp.bfloat16)
    dkey = dot_tn(dscore, query_low).astype(jnp.bfloat16)
    dvalue = dot_tn(probs.astype(jnp.bfloat16), grad_attn).astype(jnp.bfloat16)
    return dquery, dkey, dvalue


def chunk_kernel(first, last, width, head_dim, block, *refs):
    mask_ref, gains_ref, low_ref, grad_ref, weight_ref = refs[:5]
    refs = refs[5:]
    if not first:
        total_ref, refs = refs[0], refs[1:]
    if last:
        saved_ref, inv_ref, gain_ref = refs[:3]
        refs = refs[3:]
    out_ref, packed_ref = refs
    rows = low_ref.shape[0]
    query_gain, key_gain = gains_ref[0:1, :], gains_ref[1:2, :]
    mask = mask_ref[...]
    query_raw = dot_nn(low_ref[...], weight_ref[:, 0:width])
    key_raw = dot_nn(low_ref[...], weight_ref[:, width : 2 * width])
    value = dot_nn(low_ref[...], weight_ref[:, 2 * width : 3 * width]).astype(jnp.bfloat16)
    grad_attn = dot_nn(grad_ref[...], weight_ref[:, 3 * width : 4 * width]).astype(jnp.bfloat16)
    for head in range(width // head_dim):
        cols = slice(head * head_dim, (head + 1) * head_dim)
        query_hat, query_scale = head_norm(query_raw[:, cols])
        key_hat, key_scale = head_norm(key_raw[:, cols])
        query_low = (query_hat * query_gain).astype(jnp.bfloat16)
        key_low = (key_hat * key_gain).astype(jnp.bfloat16)
        for part in range(rows // block):
            own = slice(part * block, (part + 1) * block)
            dquery, dkey, dvalue = attend_back(
                query_low[own], key_low[own], value[own, cols], grad_attn[own, cols], mask
            )
            packed_ref[own, cols] = norm_back(dquery, query_hat[own], query_scale[own], query_gain)
            packed_ref[own, width + cols.start : width + cols.stop] = norm_back(
                dkey, key_hat[own], key_scale[own], key_gain
            )
            packed_ref[own, 2 * width + cols.start : 2 * width + cols.stop] = dvalue
    dnorm = dot_nt(packed_ref[...], weight_ref[:, 0 : 3 * width])
    if not first:
        dnorm = dnorm + total_ref[...]
    if not last:
        out_ref[...] = dnorm
        return
    inv_rms = inv_ref[...]
    normed = saved_ref[...].astype(jnp.float32) * inv_rms
    grad_hat = dnorm * gain_ref[...]
    term = inv_rms * (grad_hat - normed * jnp.mean(grad_hat * normed, axis=-1, keepdims=True))
    term = term.astype(jnp.bfloat16)
    shares, _, share_width = out_ref.shape
    for share in range(shares):
        out_ref[share] = term[:, share * share_width : (share + 1) * share_width]


def run_chunk(mask, gains, low, grad, weight, total, extra, part, parts, shares, head_dim):
    rows, feat = low.shape[0] // parts, low.shape[1]
    width = weight.shape[1] // 4
    block = mask.shape[0]
    tile = 2 * block if rows % (2 * block) == 0 else block
    steps = rows // tile
    first, last = total is None, extra is not None

    def at(step):
        return (part * steps + step, 0)

    def whole(step):
        return (0, 0)

    once = pl.Buffered(1)
    in_specs = [
        pl.BlockSpec(mask.shape, whole, pipeline_mode=once),
        pl.BlockSpec(gains.shape, whole, pipeline_mode=once),
        pl.BlockSpec((tile, feat), at),
        pl.BlockSpec((tile, feat), at),
        pl.BlockSpec(weight.shape, whole, pipeline_mode=once),
    ]
    args = [mask, gains, low, grad, weight]
    if not first:
        in_specs.append(pl.BlockSpec((tile, feat), at))
        args.append(total)
    if last:
        saved, inv_rms, gain_row = extra
        in_specs += [
            pl.BlockSpec((tile, feat), at),
            pl.BlockSpec((tile, 1), at),
            pl.BlockSpec(gain_row.shape, whole, pipeline_mode=once),
        ]
        args += [saved, inv_rms, gain_row]
        share_width = feat // shares
        out_shape = jax.ShapeDtypeStruct((shares, rows, share_width), jnp.bfloat16)
        out_specs = pl.BlockSpec((shares, tile, share_width), lambda step: (0, step, 0))
    else:
        out_shape = jax.ShapeDtypeStruct((rows, feat), jnp.float32)
        out_specs = pl.BlockSpec((tile, feat), lambda step: (step, 0))
    moved = rows * feat * (4 + 4 * (not first) + 4 * (not last)) + weight.size * 2
    return pl.pallas_call(
        functools.partial(chunk_kernel, first, last, width, head_dim, block),
        grid=(steps,),
        in_specs=in_specs,
        out_specs=out_specs,
        out_shape=out_shape,
        scratch_shapes=[pltpu.VMEM((tile, 3 * width), jnp.bfloat16)],
        input_output_aliases={5: 0} if (not first and not last) else {},
        compiler_params=pltpu.CompilerParams(
            dimension_semantics=("arbitrary",), vmem_limit_bytes=48 << 20
        ),
        cost_estimate=pl.CostEstimate(
            flops=14 * rows * feat * width, bytes_accessed=moved, transcendentals=rows * width
        ),
        name="chunk_last" if last else "chunk",
    )(*args)


def on_device(inputs, upstream, norm_gain, head_gain, w_query, w_key, w_value, w_out):
    on_last = lax.axis_index("section") == 1
    frame_count, head_count = lax.axis_size("frame"), lax.axis_size("head")
    my_frame, my_head = lax.axis_index("frame"), lax.axis_index("head")
    batches, frames, patches, feat = inputs.shape[1:]
    rows = frames * patches
    total_frames = frames * frame_count
    few = patches // frame_count
    piece = frames * few
    head_dim = head_gain.shape[-1]
    share = feat // head_count
    local_width = w_query.shape[2]
    width = 2 * head_dim if local_width % (2 * head_dim) == 0 else head_dim
    chunks = local_width // width
    gain_row = norm_gain
    gains = jnp.stack([head_gain[0, 0] * head_dim ** (-0.5), head_gain[0, 1]])

    def reorder(array_in, source):
        pick = (source[:, None] == jnp.arange(rows)[None, :]).astype(jnp.bfloat16)
        flat = array_in.reshape(-1, rows, array_in.shape[-1])
        moved = jnp.einsum("rs,bsc->brc", pick, flat, preferred_element_type=jnp.float32)
        return moved.astype(jnp.bfloat16)

    index = jnp.arange(rows)
    shift, in_frame, in_few = index // piece, (index % piece) // few, index % few
    target = (my_frame + shift) % frame_count
    leave_space = in_frame * patches + target * few + in_few
    leave_time = in_few * total_frames + target * frames + in_frame
    time_patch, time_frame = index // total_frames, index % total_frames
    enter_time = (
        ((my_frame - time_frame // frames) % frame_count) * piece
        + (time_frame % frames) * few
        + time_patch
    )
    space_frame, space_patch = index // patches, index % patches
    enter_space = (
        ((my_frame - space_patch // few) % frame_count) * piece
        + space_frame * few
        + space_patch % few
    )

    def exchange(array_in, leave, enter, from_section):
        sorted_rows = reorder(array_in, leave)
        pieces = []
        for step in range(frame_count):
            part = sorted_rows[:, step * piece : (step + 1) * piece]
            if step or from_section:
                part = lax.ppermute(
                    part,
                    ("section", "frame"),
                    [
                        (from_section * frame_count + source, (source + step) % frame_count)
                        for source in range(frame_count)
                    ],
                )
            pieces.append(part)
        return reorder(jnp.concatenate(pieces, axis=1), enter)

    def swap(array_in, bit):
        return lax.ppermute(array_in, "head", [(i, i ^ bit) for i in range(head_count)])

    my_core, my_side = my_head % 2, my_head // 2

    def gather_share(own):
        far = swap(own, 2)
        low_side = jnp.where(my_side == 0, own, far)
        high_side = jnp.where(my_side == 0, far, own)
        both = jnp.stack([low_side, high_side])
        other = swap(both, 1)
        first, second = jnp.where(my_core == 0, both, other), jnp.where(my_core == 0, other, both)
        return jnp.concatenate([first[0], second[0], first[1], second[1]], axis=-1)

    def sum_share(term):
        shaped = term.reshape(2, 2, *term.shape[1:])
        keep = lax.dynamic_index_in_dim(shaped, my_core, 1, keepdims=False)
        other = swap(lax.dynamic_index_in_dim(shaped, 1 - my_core, 1, keepdims=False), 1)
        pair = keep.astype(jnp.float32) + other.astype(jnp.float32)
        far = lax.dynamic_index_in_dim(pair, 1 - my_side, 0, keepdims=False).astype(jnp.bfloat16)
        own = lax.dynamic_index_in_dim(pair, my_side, 0, keepdims=False)
        return own + swap(far, 2).astype(jnp.float32)

    def my_share(array_in):
        return lax.dynamic_slice_in_dim(array_in, my_head * share, share, array_in.ndim - 1)

    def pack(chunk):
        cols = slice(chunk * width, (chunk + 1) * width)
        return jnp.concatenate(
            [w_query[0][:, cols], w_key[0][:, cols], w_value[0][:, cols], w_out[0][cols].T], axis=1
        )

    weights = [lax.all_gather(pack(c), "frame", axis=0, tiled=True) for c in range(chunks)]

    saved_space = inputs[0].reshape(batches, rows, feat)
    saved_time = gather_share(exchange(my_share(saved_space), leave_space, enter_time, 0))
    saved = jnp.where(on_last, saved_space, saved_time).reshape(batches * rows, feat)
    wide = saved.astype(jnp.float32)
    inv_rms = lax.rsqrt(jnp.mean(wide * wide, axis=-1, keepdims=True) + EPS)
    low = (wide * inv_rms * gain_row).astype(jnp.bfloat16)

    place = jnp.arange(patches) // FRAMES
    mask = jnp.where(on_last, 1.0, (place[:, None] == place[None, :]).astype(jnp.float32))
    extra = (saved, inv_rms, gain_row)

    def sublayer(grad, lows, extras):
        total = None
        parts = grad.shape[0] // rows
        for chunk in range(chunks):
            last = chunk == chunks - 1
            if not last:
                total = run_chunk(
                    mask, gains, lows, grad, weights[chunk], total, None, 0, 1, head_count, head_dim
                )
        return [
            run_chunk(
                mask, gains, lows, grad, weights[-1], total, extras, b, parts, head_count, head_dim
            )
            for b in range(parts)
        ]

    grad_space = upstream.reshape(batches * rows, feat)
    share_space = my_share(upstream.reshape(batches, rows, feat))
    space_parts, time_parts = [], []
    for b, term in enumerate(sublayer(grad_space, low, extra)):
        summed = sum_share(term)
        space_parts.append((share_space[b].astype(jnp.float32) + summed).astype(jnp.bfloat16))
    for b in range(batches):
        grad_share = exchange(space_parts[b], leave_space, enter_time, 1)[0]
        grad_time = gather_share(grad_share)
        part = slice(b * rows, (b + 1) * rows)
        (term,) = sublayer(grad_time, low[part], (saved[part], inv_rms[part], gain_row))
        summed = sum_share(term)
        result = (grad_share.astype(jnp.float32) + summed).astype(jnp.bfloat16)
        time_parts.append(exchange(result, leave_time, enter_space, 0)[0])
    result = jnp.where(on_last, jnp.stack(space_parts), jnp.stack(time_parts))
    return result.reshape(1, batches, frames, patches, share)


def solution(mesh):
    in_specs = (
        P("section", None, "frame", None, None),
        P(None, "frame", None, None),
        P("section", None),
        P("section", None, None),
        P("section", "frame", "head"),
        P("section", "frame", "head"),
        P("section", "frame", "head"),
        P("section", "head", "frame"),
    )
    out_specs = P("section", None, "frame", None, "head")
    return jax.shard_map(
        on_device, mesh=mesh, in_specs=in_specs, out_specs=out_specs, check_vma=False
    )
```

time: 1440 us -> 723 us (0.50)
  waiting for transfers between devices: 905 us -> 372 us
  Pallas kernels: 0 us -> 179 us
  matrix products: 151 us -> 13.1 us
  local copies, waits for them, and re-layouts: 158 us -> 29 us
  loops' own time: 43.8 us -> 0 us
  starting transfers between devices: 93.4 us -> 57.1 us
    all_to_all x21 -> x0, waiting for transfers between devices: 223 us -> none  [the longest x3 48.9 us: temporal_branch(): lax.all_to_all(out_time(dquery), 'frame', split_axis=0, concat_axis=1, ti...]
    psum x3 -> x0, waiting for transfers between devices: 200 us -> none  [finish(): summed = lax.psum(term_low.astype(jnp.bfloat16), 'head').astype(jnp.float32)]
    pallas_call x0 -> x10, Pallas kernels: none -> 179 us  [run_chunk(): pl.pallas_call(functools.partial(chunk_kernel, first, last, width, head_d...]
    all_gather x4 -> x3, waiting for transfers between devices: 349 us -> 192 us  [on_device(): lax.all_gather(pack(c), 'frame', axis=0, tiled=True)]
    dot_general x33 -> x10, matrix products: 140 us -> 13.1 us  [reorder(): jnp.einsum('rs,bsc->brc', pick, flat, preferred_element_type=jnp.float32)]
    all_to_all x21 -> x0, starting transfers between devices: 89.6 us -> none  [the longest x3 13.2 us: temporal_branch(): lax.all_to_all(state[6], 'frame', split_axis=1, concat_axis=0, tiled=True)]
    ppermute x2 -> x31, starting transfers between devices: 2.85 us -> 57 us  [the longest x17 48.9 us: exchange(): lax.ppermute(part, ('section', 'frame'), [(from_section * frame_count + s...]
    ppermute x2 -> x31, waiting for transfers between devices: 132 us -> 180 us  [the longest x14 111 us: swap(): lax.ppermute(array_in, 'head', [(i, i ^ bit) for i in range(head_count)])]
  transfers between devices with their start and end apart: 30 -> 34, of which waited for: 30 -> 19; matrix products, arithmetic and copies ran while one was open for 14% -> 10% of each run, Pallas kernels for 0% -> 23%
where the time goes in v1:
time: 723 us; the launch traced here: 717 us
  waiting for transfers between devices  372 us (51%)
  Pallas kernels  179 us (25%)
  starting transfers between devices  57.1 us (8%)
  other arithmetic  52.7 us (7%)
  local copies, waits for them, and re-layouts  29 us (4%)
  between operations  14.4 us (2%)
  matrix products  13.1 us (2%)
    all_gather x3, waiting for transfers between devices, on_device(): lax.all_gather(pack(c), 'frame', axis=0, tiled=True)  192 us
    pallas_call x10, Pallas kernels, run_chunk(): pl.pallas_call(functools.partial(chunk_kernel, first, last, width, head_d...  179 us
    ppermute x14, waiting for transfers between devices, swap(): lax.ppermute(array_in, 'head', [(i, i ^ bit) for i in range(head_count)])  111 us
    ppermute x17, waiting for transfers between devices, exchange(): lax.ppermute(part, ('section', 'frame'), [(from_section * frame_count + s...  68.9 us
    ppermute x17, starting transfers between devices, exchange(): lax.ppermute(part, ('section', 'frame'), [(from_section * frame_count + s...  48.9 us
  transfers between devices with their start and end apart: 34, of which 19 were waited for; matrix products, arithmetic and copies ran while one was open for 10% of the time, Pallas kernels for 23%

profile of v1, /device:TPU:0, one launch (start us, length us, event | category | flops | bytes accessed | tf_op | source)
XLA Modules:
  0.0 717.0 jit_solution(15801954937072295752)
XLA Ops:
  8.0 1.5 fusion.111
  13.4 2.4 fusion.14
  15.9 4.9 collective-permute-start
  20.9 4.5 collective-permute-start.1
  25.4 3.3 collective-permute-start.2
  28.7 9.1 %collective-permute-done = bf16[2,128,768]{2,1,0:T(8,128)(2,1)S(1)} collective-permute-done((bf16[2,128,768]{2,1,0:T(8,128)(2,1)S(1)}, bf16[2,128,768]{2,1,0:T(8,128)(2,1)S(1)}, u32[]{:S(2)}, u32[]{:S(2)}) %collective-permute-start) | collective-permute-done | bytes 393248 | tf_op jit(solution)/shard_map/ppermute | solution.py:202
  37.7 32.3 %collective-permute-done.1 = bf16[2,128,768]{2,1,0:T(8,128)(2,1)S(1)} collective-permute-done((bf16[2,128,768]{2,1,0:T(8,128)(2,1)S(1)}, bf16[2,128,768]{2,1,0:T(8,128)(2,1)S(1)}, u32[]{:S(2)}, u32[]{:S(2)}) %collective-permute-start.1) | collective-permute-done | bytes 393248 | tf_op jit(solution)/shard_map/ppermute | solution.py:202
  70.0 2.2 fusion.17
  72.2 1.5 collective-permute-start.3
  75.3 33.3 %collective-permute-done.3 = bf16[2,512,768]{2,1,0:T(8,128)(2,1)} collective-permute-done((bf16[2,512,768]{2,1,0:T(8,128)(2,1)}, bf16[2,512,768]{2,1,0:T(8,128)(2,1)}, u32[]{:S(2)}, u32[]{:S(2)}) %collective-permute-start.3) | collective-permute-done | bytes 1572896 | tf_op jit(solution)/shard_map/ppermute | solution.py:214
  108.6 2.1 select_bitcast_fusion.1
  110.8 1.9 pad_maximum_fusion
  112.8 5.9 collective-permute-done.4
  118.7 2.3 broadcast_select_fusion.1
  121.0 3.3 slice_bitcast_fusion.13
  124.3 1.5 slice-done.2
  125.8 2.0 slice-done.3
  127.8 7.3 %multiply_reduce_fusion = f32[2,4,128]{2,1,0:T(4,128)S(1)} fusion(bf16[1,2,4,128,3072]{4,3,2,1,0:T(8,128)(2,1)S(1)} %bitcast.227, bf16[1,2,4,128,768]{4,3,2,1,0:T(8,128)(2,1)S(1)} %bitcast.231, bf16[1,2,4,128,768]{4,3,2,1,0:T(8,128)(2,1)S(1)} %bitcast.237, bf16[1,2,4,128,768]{4,3,2,1,0:T(8,128)(2,1)S(1)} %bitcast.233, ...), kind=kLoop, calls=%fused_computation.1 | loop fusion | flops 37747712 | bytes 12587009 | tf_op jit(solution)/shard_map/reduce_sum | solution.py:251
  135.4 11.6 %multiply_convert_fusion = (bf16[1024,3072]{1,0:T(8,128)(2,1)}, bf16[1024,3072]{1,0:T(8,128)(2,1)}) fusion(f32[3072]{0:T(1024)S(1)} %bitcast.217, f32[1024]{0:T(1024)S(1)} %bitcast.250, bf16[1024,768]{1,0:T(8,128)(2,1)S(1)} %bitcast.232, bf16[1024,768]{1,0:T(8,128)(2,1)} %bitcast.238, bf16[1024,768]{1,0:T(8,128)(2,1)} %bitcast.234, ...), kind=kLoop, calls=%fused_computation | loop fusion | flops 40894464 | bytes 25182208 | tf_op jit(solution)/shard_map/convert_element_type | solution.py:252
  147.0 11.9 %all-gather.8.cloned.1.call-done.refs_4_ = bf16[3072,1024]{1,0:T(8,128)(2,1)} async-done(((bf16[768,1024]{1,0:T(8,128)(2,1)}), bf16[3072,1024]{1,0:T(8,128)(2,1)}) %all-gather.8.cloned.1.call-update) | async-done | bytes 6291472 | tf_op jit(solution)/shard_map/all_gather | solution.py:245
  158.9 24.5 %chunk.6.refs_5_ = f32[1024,3072]{1,0:T(8,128)} custom-call(f32[128,128]{1,0:T(8,128)S(1)} %convert_select_fusion.refs_0_, f32[2,128]{1,0:T(2,128)S(1)} %pad_maximum_fusion.8.refs_1_, bf16[1024,3072]{1,0:T(8,128)(2,1)} %get-tuple-element.5.refs_2_, bf16[1024,3072]{1,0:T(8,128)(2,1)} %bitcast.220, bf16[3072,1024]{1,0:T(8,128)(2,1)} %all-gather.8.cloned.1.call-done.refs_4_), custom_call_target="tpu_custom_call" | custom-call | flops 11274289152 | bytes 31457280 | tf_op jit(solution)/shard_map/chunk/pallas_call | solution.py:137
  183.5 90.9 %all-gather.6.cloned.1.call-done.refs_4_ = bf16[3072,1024]{1,0:T(8,128)(2,1)} async-done(((bf16[768,1024]{1,0:T(8,128)(2,1)}), bf16[3072,1024]{1,0:T(8,128)(2,1)}) %all-gather.6.cloned.1.call-update) | async-done | bytes 6291472 | tf_op jit(solution)/shard_map/all_gather | solution.py:245
  274.3 26.4 %chunk.7.refs_5_ = f32[1024,3072]{1,0:T(8,128)} custom-call(f32[128,128]{1,0:T(8,128)S(1)} %convert_select_fusion.refs_0_, f32[2,128]{1,0:T(2,128)S(1)} %pad_maximum_fusion.8.refs_1_, bf16[1024,3072]{1,0:T(8,128)(2,1)} %get-tuple-element.5.refs_2_, bf16[1024,3072]{1,0:T(8,128)(2,1)} %bitcast.221, ...), custom_call_target="tpu_custom_call", output_to_operand_aliasing={{}: (5, {})} | custom-call | flops 11274289152 | bytes 44040192 | tf_op jit(solution)/shard_map/chunk/pallas_call | solution.py:137
  300.7 88.8 %all-gather.4.cloned.1.call-done.refs_4_ = bf16[3072,1024]{1,0:T(8,128)(2,1)} async-done(((bf16[768,1024]{1,0:T(8,128)(2,1)}), bf16[3072,1024]{1,0:T(8,128)(2,1)}) %all-gather.4.cloned.1.call-update) | async-done | bytes 6291472 | tf_op jit(solution)/shard_map/all_gather | solution.py:245
  389.5 17.0 %chunk_last.5 = bf16[4,512,768]{2,1,0:T(8,128)(2,1)S(1)} custom-call(f32[128,128]{1,0:T(8,128)S(1)} %convert_select_fusion.refs_0_, f32[2,128]{1,0:T(2,128)S(1)} %pad_maximum_fusion.8.refs_1_, bf16[1024,3072]{1,0:T(8,128)(2,1)} %get-tuple-element.5.refs_2_, bf16[1024,3072]{1,0:T(8,128)(2,1)} %bitcast.222, ...), custom_call_target="tpu_custom_call" | custom-call | flops 5637144576 | bytes 18874368 | tf_op jit(solution)/shard_map/chunk_last/pallas_call | solution.py:137
  408.8 17.0 %chunk_last.4 = bf16[4,512,768]{2,1,0:T(8,128)(2,1)S(1)} custom-call(f32[128,128]{1,0:T(8,128)S(1)} %convert_select_fusion.refs_0_, f32[2,128]{1,0:T(2,128)S(1)} %pad_maximum_fusion.8.refs_1_, bf16[1024,3072]{1,0:T(8,128)(2,1)} %get-tuple-element.5.refs_2_, bf16[1024,3072]{1,0:T(8,128)(2,1)} %bitcast.223, ...), custom_call_target="tpu_custom_call" | custom-call | flops 5637144576 | bytes 18874368 | tf_op jit(solution)/shard_map/chunk_last/pallas_call | solution.py:137
  427.5 2.2 convert_add_fusion.2
  432.4 1.7 convert_add_fusion.3
  434.3 1.5 copy-done.11
  436.4 15.3 %collective-permute-done.8 = bf16[512,768]{1,0:T(8,128)(2,1)} collective-permute-done((bf16[512,768]{1,0:T(8,128)(2,1)}, bf16[512,768]{1,0:T(8,128)(2,1)}, u32[]{:S(2)}, u32[]{:S(2)}) %collective-permute-start.8) | collective-permute-done | bytes 786464 | tf_op jit(solution)/shard_map/ppermute | solution.py:214
  451.6 15.8 %collective-permute-done.6 = bf16[512,768]{1,0:T(8,128)(2,1)S(1)} collective-permute-done((bf16[512,768]{1,0:T(8,128)(2,1)S(1)}, bf16[512,768]{1,0:T(8,128)(2,1)S(1)}, u32[]{:S(2)}, u32[]{:S(2)}) %collective-permute-start.6) | collective-permute-done | bytes 786464 | tf_op jit(solution)/shard_map/ppermute | solution.py:214
  467.5 4.1 fusion.8
  477.9 4.3 maximum_select_fusion.2
  482.1 3.1 collective-permute-done.10
  485.2 6.5 collective-permute-done.11
  491.7 4.1 collective-permute-done.9
  495.8 1.5 fusion.21
  497.4 1.5 collective-permute-start.13
  498.9 2.1 fusion.107
  502.2 1.9 fusion.23
  509.4 7.7 %collective-permute-done.13 = bf16[512,768]{1,0:T(8,128)(2,1)} collective-permute-done((bf16[512,768]{1,0:T(8,128)(2,1)}, bf16[512,768]{1,0:T(8,128)(2,1)}, u32[]{:S(2)}, u32[]{:S(2)}) %collective-permute-start.13) | collective-permute-done | bytes 786464 | tf_op jit(solution)/shard_map/ppermute | solution.py:214
  518.9 6.4 collective-permute-done.20
  526.5 6.0 slice_bitcast_fusion.1
  532.5 12.8 %collective-permute-done.24 = bf16[512,768]{1,0:T(8,128)(2,1)S(1)} collective-permute-done((bf16[512,768]{1,0:T(8,128)(2,1)S(1)}, bf16[512,768]{1,0:T(8,128)(2,1)S(1)}, u32[]{:S(2)}, u32[]{:S(2)}) %collective-permute-start.24) | collective-permute-done | bytes 786464 | tf_op jit(solution)/shard_map/ppermute | solution.py:214
  547.2 1.9 pad_maximum_fusion.1.refs_3_
  550.2 14.4 %chunk.8.refs_5_ = f32[512,3072]{1,0:T(8,128)} custom-call(f32[128,128]{1,0:T(8,128)S(1)} %convert_select_fusion.refs_0_, f32[2,128]{1,0:T(2,128)S(1)} %pad_maximum_fusion.8.refs_1_, bf16[512,3072]{1,0:T(8,128)(2,1)S(1)} %copy-done.1, bf16[512,3072]{1,0:T(8,128)(2,1)} %pad_maximum_fusion.1.refs_3_, bf16[3072,1024]{1,0:T(8,128)(2,1)} %all-gather.8.cloned.1.call-done.refs_4_), custom_call_target="tpu_custom_call" | custom-call | flops 5637144576 | bytes 18874368 | tf_op jit(solution)/shard_map/chunk/pallas_call | solution.py:137
  564.6 15.4 %chunk.9.refs_5_ = f32[512,3072]{1,0:T(8,128)} custom-call(f32[128,128]{1,0:T(8,128)S(1)} %convert_select_fusion.refs_0_, f32[2,128]{1,0:T(2,128)S(1)} %pad_maximum_fusion.8.refs_1_, bf16[512,3072]{1,0:T(8,128)(2,1)S(1)} %copy-done.1, bf16[512,3072]{1,0:T(8,128)(2,1)} %pad_maximum_fusion.1.refs_3_, ...), custom_call_target="tpu_custom_call", output_to_operand_aliasing={{}: (5, {})} | custom-call | flops 5637144576 | bytes 25165824 | tf_op jit(solution)/shard_map/chunk/pallas_call | solution.py:137
  580.0 17.2 %chunk_last.6 = bf16[4,512,768]{2,1,0:T(8,128)(2,1)S(1)} custom-call(f32[128,128]{1,0:T(8,128)S(1)} %convert_select_fusion.refs_0_, f32[2,128]{1,0:T(2,128)S(1)} %pad_maximum_fusion.8.refs_1_, bf16[512,3072]{1,0:T(8,128)(2,1)} %get-tuple-element.9.refs_2_, bf16[512,3072]{1,0:T(8,128)(2,1)} %pad_maximum_fusion.1.refs_3_, ...), custom_call_target="tpu_custom_call" | custom-call | flops 5637144576 | bytes 18874368 | tf_op jit(solution)/shard_map/chunk_last/pallas_call | solution.py:137
  597.9 1.6 broadcast_select_fusion.3
  599.8 1.8 pad_maximum_fusion.2.refs_3_
  601.6 14.4 %chunk.10.refs_5_ = f32[512,3072]{1,0:T(8,128)} custom-call(f32[128,128]{1,0:T(8,128)S(1)} %convert_select_fusion.refs_0_, f32[2,128]{1,0:T(2,128)S(1)} %pad_maximum_fusion.8.refs_1_, bf16[512,3072]{1,0:T(8,128)(2,1)S(1)} %get-tuple-element.10.refs_2_, bf16[512,3072]{1,0:T(8,128)(2,1)} %pad_maximum_fusion.2.refs_3_, ...), custom_call_target="tpu_custom_call" | custom-call | flops 5637144576 | bytes 18874368 | tf_op jit(solution)/shard_map/chunk/pallas_call | solution.py:137
  616.0 15.4 %chunk.11.refs_5_ = f32[512,3072]{1,0:T(8,128)} custom-call(f32[128,128]{1,0:T(8,128)S(1)} %convert_select_fusion.refs_0_, f32[2,128]{1,0:T(2,128)S(1)} %pad_maximum_fusion.8.refs_1_, bf16[512,3072]{1,0:T(8,128)(2,1)S(1)} %get-tuple-element.10.refs_2_, bf16[512,3072]{1,0:T(8,128)(2,1)} %pad_maximum_fusion.2.refs_3_, ...), custom_call_target="tpu_custom_call", output_to_operand_aliasing={{}: (5, {})} | custom-call | flops 5637144576 | bytes 25165824 | tf_op jit(solution)/shard_map/chunk/pallas_call | solution.py:137
  631.4 17.2 %chunk_last.7 = bf16[4,512,768]{2,1,0:T(8,128)(2,1)S(1)} custom-call(f32[128,128]{1,0:T(8,128)S(1)} %convert_select_fusion.refs_0_, f32[2,128]{1,0:T(2,128)S(1)} %pad_maximum_fusion.8.refs_1_, bf16[512,3072]{1,0:T(8,128)(2,1)} %copy-done, bf16[512,3072]{1,0:T(8,128)(2,1)} %pad_maximum_fusion.2.refs_3_, ...), custom_call_target="tpu_custom_call" | custom-call | flops 5637144576 | bytes 18874368 | tf_op jit(solution)/shard_map/chunk_last/pallas_call | solution.py:137
  649.9 2.3 collective-permute-done.26
  653.4 16.4 %collective-permute-done.16 = bf16[512,768]{1,0:T(8,128)(2,1)S(1)} collective-permute-done((bf16[512,768]{1,0:T(8,128)(2,1)S(1)}, bf16[512,768]{1,0:T(8,128)(2,1)S(1)}, u32[]{:S(2)}, u32[]{:S(2)}) %collective-permute-start.16) | collective-permute-done | bytes 786464 | tf_op jit(solution)/shard_map/ppermute | solution.py:214
  669.7 1.8 fusion.22
  671.6 6.7 collective-permute-start.17
  678.3 1.9 collective-permute-start.18
  680.2 4.3 collective-permute-start.19
  684.5 1.7 collective-permute-done.27
  687.0 6.7 collective-permute-start.28
  693.7 1.9 collective-permute-start.29
  695.6 4.3 collective-permute-start.30
  700.6 7.3 %collective-permute-done.29 = bf16[1,128,768]{2,1,0:T(8,128)(2,1)S(1)} collective-permute-done((bf16[1,128,768]{2,1,0:T(8,128)(2,1)S(1)}, bf16[1,128,768]{2,1,0:T(8,128)(2,1)S(1)}, u32[]{:S(2)}, u32[]{:S(2)}) %collective-permute-start.29) | collective-permute-done | bytes 196640 | tf_op jit(solution)/shard_map/ppermute | solution.py:202
  (148 shorter events, 39.9 us)
Async XLA Ops:
  6.5 152.4 %all-gather.8.cloned.1.call-start = ((), (), s32[]{:S(2)}) async-start(), calls=%async_computation.2 | async-start | bytes 7864320 | tf_op jit(solution)/shard_map/all_gather | solution.py:245
  8.0 1.6 copy-start.19
  8.0 2.0 copy-start.20
  11.7 262.7 %all-gather.6.cloned.1.call-start = ((), (), s32[]{:S(2)}) async-start(), calls=%async_computation.1 | async-start | bytes 7864320 | tf_op jit(solution)/shard_map/all_gather | solution.py:245
  13.3 376.2 %all-gather.4.cloned.1.call-start = ((), (), s32[]{:S(2)}) async-start(), calls=%async_computation | async-start | bytes 7864320 | tf_op jit(solution)/shard_map/all_gather | solution.py:245
  15.9 21.8 %collective-permute-start = (bf16[2,128,768]{2,1,0:T(8,128)(2,1)S(1)}, bf16[2,128,768]{2,1,0:T(8,128)(2,1)S(1)}, u32[]{:S(2)}, u32[]{:S(2)}) collective-permute-start(bf16[2,128,768]{2,1,0:T(8,128)(2,1)S(1)} %get-tuple-element.44), channel_id=1, source_target_pairs={{0,4},{4,8},{8,12},{12,0},{1,5},{5,9},{9,13},{13,1},{2,6},{6,10},{... | collective-permute-start | bytes 1179656 | tf_op jit(solution)/shard_map/ppermute | solution.py:202
  20.9 49.2 %collective-permute-start.1 = (bf16[2,128,768]{2,1,0:T(8,128)(2,1)S(1)}, bf16[2,128,768]{2,1,0:T(8,128)(2,1)S(1)}, u32[]{:S(2)}, u32[]{:S(2)}) collective-permute-start(bf16[2,128,768]{2,1,0:T(8,128)(2,1)S(1)} %get-tuple-element.43), channel_id=1, source_target_pairs={{0,8},{4,12},{8,0},{12,4},{1,9},{5,13},{9,1},{13,5},{2,10},{6,14},... | collective-permute-start | bytes 1179656 | tf_op jit(solution)/shard_map/ppermute | solution.py:202
  25.4 44.7 %collective-permute-start.2 = (bf16[2,128,768]{2,1,0:T(8,128)(2,1)S(1)}, bf16[2,128,768]{2,1,0:T(8,128)(2,1)S(1)}, u32[]{:S(2)}, u32[]{:S(2)}) collective-permute-start(bf16[2,128,768]{2,1,0:T(8,128)(2,1)S(1)} %get-tuple-element.42), channel_id=1, source_target_pairs={{0,12},{4,0},{8,4},{12,8},{1,13},{5,1},{9,5},{13,9},{2,14},{6,2},{... | collective-permute-start | bytes 1179656 | tf_op jit(solution)/shard_map/ppermute | solution.py:202
  72.2 36.4 %collective-permute-start.3 = (bf16[2,512,768]{2,1,0:T(8,128)(2,1)}, bf16[2,512,768]{2,1,0:T(8,128)(2,1)}, u32[]{:S(2)}, u32[]{:S(2)}) collective-permute-start(bf16[2,512,768]{2,1,0:T(8,128)(2,1)} %fusion.17), channel_id=1, source_target_pairs={{0,2},{1,3},{2,0},{3,1},{4,6},{5,7},{6,4},{7,5},{8,10},{9,11},{10,... | collective-permute-start | bytes 4718600 | tf_op jit(solution)/shard_map/ppermute | solution.py:214
  110.7 1.9 copy-start.21
  112.7 6.0 collective-permute-start.4
  121.0 4.8 slice-start.2
  121.0 6.8 slice-start.3
  124.3 10.8 %copy-start.7 = (bf16[1,2,512,768]{3,2,1,0:T(8,128)(2,1)}, bf16[1,2,512,768]{3,2,1,0:T(8,128)(2,1)S(1)}, u32[]{:S(2)}) copy-start(bf16[1,2,512,768]{3,2,1,0:T(8,128)(2,1)S(1)} %get-tuple-element.24) | copy-start | bytes 4718596
  124.3 10.8 %copy-start.8 = (bf16[1,2,512,768]{3,2,1,0:T(8,128)(2,1)}, bf16[1,2,512,768]{3,2,1,0:T(8,128)(2,1)S(1)}, u32[]{:S(2)}) copy-start(bf16[1,2,512,768]{3,2,1,0:T(8,128)(2,1)S(1)} %get-tuple-element.77) | copy-start | bytes 4718596
  124.3 10.8 %copy-start.9 = (bf16[1,2,512,768]{3,2,1,0:T(8,128)(2,1)}, bf16[1,2,512,768]{3,2,1,0:T(8,128)(2,1)S(1)}, u32[]{:S(2)}) copy-start(bf16[1,2,512,768]{3,2,1,0:T(8,128)(2,1)S(1)} %get-tuple-element.78) | copy-start | bytes 4718596
  127.8 7.6 %copy-start.6 = (f32[1,3072]{1,0:T(1,128)S(1)}, f32[1,3072]{1,0:T(1,128)}, u32[]{:S(2)}) copy-start(f32[1,3072]{1,0:T(1,128)} %refs_8_.7) | copy-start | bytes 36868
  135.4 254.1 %copy-start.3 = (f32[1024,1]{1,0:T(8,128)}, f32[1024,1]{1,0:T(8,128)S(1)}, u32[]{:S(2)}) copy-start(f32[1024,1]{1,0:T(8,128)S(1)} %copy.21.refs_7_) | copy-start | bytes 12292
  406.5 2.2 copy-start.2
  406.6 2.2 copy-start.4
  408.7 18.8 %collective-permute-start.7 = (bf16[2,512,768]{2,1,0:T(8,128)(2,1)}, bf16[2,512,768]{2,1,0:T(8,128)(2,1)}, u32[]{:S(2)}, u32[]{:S(2)}) collective-permute-start(bf16[2,512,768]{2,1,0:T(8,128)(2,1)} %dynamic-slice_bitcast_fusion.2), channel_id=1, source_target_pairs={{0,1},{1,0},{2,3},{3,2},{4,5},{5,4},{6,7},{7,6},{8,9},{9,8},{10,11... | collective-permute-start | bytes 4718600 | tf_op jit(solution)/shard_map/ppermute | solution.py:214
  427.1 5.3 collective-permute-start.5
  429.8 4.4 copy-start.10
  430.9 20.7 %collective-permute-start.8 = (bf16[512,768]{1,0:T(8,128)(2,1)}, bf16[512,768]{1,0:T(8,128)(2,1)}, u32[]{:S(2)}, u32[]{:S(2)}) collective-permute-start(bf16[512,768]{1,0:T(8,128)(2,1)} %fusion.31), channel_id=1, source_target_pairs={{0,2},{1,3},{2,0},{3,1},{4,6},{5,7},{6,4},{7,5},{8,10},{9,11},{10,... | collective-permute-start | bytes 2359304 | tf_op jit(solution)/shard_map/ppermute | solution.py:214
  434.1 1.7 copy-start.11
  434.2 43.7 %copy-start.15 = (bf16[2,512,768]{2,1,0:T(8,128)(2,1)S(1)}, bf16[2,512,768]{2,1,0:T(8,128)(2,1)}, u32[]{:S(2)}) copy-start(bf16[2,512,768]{2,1,0:T(8,128)(2,1)} %get-tuple-element.80) | copy-start | bytes 4718596
  435.8 31.6 %collective-permute-start.6 = (bf16[512,768]{1,0:T(8,128)(2,1)S(1)}, bf16[512,768]{1,0:T(8,128)(2,1)S(1)}, u32[]{:S(2)}, u32[]{:S(2)}) collective-permute-start(bf16[512,768]{1,0:T(8,128)(2,1)S(1)} %fusion.30), channel_id=1, source_target_pairs={{0,2},{1,3},{2,0},{3,1},{4,6},{5,7},{6,4},{7,5},{8,10},{9,11},{10,... | collective-permute-start | bytes 2359304 | tf_op jit(solution)/shard_map/ppermute | solution.py:214
  467.5 10.4 %slice-start.4 = ((s8[6291456]{0:T(1024)(128)(4,1)}), s8[4194304]{0:T(1024)(128)(4,1)S(1)}, s32[]{:S(2)}) async-start(s8[6291456]{0:T(1024)(128)(4,1)} %bitcast.228), calls=%async_computation.7 | async-start | bytes 8388608
  467.5 10.4 %slice-start.5 = ((s8[6291456]{0:T(1024)(128)(4,1)}), s8[2097152]{0:T(1024)(128)(4,1)S(1)}, s32[]{:S(2)}) async-start(s8[6291456]{0:T(1024)(128)(4,1)} %bitcast.228), calls=%async_computation.8 | async-start | bytes 4194304
  467.5 10.4 %copy-start.14 = (bf16[2,512,768]{2,1,0:T(8,128)(2,1)S(1)}, bf16[2,512,768]{2,1,0:T(8,128)(2,1)}, u32[]{:S(2)}) copy-start(bf16[2,512,768]{2,1,0:T(8,128)(2,1)} %get-tuple-element.79) | copy-start | bytes 4718596
  471.6 10.6 %copy-start.16 = (bf16[512,768]{1,0:T(8,128)(2,1)}, bf16[512,768]{1,0:T(8,128)(2,1)S(1)}, u32[]{:S(2)}) copy-start(bf16[512,768]{1,0:T(8,128)(2,1)S(1)} %get-tuple-element.11) | copy-start | bytes 2359300
  471.6 6.3 copy-start.12
  471.6 6.3 copy-start.13
  472.5 12.7 %collective-permute-start.10 = (bf16[1,128,768]{1,2,0:T(8,128)(2,1)S(1)}, bf16[1,128,768]{1,2,0:T(8,128)(2,1)S(1)}, u32[]{:S(2)}, u32[]{:S(2)}) collective-permute-start(bf16[1,128,768]{1,2,0:T(8,128)(2,1)S(1)} %get-tuple-element.64), channel_id=1, source_target_pairs={{16,4},{20,8},{24,12},{28,0},{17,5},{21,9},{25,13},{29,1},{18,6},{... | collective-permute-start | bytes 589832 | tf_op jit(solution)/shard_map/ppermute | solution.py:202
  473.9 17.8 %collective-permute-start.11 = (bf16[1,128,768]{1,2,0:T(8,128)(2,1)S(1)}, bf16[1,128,768]{1,2,0:T(8,128)(2,1)S(1)}, u32[]{:S(2)}, u32[]{:S(2)}) collective-permute-start(bf16[1,128,768]{1,2,0:T(8,128)(2,1)S(1)} %get-tuple-element.63), channel_id=1, source_target_pairs={{16,8},{20,12},{24,0},{28,4},{17,9},{21,13},{25,1},{29,5},{18,10},... | collective-permute-start | bytes 589832 | tf_op jit(solution)/shard_map/ppermute | solution.py:202
  475.2 16.5 %collective-permute-start.12 = (bf16[1,128,768]{1,2,0:T(8,128)(2,1)S(1)}, bf16[1,128,768]{1,2,0:T(8,128)(2,1)S(1)}, u32[]{:S(2)}, u32[]{:S(2)}) collective-permute-start(bf16[1,128,768]{1,2,0:T(8,128)(2,1)S(1)} %get-tuple-element.62), channel_id=1, source_target_pairs={{16,12},{20,0},{24,4},{28,8},{17,13},{21,1},{25,5},{29,9},{18,14},... | collective-permute-start | bytes 589832 | tf_op jit(solution)/shard_map/ppermute | solution.py:202
  476.5 19.3 %collective-permute-start.9 = (bf16[1,128,768]{1,2,0:T(8,128)(2,1)S(1)}, bf16[1,128,768]{1,2,0:T(8,128)(2,1)S(1)}, u32[]{:S(2)}, u32[]{:S(2)}) collective-permute-start(bf16[1,128,768]{1,2,0:T(8,128)(2,1)S(1)} %get-tuple-element.61), channel_id=1, source_target_pairs={{16,0},{20,4},{24,8},{28,12},{17,1},{21,5},{25,9},{29,13},{18,2},{... | collective-permute-start | bytes 589832 | tf_op jit(solution)/shard_map/ppermute | solution.py:202
  477.8 21.0 %slice-start = ((s8[6291456]{0:T(1024)(128)(4,1)}), s8[4194304]{0:T(1024)(128)(4,1)S(1)}, s32[]{:S(2)}) async-start(s8[6291456]{0:T(1024)(128)(4,1)} %bitcast.218), calls=%async_computation.3 | async-start | bytes 8388608
  477.9 21.0 %slice-start.1 = ((s8[6291456]{0:T(1024)(128)(4,1)}), s8[2097152]{0:T(1024)(128)(4,1)S(1)}, s32[]{:S(2)}) async-start(s8[6291456]{0:T(1024)(128)(4,1)} %bitcast.218), calls=%async_computation.4 | async-start | bytes 4194304
  497.4 19.8 %collective-permute-start.13 = (bf16[512,768]{1,0:T(8,128)(2,1)}, bf16[512,768]{1,0:T(8,128)(2,1)}, u32[]{:S(2)}, u32[]{:S(2)}) collective-permute-start(bf16[512,768]{1,0:T(8,128)(2,1)} %fusion.21), channel_id=1, source_target_pairs={{0,2},{1,3},{2,0},{3,1},{4,6},{5,7},{6,4},{7,5},{8,10},{9,11},{10,... | collective-permute-start | bytes 2359304 | tf_op jit(solution)/shard_map/ppermute | solution.py:214
  500.9 115.1 %copy-start = (bf16[512,3072]{1,0:T(8,128)(2,1)}, bf16[512,3072]{1,0:T(8,128)(2,1)S(1)}, u32[]{:S(2)}) copy-start(bf16[512,3072]{1,0:T(8,128)(2,1)S(1)} %get-tuple-element.10.refs_2_) | copy-start | bytes 9437188
  504.2 21.1 %collective-permute-start.20 = (bf16[1,128,768]{1,2,0:T(8,128)(2,1)S(1)}, bf16[1,128,768]{1,2,0:T(8,128)(2,1)S(1)}, u32[]{:S(2)}, u32[]{:S(2)}) collective-permute-start(bf16[1,128,768]{1,2,0:T(8,128)(2,1)S(1)} %get-tuple-element.69), channel_id=1, source_target_pairs={{16,0},{20,4},{24,8},{28,12},{17,1},{21,5},{25,9},{29,13},{18,2},{... | collective-permute-start | bytes 589832 | tf_op jit(solution)/shard_map/ppermute | solution.py:202
  505.5 19.8 %collective-permute-start.21 = (bf16[1,128,768]{1,2,0:T(8,128)(2,1)S(1)}, bf16[1,128,768]{1,2,0:T(8,128)(2,1)S(1)}, u32[]{:S(2)}, u32[]{:S(2)}) collective-permute-start(bf16[1,128,768]{1,2,0:T(8,128)(2,1)S(1)} %get-tuple-element.72), channel_id=1, source_target_pairs={{16,4},{20,8},{24,12},{28,0},{17,5},{21,9},{25,13},{29,1},{18,6},{... | collective-permute-start | bytes 589832 | tf_op jit(solution)/shard_map/ppermute | solution.py:202
  506.8 18.5 %collective-permute-start.22 = (bf16[1,128,768]{1,2,0:T(8,128)(2,1)S(1)}, bf16[1,128,768]{1,2,0:T(8,128)(2,1)S(1)}, u32[]{:S(2)}, u32[]{:S(2)}) collective-permute-start(bf16[1,128,768]{1,2,0:T(8,128)(2,1)S(1)} %get-tuple-element.71), channel_id=1, source_target_pairs={{16,8},{20,12},{24,0},{28,4},{17,9},{21,13},{25,1},{29,5},{18,10},... | collective-permute-start | bytes 589832 | tf_op jit(solution)/shard_map/ppermute | solution.py:202
  508.1 17.2 %collective-permute-start.23 = (bf16[1,128,768]{1,2,0:T(8,128)(2,1)S(1)}, bf16[1,128,768]{1,2,0:T(8,128)(2,1)S(1)}, u32[]{:S(2)}, u32[]{:S(2)}) collective-permute-start(bf16[1,128,768]{1,2,0:T(8,128)(2,1)S(1)} %get-tuple-element.70), channel_id=1, source_target_pairs={{16,12},{20,0},{24,4},{28,8},{17,13},{21,1},{25,5},{29,9},{18,14},... | collective-permute-start | bytes 589832 | tf_op jit(solution)/shard_map/ppermute | solution.py:202
  518.8 27.9 %collective-permute-start.14 = (bf16[2,512,768]{2,1,0:T(8,128)(2,1)S(1)}, bf16[2,512,768]{2,1,0:T(8,128)(2,1)S(1)}, u32[]{:S(2)}, u32[]{:S(2)}) collective-permute-start(bf16[2,512,768]{2,1,0:T(8,128)(2,1)S(1)} %pad_maximum_fusion.6), channel_id=1, source_target_pairs={{0,1},{1,0},{2,3},{3,2},{4,5},{5,4},{6,7},{7,6},{8,9},{9,8},{10,11... | collective-permute-start | bytes 4718600 | tf_op jit(solution)/shard_map/ppermute | solution.py:214
  525.9 19.4 %collective-permute-start.24 = (bf16[512,768]{1,0:T(8,128)(2,1)S(1)}, bf16[512,768]{1,0:T(8,128)(2,1)S(1)}, u32[]{:S(2)}, u32[]{:S(2)}) collective-permute-start(bf16[512,768]{1,0:T(8,128)(2,1)S(1)} %fusion.24), channel_id=1, source_target_pairs={{0,2},{1,3},{2,0},{3,1},{4,6},{5,7},{6,4},{7,5},{8,10},{9,11},{10,... | collective-permute-start | bytes 2359304 | tf_op jit(solution)/shard_map/ppermute | solution.py:214
  546.7 51.2 %collective-permute-start.25 = (bf16[2,512,768]{2,1,0:T(8,128)(2,1)}, bf16[2,512,768]{2,1,0:T(8,128)(2,1)}, u32[]{:S(2)}, u32[]{:S(2)}) collective-permute-start(bf16[2,512,768]{2,1,0:T(8,128)(2,1)} %pad_maximum_fusion.7), channel_id=1, source_target_pairs={{0,1},{1,0},{2,3},{3,2},{4,5},{5,4},{6,7},{7,6},{8,9},{9,8},{10,11... | collective-permute-start | bytes 4718600 | tf_op jit(solution)/shard_map/ppermute | solution.py:214
  547.2 3.0 copy-start.1
  564.6 15.4 %copy-start.5 = (f32[512,1]{1,0:T(8,128)S(1)}, f32[512,1]{1,0:T(8,128)}, u32[]{:S(2)}) copy-start(f32[512,1]{1,0:T(8,128)} %copy.25.refs_7_) | copy-start | bytes 6148
  597.4 51.5 %collective-permute-start.15 = (bf16[2,512,768]{2,1,0:T(8,128)(2,1)S(1)}, bf16[2,512,768]{2,1,0:T(8,128)(2,1)S(1)}, u32[]{:S(2)}, u32[]{:S(2)}) collective-permute-start(bf16[2,512,768]{2,1,0:T(8,128)(2,1)S(1)} %dynamic-slice_bitcast_fusion.1), channel_id=1, source_target_pairs={{0,1},{1,0},{2,3},{3,2},{4,5},{5,4},{6,7},{7,6},{8,9},{9,8},{10,11... | collective-permute-start | bytes 4718600 | tf_op jit(solution)/shard_map/ppermute | solution.py:214
  648.8 3.5 collective-permute-start.26
  649.3 20.4 %collective-permute-start.16 = (bf16[512,768]{1,0:T(8,128)(2,1)S(1)}, bf16[512,768]{1,0:T(8,128)(2,1)S(1)}, u32[]{:S(2)}, u32[]{:S(2)}) collective-permute-start(bf16[512,768]{1,0:T(8,128)(2,1)S(1)} %fusion.32), channel_id=1, source_target_pairs={{0,2},{1,3},{2,0},{3,1},{4,6},{5,7},{6,4},{7,5},{8,10},{9,11},{10,... | collective-permute-start | bytes 2359304 | tf_op jit(solution)/shard_map/ppermute | solution.py:214
  652.7 33.5 %collective-permute-start.27 = (bf16[512,768]{1,0:T(8,128)(2,1)S(1)}, bf16[512,768]{1,0:T(8,128)(2,1)S(1)}, u32[]{:S(2)}, u32[]{:S(2)}) collective-permute-start(bf16[512,768]{1,0:T(8,128)(2,1)S(1)} %fusion.33), channel_id=1, source_target_pairs={{0,2},{1,3},{2,0},{3,1},{4,6},{5,7},{6,4},{7,5},{8,10},{9,11},{10,... | collective-permute-start | bytes 2359304 | tf_op jit(solution)/shard_map/ppermute | solution.py:214
  671.6 24.0 %collective-permute-start.17 = (bf16[1,128,768]{2,1,0:T(8,128)(2,1)S(1)}, bf16[1,128,768]{2,1,0:T(8,128)(2,1)S(1)}, u32[]{:S(2)}, u32[]{:S(2)}) collective-permute-start(bf16[1,128,768]{2,1,0:T(8,128)(2,1)S(1)} %get-tuple-element.60), channel_id=1, source_target_pairs={{0,4},{4,8},{8,12},{12,0},{1,5},{5,9},{9,13},{13,1},{2,6},{6,10},{... | collective-permute-start | bytes 589832 | tf_op jit(solution)/shard_map/ppermute | solution.py:202
  678.3 21.6 %collective-permute-start.18 = (bf16[1,128,768]{2,1,0:T(8,128)(2,1)S(1)}, bf16[1,128,768]{2,1,0:T(8,128)(2,1)S(1)}, u32[]{:S(2)}, u32[]{:S(2)}) collective-permute-start(bf16[1,128,768]{2,1,0:T(8,128)(2,1)S(1)} %get-tuple-element.59), channel_id=1, source_target_pairs={{0,8},{4,12},{8,0},{12,4},{1,9},{5,13},{9,1},{13,5},{2,10},{6,14},... | collective-permute-start | bytes 589832 | tf_op jit(solution)/shard_map/ppermute | solution.py:202
  680.2 19.7 %collective-permute-start.19 = (bf16[1,128,768]{2,1,0:T(8,128)(2,1)S(1)}, bf16[1,128,768]{2,1,0:T(8,128)(2,1)S(1)}, u32[]{:S(2)}, u32[]{:S(2)}) collective-permute-start(bf16[1,128,768]{2,1,0:T(8,128)(2,1)S(1)} %get-tuple-element.58), channel_id=1, source_target_pairs={{0,12},{4,0},{8,4},{12,8},{1,13},{5,1},{9,5},{13,9},{2,14},{6,2},{... | collective-permute-start | bytes 589832 | tf_op jit(solution)/shard_map/ppermute | solution.py:202
  687.0 13.6 %collective-permute-start.28 = (bf16[1,128,768]{2,1,0:T(8,128)(2,1)S(1)}, bf16[1,128,768]{2,1,0:T(8,128)(2,1)S(1)}, u32[]{:S(2)}, u32[]{:S(2)}) collective-permute-start(bf16[1,128,768]{2,1,0:T(8,128)(2,1)S(1)} %get-tuple-element.68), channel_id=1, source_target_pairs={{0,4},{4,8},{8,12},{12,0},{1,5},{5,9},{9,13},{13,1},{2,6},{6,10},{... | collective-permute-start | bytes 589832 | tf_op jit(solution)/shard_map/ppermute | solution.py:202
  693.7 14.2 %collective-permute-start.29 = (bf16[1,128,768]{2,1,0:T(8,128)(2,1)S(1)}, bf16[1,128,768]{2,1,0:T(8,128)(2,1)S(1)}, u32[]{:S(2)}, u32[]{:S(2)}) collective-permute-start(bf16[1,128,768]{2,1,0:T(8,128)(2,1)S(1)} %get-tuple-element.67), channel_id=1, source_target_pairs={{0,8},{4,12},{8,0},{12,4},{1,9},{5,13},{9,1},{13,5},{2,10},{6,14},... | collective-permute-start | bytes 589832 | tf_op jit(solution)/shard_map/ppermute | solution.py:202
  695.6 12.3 %collective-permute-start.30 = (bf16[1,128,768]{2,1,0:T(8,128)(2,1)S(1)}, bf16[1,128,768]{2,1,0:T(8,128)(2,1)S(1)}, u32[]{:S(2)}, u32[]{:S(2)}) collective-permute-start(bf16[1,128,768]{2,1,0:T(8,128)(2,1)S(1)} %get-tuple-element.66), channel_id=1, source_target_pairs={{0,12},{4,0},{8,4},{12,8},{1,13},{5,1},{9,5},{13,9},{2,14},{6,2},{... | collective-permute-start | bytes 589832 | tf_op jit(solution)/shard_map/ppermute | solution.py:202
  700.5 8.0 %copy-start.17 = (bf16[512,768]{1,0:T(8,128)(2,1)S(1)}, bf16[512,768]{1,0:T(8,128)(2,1)}, u32[]{:S(2)}) copy-start(bf16[512,768]{1,0:T(8,128)(2,1)} %copy-done.16) | copy-start | bytes 2359300
  700.5 8.0 %copy-start.18 = (bf16[512,768]{1,0:T(8,128)(2,1)S(1)}, bf16[512,768]{1,0:T(8,128)(2,1)}, u32[]{:S(2)}) copy-start(bf16[512,768]{1,0:T(8,128)(2,1)} %get-tuple-element.12) | copy-start | bytes 2359300
Sparse Core Ops, SparseCore 0:
  11.8 147.1 all-gather.7
  160.5 113.7 all-gather.5
  275.9 113.5 all-gather.3

commit v2 on v1

v2 whole, which is shorter than its diff:
```python
import functools

import jax
import jax.numpy as jnp
from jax import lax
from jax.experimental import pallas as pl
from jax.experimental.pallas import tpu as pltpu
from jax.sharding import PartitionSpec as P

FRAMES = 16
EPS = 1e-06


def dot_nn(left, right):
    return lax.dot_general(left, right, (((1,), (0,)), ((), ())), preferred_element_type=jnp.float32)


def dot_nt(left, right):
    return lax.dot_general(left, right, (((1,), (1,)), ((), ())), preferred_element_type=jnp.float32)


def dot_tn(left, right):
    return lax.dot_general(left, right, (((0,), (0,)), ((), ())), preferred_element_type=jnp.float32)


def head_norm(raw_rows):
    scale_rows = lax.rsqrt(jnp.mean(raw_rows * raw_rows, axis=-1, keepdims=True) + EPS)
    return raw_rows * scale_rows, scale_rows


def norm_back(grad_low, normal_hat, scale_rows, gain_vec):
    grad_hat = grad_low.astype(jnp.float32) * gain_vec
    inner_mean = jnp.mean(grad_hat * normal_hat, axis=-1, keepdims=True)
    return (scale_rows * (grad_hat - normal_hat * inner_mean)).astype(jnp.bfloat16)


def attend_back(units, mask):
    scores = [dot_nt(key, query) for query, key, _, _ in units]
    dprobs = [dot_nt(value, grad) for _, _, value, grad in units]
    expo = [jnp.exp(score) * mask for score in scores]
    probs = [x * (1.0 / jnp.sum(x, axis=0, keepdims=True)) for x in expo]
    inner = [jnp.sum(p * d, axis=0, keepdims=True) for p, d in zip(probs, dprobs)]
    dscores = [(p * (d - i)).astype(jnp.bfloat16) for p, d, i in zip(probs, dprobs, inner)]
    dvalues = [dot_nn(p.astype(jnp.bfloat16), unit[3]) for p, unit in zip(probs, units)]
    dkeys = [dot_nn(d, unit[0]) for d, unit in zip(dscores, units)]
    dqueries = [dot_tn(d, unit[1]) for d, unit in zip(dscores, units)]
    return [
        tuple(x.astype(jnp.bfloat16) for x in triple) for triple in zip(dqueries, dkeys, dvalues)
    ]


def raw_kernel(source_ref, low_ref, *refs):
    *piece_refs, raw_ref = refs
    total = None
    for slot, piece_ref in enumerate(piece_refs):
        depth = piece_ref.shape[0]
        start = pl.multiple_of(source_ref[slot] * depth, depth)
        part = dot_nn(low_ref[:, pl.ds(start, depth)], piece_ref[...])
        total = part if total is None else total + part
    raw_ref[...] = total


def run_raw(sources, low, pieces):
    rows, feat = low.shape
    columns = pieces[0].shape[1]
    tile = rows // 4
    once = pl.Buffered(1)
    return pl.pallas_call(
        raw_kernel,
        grid_spec=pltpu.PrefetchScalarGridSpec(
            num_scalar_prefetch=1,
            grid=(rows // tile,),
            in_specs=[pl.BlockSpec((tile, feat), lambda i, source: (i, 0))]
            + [
                pl.BlockSpec(piece.shape, lambda i, source: (0, 0), pipeline_mode=once)
                for piece in pieces
            ],
            out_specs=pl.BlockSpec((tile, columns), lambda i, source: (i, 0)),
        ),
        out_shape=jax.ShapeDtypeStruct((rows, columns), jnp.float32),
        compiler_params=pltpu.CompilerParams(
            dimension_semantics=("arbitrary",), vmem_limit_bytes=40 << 20
        ),
        cost_estimate=pl.CostEstimate(
            flops=2 * rows * feat * columns,
            bytes_accessed=2 * feat * columns + 2 * rows * feat + 4 * rows * columns,
            transcendentals=0,
        ),
        name="raw_products",
    )(sources, low, *pieces)


def back_kernel(chunks, slots, head_dim, first_grad, first_saved, flag_ref, source_ref, *refs):
    @pl.when(flag_ref[0] == 1)
    def _():
        back_body(chunks, slots, head_dim, first_grad, first_saved, source_ref, *refs)


def back_body(chunks, slots, head_dim, first_grad, first_saved, source_ref, *refs):
    (mask_ref, gains_ref, inv_ref, gain_ref, grad_hbm, saved_hbm), refs = refs[:6], refs[6:]
    raw_hbm, refs = refs[:chunks], refs[chunks:]
    out_weight_hbm, refs = refs[:slots], refs[slots:]
    weight_hbm, refs = refs[: chunks * slots], refs[chunks * slots :]
    term_hbm, grad_ref, saved_ref, raw_ref, out_weight_ref, weight_ref = refs[:6]
    total_ref, packed_ref, term_ref, arrived = refs[6:]
    rows, feat = grad_ref.shape
    block = mask_ref.shape[0]
    depth, columns = weight_hbm[0].shape
    width = columns // 3
    places = [pl.multiple_of(source_ref[slot] * depth, depth) for slot in range(slots)]
    started = [0]

    def start(source, target):
        copy = pltpu.make_async_copy(source, target, arrived.at[started[0]])
        started[0] += 1
        copy.start()
        return copy

    get_first = [start(grad_hbm.at[pl.ds(first_grad, rows)], grad_ref)]
    for slot in range(slots):
        target = out_weight_ref.at[:, pl.ds(places[slot], depth)]
        get_first.append(start(out_weight_hbm[slot], target))
    get_raw = [
        start(raw_hbm[chunk].at[pl.ds(first_saved, rows)], raw_ref.at[chunk])
        for chunk in range(chunks)
    ]
    for copy in get_first:
        copy.wait()
    get_rest = []
    for slot in range(slots):
        for chunk in range(chunks):
            target = weight_ref.at[pl.ds(places[slot], depth), pl.ds(chunk * columns, columns)]
            get_rest.append(start(weight_hbm[chunk * slots + slot], target))
    get_rest.append(start(saved_hbm.at[pl.ds(first_saved, rows)], saved_ref))

    query_gain, key_gain = gains_ref[0:1, :], gains_ref[1:2, :]
    mask = mask_ref[...]
    grad_attn = dot_nt(grad_ref[...], out_weight_ref[...]).astype(jnp.bfloat16)
    for chunk in range(chunks):
        get_raw[chunk].wait()
        for head in range(width // head_dim):
            query_cols = slice(head * head_dim, (head + 1) * head_dim)
            key_cols = slice(width + query_cols.start, width + query_cols.stop)
            value_cols = slice(2 * width + query_cols.start, 2 * width + query_cols.stop)
            grad_cols = slice(chunk * width + query_cols.start, chunk * width + query_cols.stop)

            def out_cols(cols):
                return slice(chunk * columns + cols.start, chunk * columns + cols.stop)

            for begin in range(0, rows, 4 * block):
                owns = [
                    slice(first, first + block)
                    for first in range(begin, min(rows, begin + 4 * block), block)
                ]
                queries = [head_norm(raw_ref[chunk, own, query_cols]) for own in owns]
                keys = [head_norm(raw_ref[chunk, own, key_cols]) for own in owns]
                units = [
                    (
                        (query[0] * query_gain).astype(jnp.bfloat16),
                        (key[0] * key_gain).astype(jnp.bfloat16),
                        raw_ref[chunk, own, value_cols].astype(jnp.bfloat16),
                        grad_attn[own, grad_cols],
                    )
                    for own, query, key in zip(owns, queries, keys)
                ]
                backs = attend_back(units, mask)
                for own, query, key, (dquery, dkey, dvalue) in zip(owns, queries, keys, backs):
                    packed_ref[own, out_cols(query_cols)] = norm_back(dquery, *query, query_gain)
                    packed_ref[own, out_cols(key_cols)] = norm_back(dkey, *key, key_gain)
                    packed_ref[own, out_cols(value_cols)] = dvalue
    for copy in get_rest:
        copy.wait()
    shares, _, share_width = term_ref.shape
    packed = packed_ref[...]
    for share in range(shares):
        part = slice(share * share_width, (share + 1) * share_width)
        total_ref[:, part] = dot_nt(packed, weight_ref[part, :])
    sends = []
    for first in range(0, rows, block):
        own = slice(first, first + block)
        inv_rms = inv_ref[first_saved + first : first_saved + first + block, :]
        normed = saved_ref[own, :].astype(jnp.float32) * inv_rms
        grad_hat = total_ref[own, :] * gain_ref[...]
        inner_mean = jnp.mean(grad_hat * normed, axis=-1, keepdims=True)
        term = (inv_rms * (grad_hat - normed * inner_mean)).astype(jnp.bfloat16)
        for share in range(shares):
            term_ref[share, own, :] = term[:, share * share_width : (share + 1) * share_width]
        window = pl.ds(first, block)
        sends.append(start(term_ref.at[:, window], term_hbm.at[:, window]))
    for send in sends:
        send.wait()


def run_back(flag, sources, mask, gains, inv_rms, gain_row, grad, first_grad, saved, first_saved, rows, raws, out_pieces, pieces, shares, head_dim):
    feat = grad.shape[1]
    chunks, slots = len(raws), len(out_pieces)
    columns = pieces[0][0].shape[1]
    heads_width = out_pieces[0].shape[0]
    share_width = feat // shares
    block = mask.shape[0]
    vmem = pl.BlockSpec(memory_space=pltpu.VMEM)
    smem = pl.BlockSpec(memory_space=pltpu.SMEM)
    anywhere = pl.BlockSpec(memory_space=pl.ANY)
    arrays = [grad, saved, *raws, *out_pieces, *(piece for group in pieces for piece in group)]
    copies = len(arrays) + rows // block
    return pl.pallas_call(
        functools.partial(back_kernel, chunks, slots, head_dim, first_grad, first_saved),
        in_specs=[smem] * 2 + [vmem] * 4 + [anywhere] * len(arrays),
        out_specs=anywhere,
        out_shape=jax.ShapeDtypeStruct((shares, rows, share_width), jnp.bfloat16),
        scratch_shapes=[
            pltpu.VMEM((rows, feat), jnp.bfloat16),
            pltpu.VMEM((rows, feat), jnp.bfloat16),
            pltpu.VMEM((chunks, rows, columns), jnp.float32),
            pltpu.VMEM((heads_width, feat), jnp.bfloat16),
            pltpu.VMEM((feat, chunks * columns), jnp.bfloat16),
            pltpu.VMEM((rows, feat), jnp.float32),
            pltpu.VMEM((rows, chunks * columns), jnp.bfloat16),
            pltpu.VMEM((shares, rows, share_width), jnp.bfloat16),
            pltpu.SemaphoreType.DMA((copies,)),
        ],
        compiler_params=pltpu.CompilerParams(vmem_limit_bytes=56 << 20),
        cost_estimate=pl.CostEstimate(
            flops=16 * rows * feat * heads_width,
            bytes_accessed=8 * feat * heads_width + 6 * rows * feat,
            transcendentals=rows * heads_width,
        ),
        name="sublayer_back",
    )(flag, sources, mask, gains, inv_rms, gain_row, *arrays)


def on_device(inputs, upstream, norm_gain, head_gain, w_query, w_key, w_value, w_out):
    on_last = lax.axis_index("section") == 1
    frame_count, head_count = lax.axis_size("frame"), lax.axis_size("head")
    my_frame, my_head = lax.axis_index("frame"), lax.axis_index("head")
    batches, frames, patches, feat = inputs.shape[1:]
    rows = frames * patches
    total_frames = frames * frame_count
    few = patches // frame_count
    piece = frames * few
    head_dim = head_gain.shape[-1]
    share = feat // head_count
    local_width = w_query.shape[2]
    width = 2 * head_dim if local_width % (2 * head_dim) == 0 else head_dim
    chunks = local_width // width
    gain_row = norm_gain
    gains = jnp.stack([head_gain[0, 0] * head_dim ** (-0.5), head_gain[0, 1]])

    def reorder(array_in, source):
        pick = (source[:, None] == jnp.arange(rows)[None, :]).astype(jnp.bfloat16)
        flat = array_in.reshape(-1, rows, array_in.shape[-1])
        moved = jnp.einsum("rs,bsc->brc", pick, flat, preferred_element_type=jnp.float32)
        return moved.astype(jnp.bfloat16)

    index = jnp.arange(rows)
    shift, in_frame, in_few = index // piece, (index % piece) // few, index % few
    target = (my_frame + shift) % frame_count
    leave_space = in_frame * patches + target * few + in_few
    leave_time = in_few * total_frames + target * frames + in_frame
    time_patch, time_frame = index // total_frames, index % total_frames
    enter_time = (
        ((my_frame - time_frame // frames) % frame_count) * piece
        + (time_frame % frames) * few
        + time_patch
    )
    space_frame, space_patch = index // patches, index % patches
    enter_space = (
        ((my_frame - space_patch // few) % frame_count) * piece
        + space_frame * few
        + space_patch % few
    )

    def send_rows(array_in, leave, from_section):
        sorted_rows = reorder(array_in, leave)
        parts = []
        for step in range(frame_count):
            part = sorted_rows[:, step * piece : (step + 1) * piece]
            if step or from_section:
                part = lax.ppermute(
                    part,
                    ("section", "frame"),
                    [
                        (from_section * frame_count + source, (source + step) % frame_count)
                        for source in range(frame_count)
                    ],
                )
            parts.append(part)
        return parts

    def place_rows(parts, enter):
        return reorder(jnp.concatenate(parts, axis=1), enter)

    def swap(array_in, bit):
        return lax.ppermute(array_in, "head", [(i, i ^ bit) for i in range(head_count)])

    my_core, my_side = my_head % 2, my_head // 2

    def gather_share(own):
        far = swap(own, 2)
        low_side = jnp.where(my_side == 0, own, far)
        high_side = jnp.where(my_side == 0, far, own)
        both = jnp.stack([low_side, high_side])
        other = swap(both, 1)
        first, second = jnp.where(my_core == 0, both, other), jnp.where(my_core == 0, other, both)
        return jnp.concatenate([first[0], second[0], first[1], second[1]], axis=-1)

    def core_sum(term):
        shaped = term.reshape(2, 2, *term.shape[1:])
        keep = lax.dynamic_index_in_dim(shaped, my_core, 1, keepdims=False)
        other = swap(lax.dynamic_index_in_dim(shaped, 1 - my_core, 1, keepdims=False), 1)
        pair = keep.astype(jnp.float32) + other.astype(jnp.float32)
        far = lax.dynamic_index_in_dim(pair, 1 - my_side, 0, keepdims=False).astype(jnp.bfloat16)
        return lax.dynamic_index_in_dim(pair, my_side, 0, keepdims=False), far

    def side_sum(own, far):
        return own + swap(far, 2).astype(jnp.float32)

    def my_share(array_in):
        return lax.dynamic_slice_in_dim(array_in, my_head * share, share, array_in.ndim - 1)

    def along(array_in, pairs):
        return lax.ppermute(array_in, "frame", pairs)

    at_end = jnp.logical_or(my_frame == 0, my_frame == 3)
    outer, inner = [(0, 1), (1, 0), (2, 3), (3, 2)], [(1, 2), (2, 1)]

    def fetch(shards):
        near = [along(x, outer) for x in shards]
        middle = [along(x, inner) for x in shards]
        across = [along(x, inner) for x in near]
        second = [jnp.where(at_end, along(x, outer), x) for x in middle]
        return near, second, across

    def last_hop(across):
        return jnp.where(at_end, along(across, outer), across)

    if frame_count == 4:
        upper = my_frame // 2
        sources = jnp.stack([my_frame, my_frame + 1 - 2 * (my_frame % 2), 2 - upper, 3 - 3 * upper])
    else:
        sources = jnp.zeros((1,), jnp.int32)
    sources = sources.astype(jnp.int32)

    shards = []
    for chunk in range(chunks):
        cols = slice(chunk * width, (chunk + 1) * width)
        columns = [w_query[0][:, cols], w_key[0][:, cols], w_value[0][:, cols]]
        shards.append(jnp.concatenate(columns, axis=1))
    shards.append(w_out[0])

    saved_space = inputs[0].reshape(batches, rows, feat)
    share_saved = my_share(saved_space)
    if frame_count == 4:
        near, second, across = fetch(shards)
    saved_time = gather_share(place_rows(send_rows(share_saved, leave_space, 0), enter_time))
    saved = jnp.where(on_last, saved_space, saved_time).reshape(batches * rows, feat)
    wide = saved.astype(jnp.float32)
    inv_rms = lax.rsqrt(jnp.mean(wide * wide, axis=-1, keepdims=True) + EPS)
    low = (wide * inv_rms * gain_row).astype(jnp.bfloat16)

    place = jnp.arange(patches) // FRAMES
    mask = jnp.where(on_last, 1.0, (place[:, None] == place[None, :]).astype(jnp.float32))
    raws, pieces = [], []
    if frame_count == 4:
        for chunk in range(chunks):
            pieces.append([shards[chunk], near[chunk], second[chunk], last_hop(across[chunk])])
            raws.append(run_raw(sources, low, pieces[-1]))
        *_, across[-1] = lax.optimization_barrier((*raws[:-1], across[-1]))
        out_pieces = [shards[-1], near[-1], second[-1], last_hop(across[-1])]
    else:
        for chunk in range(chunks):
            pieces.append([lax.all_gather(shards[chunk], "frame", axis=0, tiled=True)])
            raws.append(run_raw(sources, low, pieces[-1]))
        out_pieces = [lax.all_gather(shards[-1], "frame", axis=1, tiled=True)]
    flags = [(lax.axis_index("section") == s).astype(jnp.int32).reshape(1) for s in range(2)]
    halves = 2 if rows % (2 * patches) == 0 else 1

    def sublayer(flag, grad, first_grad, first, count):
        return run_back(
            flag, sources, mask, gains, inv_rms, gain_row, grad, first_grad, saved, first, count,
            raws, out_pieces, pieces, head_count, head_dim,
        )

    def in_parts(flag, grad, first_grad, b, count, tie=None):
        sums, first_term = [], None
        for start in range(0, rows, count):
            if tie is not None and start + count == rows:
                flag, tie = lax.optimization_barrier((flag, tie))
            term = sublayer(flag, grad, first_grad + start, b * rows + start, count)
            first_term = term if first_term is None else first_term
            sums.append(side_sum(*core_sum(term)))
        return jnp.concatenate(sums, axis=0), first_term, tie

    def add(residual, summed):
        return (residual.astype(jnp.float32) + summed).astype(jnp.bfloat16)

    grad_space = upstream.reshape(batches * rows, feat)
    share_space = my_share(upstream.reshape(batches, rows, feat))
    space_parts, sent, shares, fulls = [], [], [], []

    def receive(arrived):
        shares.append(place_rows(arrived, enter_time)[0])
        fulls.append(gather_share(shares[-1]))

    for b in range(batches):
        tie = space_parts[-1] if b else None
        count = rows // halves if b else rows
        summed, _, tie = in_parts(flags[1], grad_space, b * rows, b, count, tie)
        if b:
            space_parts[-1] = tie
            receive(send_rows(tie, leave_space, 1))
            summed, fulls[-1] = lax.optimization_barrier((summed, fulls[-1]))
        space_parts.append(add(share_space[b], summed))
    sent = send_rows(space_parts[-1], leave_space, 1)
    time_parts, returned, first_term = [], [], None
    for b in range(batches):
        if b == batches - 1:
            if b:
                sent, first_term = lax.optimization_barrier((sent, first_term))
            receive(sent)
        tie = time_parts[-1] if b else None
        summed, first_term, tie = in_parts(flags[0], fulls[b], 0, b, rows // halves, tie)
        if b:
            time_parts[-1] = tie
            returned.append(send_rows(tie, leave_time, 0))
        time_parts.append(add(shares[b], summed))
    returned.append(send_rows(time_parts[-1], leave_time, 0))
    time_parts = [place_rows(parts, enter_space)[0] for parts in returned]
    result = jnp.where(on_last, jnp.stack(space_parts), jnp.stack(time_parts))
    return result.reshape(1, batches, frames, patches, share)


def solution(mesh):
    in_specs = (
        P("section", None, "frame", None, None),
        P(None, "frame", None, None),
        P("section", None),
        P("section", None, None),
        P("section", "frame", "head"),
        P("section", "frame", "head"),
        P("section", "frame", "head"),
        P("section", "head", "frame"),
    )
    out_specs = P("section", None, "frame", None, "head")
    return jax.shard_map(
        on_device, mesh=mesh, in_specs=in_specs, out_specs=out_specs, check_vma=False
    )
```

time: 723 us -> 632 us (0.87)
  Pallas kernels: 179 us -> 89.5 us
  starting transfers between devices: 57.1 us -> 112 us
  waiting for transfers between devices: 372 us -> 338 us
  between operations: 14.4 us -> 1.46 us
    all_gather x3 -> x0, waiting for transfers between devices: 192 us -> none  [on_device(): lax.all_gather(pack(c), 'frame', axis=0, tiled=True)]
    ppermute x17 -> x37, waiting for transfers between devices: 68.9 us -> 256 us  [the longest x20 178 us: along(): return lax.ppermute(array_in, 'frame', pairs)]
    pallas_call x10, Pallas kernels: 179 us -> 89.5 us  [the longest x7 66.1 us: run_back(): pl.pallas_call(functools.partial(back_kernel, chunks, slots, head_dim, fi...]
    ppermute x17 -> x37, starting transfers between devices: 48.9 us -> 99.1 us  [the longest x20 56.7 us: along(): return lax.ppermute(array_in, 'frame', pairs)]
    ppermute x14 -> x20, waiting for transfers between devices: 111 us -> 81.6 us  [swap(): lax.ppermute(array_in, 'head', [(i, i ^ bit) for i in range(head_count)])]
    slice x13 -> x8, local copies, waits for them, and re-layouts: 12.7 us -> 1.12 us  [the longest x5 0.48 us: send_rows(): part = sorted_rows[:, step * piece:(step + 1) * piece]]
    select_n x1 -> x8, other arithmetic: 4.25 us -> 14 us  [the longest x4 7.03 us: fetch(): second = [jnp.where(at_end, along(x, outer), x) for x in middle]]
  transfers between devices with their start and end apart: 34 -> 57, of which waited for: 19 -> 26; matrix products, arithmetic and copies ran while one was open for 10% -> 8% of each run, Pallas kernels for 23% -> 12%
where the time goes in v2:
time: 632 us; the launch traced here: 626 us
  waiting for transfers between devices  338 us (53%)
  starting transfers between devices  112 us (18%)
  Pallas kernels  89.5 us (14%)
  other arithmetic  52 us (8%)
  local copies, waits for them, and re-layouts  24.7 us (4%)
  matrix products  8.69 us (1%)
    ppermute x20, waiting for transfers between devices, along(): return lax.ppermute(array_in, 'frame', pairs)  178 us
    ppermute x20, waiting for transfers between devices, swap(): lax.ppermute(array_in, 'head', [(i, i ^ bit) for i in range(head_count)])  81.6 us
    ppermute x17, waiting for transfers between devices, send_rows(): lax.ppermute(part, ('section', 'frame'), [(from_section * frame_count + s...  77.4 us
    pallas_call x7, Pallas kernels, run_back(): pl.pallas_call(functools.partial(back_kernel, chunks, slots, head_dim, fi...  66.1 us
    ppermute x20, starting transfers between devices, along(): return lax.ppermute(array_in, 'frame', pairs)  56.7 us
    ppermute x17, starting transfers between devices, send_rows(): lax.ppermute(part, ('section', 'frame'), [(from_section * frame_count + s...  42.4 us
    pallas_call x3, Pallas kernels, run_raw(): pl.pallas_call(raw_kernel, grid_spec=pltpu.PrefetchScalarGridSpec(num_sca...  23.4 us
    ppermute x20, starting transfers between devices, swap(): lax.ppermute(array_in, 'head', [(i, i ^ bit) for i in range(head_count)])  12.7 us
  transfers between devices with their start and end apart: 57, of which 26 were waited for; matrix products, arithmetic and copies ran while one was open for 8% of the time, Pallas kernels for 12%

profile of v2, /device:TPU:0, one launch (start us, length us, event | category | flops | bytes accessed | tf_op | source)
XLA Modules:
  0.0 625.7 jit_solution(17763279972897482904)
XLA Ops:
  1.7 2.4 fusion.12
  4.3 7.1 %collective-permute-start.2 = (bf16[2,128,768]{2,1,0:T(8,128)(2,1)S(1)}, bf16[2,128,768]{2,1,0:T(8,128)(2,1)S(1)}, u32[]{:S(2)}, u32[]{:S(2)}) collective-permute-start(bf16[2,128,768]{2,1,0:T(8,128)(2,1)S(1)} %get-tuple-element.54), channel_id=1, source_target_pairs={{0,12},{4,0},{8,4},{12,8},{1,13},{5,1},{9,5},{13,9},{2,14},{6,2},{... | collective-permute-start | bytes 1179656 | tf_op jit(solution)/shard_map/ppermute | solution.py:279
  11.4 3.2 collective-permute-start.1
  14.6 2.4 collective-permute-start
  17.1 3.8 collective-permute-done.2
  20.9 45.0 %collective-permute-done.1 = bf16[2,128,768]{2,1,0:T(8,128)(2,1)S(1)} collective-permute-done((bf16[2,128,768]{2,1,0:T(8,128)(2,1)S(1)}, bf16[2,128,768]{2,1,0:T(8,128)(2,1)S(1)}, u32[]{:S(2)}, u32[]{:S(2)}) %collective-permute-start.1) | collective-permute-done | bytes 393248 | tf_op jit(solution)/shard_map/ppermute | solution.py:279
  72.5 4.5 collective-permute-start.10
  77.0 20.9 %collective-permute-done.5.refs_1_.refs_14_ = bf16[768,768]{1,0:T(8,128)(2,1)} collective-permute-done((bf16[768,768]{1,0:T(8,128)(2,1)S(1)}, bf16[768,768]{1,0:T(8,128)(2,1)}, u32[]{:S(2)}, u32[]{:S(2)}) %collective-permute-start.5) | collective-permute-done | bytes 1179680 | tf_op jit(solution)/shard_map/ppermute | solution.py:322
  97.9 4.5 collective-permute-done.3
  103.5 1.7 collective-permute-start.8
  105.2 2.1 select_bitcast_fusion.1
  107.3 2.1 pad_maximum_fusion
  110.0 17.1 %collective-permute-start.7 = (bf16[768,768]{1,0:T(8,128)(2,1)}, bf16[768,768]{1,0:T(8,128)(2,1)}, u32[]{:S(2)}, u32[]{:S(2)}) collective-permute-start(bf16[768,768]{1,0:T(8,128)(2,1)} %collective-permute-done.6), channel_id=1, source_target_pairs={{0,4},{4,0},{8,12},{12,8},{1,5},{5,1},{9,13},{13,9},{2,6},{6,2},{1... | collective-permute-start | bytes 3538952 | tf_op jit(solution)/shard_map/ppermute | solution.py:322
  127.1 21.3 %collective-permute-done.15.refs_1_.refs_22_ = bf16[768,768]{1,0:T(8,128)(2,1)} collective-permute-done((bf16[768,768]{1,0:T(8,128)(2,1)S(1)}, bf16[768,768]{1,0:T(8,128)(2,1)}, u32[]{:S(2)}, u32[]{:S(2)}) %collective-permute-start.15) | collective-permute-done | bytes 1179680 | tf_op jit(solution)/shard_map/ppermute | solution.py:322
  150.1 2.4 collective-permute-start.9
  153.1 20.6 %collective-permute-done.7 = bf16[768,768]{1,0:T(8,128)(2,1)} collective-permute-done((bf16[768,768]{1,0:T(8,128)(2,1)}, bf16[768,768]{1,0:T(8,128)(2,1)}, u32[]{:S(2)}, u32[]{:S(2)}) %collective-permute-start.7) | collective-permute-done | bytes 1179680 | tf_op jit(solution)/shard_map/ppermute | solution.py:322
  173.7 25.3 %collective-permute-done.12 = bf16[768,768]{1,0:T(8,128)(2,1)} collective-permute-done((bf16[768,768]{1,0:T(8,128)(2,1)}, bf16[768,768]{1,0:T(8,128)(2,1)}, u32[]{:S(2)}, u32[]{:S(2)}) %collective-permute-start.12) | collective-permute-done | bytes 1179680 | tf_op jit(solution)/shard_map/ppermute | solution.py:322
  202.4 21.9 %collective-permute-done.9 = bf16[768,768]{1,0:T(8,128)(2,1)} collective-permute-done((bf16[768,768]{1,0:T(8,128)(2,1)}, bf16[768,768]{1,0:T(8,128)(2,1)}, u32[]{:S(2)}, u32[]{:S(2)}) %collective-permute-start.9) | collective-permute-done | bytes 1179680 | tf_op jit(solution)/shard_map/ppermute | solution.py:322
  226.5 1.8 broadcast_select_fusion.11.refs_2_.refs_19_
  228.3 1.8 broadcast_select_fusion.12.refs_3_.refs_16_
  230.2 19.4 %collective-permute-done.20.refs_10_ = bf16[768,768]{1,0:T(8,128)(2,1)} collective-permute-done((bf16[768,768]{1,0:T(8,128)(2,1)}, bf16[768,768]{1,0:T(8,128)(2,1)}, u32[]{:S(2)}, u32[]{:S(2)}) %collective-permute-start.20) | collective-permute-done | bytes 1179680 | tf_op jit(solution)/shard_map/ppermute | solution.py:322
  249.6 15.9 %collective-permute-start.23 = (bf16[768,768]{1,0:T(8,128)(2,1)}, bf16[768,768]{1,0:T(8,128)(2,1)}, u32[]{:S(2)}, u32[]{:S(2)}) collective-permute-start(bf16[768,768]{1,0:T(8,128)(2,1)} %collective-permute-done.20.refs_10_), channel_id=1, source_target_pairs={{4,8},{8,4},{5,9},{9,5},{6,10},{10,6},{7,11},{11,7},{20,24},{24,20... | collective-permute-start | bytes 3538952 | tf_op jit(solution)/shard_map/ppermute | solution.py:322
  265.5 2.7 collective-permute-start.17
  268.2 6.6 %collective-permute-done.14 = bf16[768,768]{1,0:T(8,128)(2,1)} collective-permute-done((bf16[768,768]{1,0:T(8,128)(2,1)}, bf16[768,768]{1,0:T(8,128)(2,1)}, u32[]{:S(2)}, u32[]{:S(2)}) %collective-permute-start.14) | collective-permute-done | bytes 1179680 | tf_op jit(solution)/shard_map/ppermute | solution.py:322
  276.3 2.5 broadcast_select_fusion.1
  279.2 1.8 slice-done
  281.7 7.3 %multiply_reduce_fusion = f32[2,4,128]{2,1,0:T(4,128)S(1)} fusion(bf16[1,2,4,128,3072]{4,3,2,1,0:T(8,128)(2,1)S(1)} %bitcast.250, bf16[1,2,4,128,768]{4,3,2,1,0:T(8,128)(2,1)S(1)} %bitcast.255, bf16[1,2,4,128,768]{4,3,2,1,0:T(8,128)(2,1)S(1)} %bitcast.253, bf16[1,2,4,128,768]{4,3,2,1,0:T(8,128)(2,1)S(1)} %bitcast.257, ...), kind=kLoop, calls=%fused_computation.1 | loop fusion | flops 37747712 | bytes 12587009 | tf_op jit(solution)/shard_map/reduce_sum | solution.py:358
  289.0 5.6 multiply_convert_fusion
  294.7 8.4 %raw_products.4.refs_7_ = f32[1024,768]{1,0:T(8,128)S(1)} custom-call(s32[4]{0:T(128)S(1)} %pad_add_fusion.source_ref, bf16[1024,3072]{1,0:T(8,128)(2,1)S(1)} %get-tuple-element.27.low_ref, bf16[768,768]{1,0:T(8,128)(2,1)S(1)} %pad_maximum_fusion.7.refs_0_.refs_17_, bf16[768,768]{1,0:T(8,128)(2,1)} %collective-permute-done.10.refs_1_.refs_18_, ...), custom_call_target="tpu_custom_call" | custom-call | flops 4831838208 | bytes 14155776 | tf_op jit(solution)/shard_map/raw_products/pallas_call | solution.py:68
  304.8 7.5 %raw_products.3.refs_6_ = f32[1024,768]{1,0:T(8,128)S(1)} custom-call(s32[4]{0:T(128)S(1)} %pad_add_fusion.source_ref, bf16[1024,3072]{1,0:T(8,128)(2,1)S(1)} %get-tuple-element.27.low_ref, bf16[768,768]{1,0:T(8,128)(2,1)S(1)} %pad_maximum_fusion.6.refs_0_.refs_13_, bf16[768,768]{1,0:T(8,128)(2,1)} %collective-permute-done.5.refs_1_.refs_14_, ...), custom_call_target="tpu_custom_call" | custom-call | flops 4831838208 | bytes 14155776 | tf_op jit(solution)/shard_map/raw_products/pallas_call | solution.py:68
  312.3 2.1 collective-permute-start.24
  314.4 2.4 broadcast_select_fusion.7.refs_11_
  316.8 8.6 %collective-permute-done.17 = bf16[768,768]{1,0:T(8,128)(2,1)} collective-permute-done((bf16[768,768]{1,0:T(8,128)(2,1)}, bf16[768,768]{1,0:T(8,128)(2,1)}, u32[]{:S(2)}, u32[]{:S(2)}) %collective-permute-start.17) | collective-permute-done | bytes 1179680 | tf_op jit(solution)/shard_map/ppermute | solution.py:322
  326.8 23.9 %collective-permute-done.19 = bf16[768,768]{1,0:T(8,128)(2,1)} collective-permute-done((bf16[768,768]{1,0:T(8,128)(2,1)}, bf16[768,768]{1,0:T(8,128)(2,1)}, u32[]{:S(2)}, u32[]{:S(2)}) %collective-permute-start.19) | collective-permute-done | bytes 1179680 | tf_op jit(solution)/shard_map/ppermute | solution.py:322
  353.3 2.8 copy-done.13
  356.1 7.5 %raw_products.5.refs_8_ = f32[1024,768]{1,0:T(8,128)S(1)} custom-call(s32[4]{0:T(128)S(1)} %pad_add_fusion.source_ref, bf16[1024,3072]{1,0:T(8,128)(2,1)S(1)} %copy-done.13, bf16[768,768]{1,0:T(8,128)(2,1)S(1)} %pad_maximum_fusion.8.refs_0_.refs_21_, bf16[768,768]{1,0:T(8,128)(2,1)} %collective-permute-done.15.refs_1_.refs_22_, ...), custom_call_target="tpu_custom_call" | custom-call | flops 4831838208 | bytes 14155776 | tf_op jit(solution)/shard_map/raw_products/pallas_call | solution.py:68
  363.6 10.0 %collective-permute-done.24 = bf16[768,768]{1,0:T(8,128)(2,1)} collective-permute-done((bf16[768,768]{1,0:T(8,128)(2,1)}, bf16[768,768]{1,0:T(8,128)(2,1)}, u32[]{:S(2)}, u32[]{:S(2)}) %collective-permute-start.24) | collective-permute-done | bytes 1179680 | tf_op jit(solution)/shard_map/ppermute | solution.py:322
  373.6 2.4 broadcast_select_fusion.6.refs_12_
  376.0 1.7 sublayer_back.7
  379.4 3.5 collective-permute-done.25
  382.9 2.2 convert_add_fusion
  387.2 18.8 %collective-permute-done.26 = bf16[512,768]{1,0:T(8,128)(2,1)} collective-permute-done((bf16[512,768]{1,0:T(8,128)(2,1)}, bf16[512,768]{1,0:T(8,128)(2,1)}, u32[]{:S(2)}, u32[]{:S(2)}) %collective-permute-start.26) | collective-permute-done | bytes 786464 | tf_op jit(solution)/shard_map/ppermute | solution.py:294
  416.3 5.7 collective-permute-done.31
  422.1 9.4 %collective-permute-done.33 = bf16[1,128,768]{1,2,0:T(8,128)(2,1)S(1)} collective-permute-done((bf16[1,128,768]{1,2,0:T(8,128)(2,1)S(1)}, bf16[1,128,768]{1,2,0:T(8,128)(2,1)S(1)}, u32[]{:S(2)}, u32[]{:S(2)}) %collective-permute-start.33) | collective-permute-done | bytes 196640 | tf_op jit(solution)/shard_map/ppermute | solution.py:279
  436.1 14.0 %collective-permute-done.35 = bf16[512,768]{1,0:T(8,128)(2,1)S(1)} collective-permute-done((bf16[512,768]{1,0:T(8,128)(2,1)S(1)}, bf16[512,768]{1,0:T(8,128)(2,1)S(1)}, u32[]{:S(2)}, u32[]{:S(2)}) %collective-permute-start.35) | collective-permute-done | bytes 786464 | tf_op jit(solution)/shard_map/ppermute | solution.py:294
  457.4 8.1 %collective-permute-done.28 = bf16[256,768]{1,0:T(8,128)(2,1)S(1)} collective-permute-done((bf16[256,768]{1,0:T(8,128)(2,1)}, bf16[256,768]{1,0:T(8,128)(2,1)S(1)}, u32[]{:S(2)}, u32[]{:S(2)}) %collective-permute-start.28) | collective-permute-done | bytes 393248 | tf_op jit(solution)/shard_map/ppermute | solution.py:294
  465.5 7.3 %collective-permute-done.30 = bf16[256,768]{1,0:T(8,128)(2,1)} collective-permute-done((bf16[256,768]{1,0:T(8,128)(2,1)}, bf16[256,768]{1,0:T(8,128)(2,1)}, u32[]{:S(2)}, u32[]{:S(2)}) %collective-permute-start.30) | collective-permute-done | bytes 393248 | tf_op jit(solution)/shard_map/ppermute | solution.py:294
  475.9 1.9 pad_maximum_fusion.1.refs_4_
  485.2 15.4 %sublayer_back.10 = bf16[4,256,768]{2,1,0:T(8,128)(2,1)} custom-call(s32[1]{0:T(128)} %bitcast.66.flag_ref, s32[4]{0:T(128)} %copy-done.14, f32[128,128]{1,0:T(8,128)} %convert_select_fusion.refs_0_, f32[2,128]{1,0:T(2,128)} %pad_maximum_fusion.9.refs_1_, f32[1024,1]{1,0:T(8,128)} %copy.13.refs_2_, f32[1,3072]{1,0:T(1,128)} %refs_3_.13, ...), custom_call_target="tpu_custom_call" | custom-call | flops 9663676416 | bytes 23592960 | tf_op jit(solution)/shard_map/sublayer_back/pallas_call | solution.py:206
  500.6 2.6 collective-permute-done.46
  505.0 15.3 %sublayer_back.11 = bf16[4,256,768]{2,1,0:T(8,128)(2,1)} custom-call(s32[1]{0:T(128)} %bitcast.66.flag_ref, s32[4]{0:T(128)} %copy-done.14, f32[128,128]{1,0:T(8,128)} %convert_select_fusion.refs_0_, f32[2,128]{1,0:T(2,128)} %pad_maximum_fusion.9.refs_1_, f32[1024,1]{1,0:T(8,128)} %copy.13.refs_2_, f32[1,3072]{1,0:T(1,128)} %refs_3_.13, ...), custom_call_target="tpu_custom_call" | custom-call | flops 9663676416 | bytes 23592960 | tf_op jit(solution)/shard_map/sublayer_back/pallas_call | solution.py:206
  526.7 9.6 %collective-permute-done.40 = bf16[256,768]{1,0:T(8,128)(2,1)S(1)} collective-permute-done((bf16[256,768]{1,0:T(8,128)(2,1)S(1)}, bf16[256,768]{1,0:T(8,128)(2,1)S(1)}, u32[]{:S(2)}, u32[]{:S(2)}) %collective-permute-start.40) | collective-permute-done | bytes 393248 | tf_op jit(solution)/shard_map/ppermute | solution.py:294
  536.4 7.5 %collective-permute-done.38 = bf16[256,768]{1,0:T(8,128)(2,1)S(1)} collective-permute-done((bf16[256,768]{1,0:T(8,128)(2,1)S(1)}, bf16[256,768]{1,0:T(8,128)(2,1)S(1)}, u32[]{:S(2)}, u32[]{:S(2)}) %collective-permute-start.38) | collective-permute-done | bytes 393248 | tf_op jit(solution)/shard_map/ppermute | solution.py:294
  544.6 1.9 pad_maximum_fusion.2.refs_4_
  546.6 15.6 %sublayer_back.12 = bf16[4,256,768]{2,1,0:T(8,128)(2,1)} custom-call(s32[1]{0:T(128)} %bitcast.66.flag_ref, s32[4]{0:T(128)} %copy-done.14, f32[128,128]{1,0:T(8,128)} %convert_select_fusion.refs_0_, f32[2,128]{1,0:T(2,128)} %pad_maximum_fusion.9.refs_1_, f32[1024,1]{1,0:T(8,128)} %copy.13.refs_2_, f32[1,3072]{1,0:T(1,128)} %refs_3_.13, ...), custom_call_target="tpu_custom_call" | custom-call | flops 9663676416 | bytes 23592960 | tf_op jit(solution)/shard_map/sublayer_back/pallas_call | solution.py:206
  563.4 15.3 %sublayer_back.13 = bf16[4,256,768]{2,1,0:T(8,128)(2,1)} custom-call(s32[1]{0:T(128)} %bitcast.66.flag_ref, s32[4]{0:T(128)} %copy-done.14, f32[128,128]{1,0:T(8,128)} %convert_select_fusion.refs_0_, f32[2,128]{1,0:T(2,128)} %pad_maximum_fusion.9.refs_1_, f32[1024,1]{1,0:T(8,128)} %copy.13.refs_2_, f32[1,3072]{1,0:T(1,128)} %refs_3_.13, ...), custom_call_target="tpu_custom_call" | custom-call | flops 9663676416 | bytes 23592960 | tf_op jit(solution)/shard_map/sublayer_back/pallas_call | solution.py:206
  583.9 4.6 collective-permute-start.43
  588.5 1.9 collective-permute-start.42
  590.5 3.3 collective-permute-start.41
  593.8 7.2 %collective-permute-done.53 = bf16[256,768]{1,0:T(8,128)(2,1)S(1)} collective-permute-done((bf16[256,768]{1,0:T(8,128)(2,1)S(1)}, bf16[256,768]{1,0:T(8,128)(2,1)S(1)}, u32[]{:S(2)}, u32[]{:S(2)}) %collective-permute-start.53) | collective-permute-done | bytes 393248 | tf_op jit(solution)/shard_map/ppermute | solution.py:294
  601.8 4.5 collective-permute-start.56
  606.3 2.0 collective-permute-start.55
  608.3 3.2 collective-permute-start.54
  612.1 10.8 %collective-permute-done.55 = bf16[1,128,768]{2,1,0:T(8,128)(2,1)S(1)} collective-permute-done((bf16[1,128,768]{2,1,0:T(8,128)(2,1)S(1)}, bf16[1,128,768]{2,1,0:T(8,128)(2,1)S(1)}, u32[]{:S(2)}, u32[]{:S(2)}) %collective-permute-start.55) | collective-permute-done | bytes 196640 | tf_op jit(solution)/shard_map/ppermute | solution.py:279
  (242 shorter events, 81.5 us)
Async XLA Ops:
  0.0 72.5 %collective-permute-start.21 = (bf16[768,768]{1,0:T(8,128)(2,1)}, bf16[768,768]{1,0:T(8,128)(2,1)}, u32[]{:S(2)}, u32[]{:S(2)}) collective-permute-start(bf16[768,768]{1,0:T(8,128)(2,1)} %bitcast.234), channel_id=1, source_target_pairs={{4,8},{8,4},{5,9},{9,5},{6,10},{10,6},{7,11},{11,7},{20,24},{24,20... | collective-permute-start | bytes 3538952 | tf_op jit(solution)/shard_map/ppermute | solution.py:322
  4.3 16.6 %collective-permute-start.2 = (bf16[2,128,768]{2,1,0:T(8,128)(2,1)S(1)}, bf16[2,128,768]{2,1,0:T(8,128)(2,1)S(1)}, u32[]{:S(2)}, u32[]{:S(2)}) collective-permute-start(bf16[2,128,768]{2,1,0:T(8,128)(2,1)S(1)} %get-tuple-element.54), channel_id=1, source_target_pairs={{0,12},{4,0},{8,4},{12,8},{1,13},{5,1},{9,5},{13,9},{2,14},{6,2},{... | collective-permute-start | bytes 1179656 | tf_op jit(solution)/shard_map/ppermute | solution.py:279
  11.4 54.6 %collective-permute-start.1 = (bf16[2,128,768]{2,1,0:T(8,128)(2,1)S(1)}, bf16[2,128,768]{2,1,0:T(8,128)(2,1)S(1)}, u32[]{:S(2)}, u32[]{:S(2)}) collective-permute-start(bf16[2,128,768]{2,1,0:T(8,128)(2,1)S(1)} %get-tuple-element.55), channel_id=1, source_target_pairs={{0,8},{4,12},{8,0},{12,4},{1,9},{5,13},{9,1},{13,5},{2,10},{6,14},... | collective-permute-start | bytes 1179656 | tf_op jit(solution)/shard_map/ppermute | solution.py:279
  14.6 51.4 %collective-permute-start = (bf16[2,128,768]{2,1,0:T(8,128)(2,1)S(1)}, bf16[2,128,768]{2,1,0:T(8,128)(2,1)S(1)}, u32[]{:S(2)}, u32[]{:S(2)}) collective-permute-start(bf16[2,128,768]{2,1,0:T(8,128)(2,1)S(1)} %get-tuple-element.56), channel_id=1, source_target_pairs={{0,4},{4,8},{8,12},{12,0},{1,5},{5,9},{9,13},{13,1},{2,6},{6,10},{... | collective-permute-start | bytes 1179656 | tf_op jit(solution)/shard_map/ppermute | solution.py:279
  67.0 35.3 %collective-permute-start.3 = (bf16[2,512,768]{2,1,0:T(8,128)(2,1)S(1)}, bf16[2,512,768]{2,1,0:T(8,128)(2,1)S(1)}, u32[]{:S(2)}, u32[]{:S(2)}) collective-permute-start(bf16[2,512,768]{2,1,0:T(8,128)(2,1)S(1)} %fusion.15), channel_id=1, source_target_pairs={{0,2},{1,3},{2,0},{3,1},{4,6},{5,7},{6,4},{7,5},{8,10},{9,11},{10,... | collective-permute-start | bytes 4718600 | tf_op jit(solution)/shard_map/ppermute | solution.py:294
  68.8 234.3 %copy-start.3 = (bf16[768,768]{1,0:T(8,128)(2,1)}, bf16[768,768]{1,0:T(8,128)(2,1)S(1)}, u32[]{:S(2)}) copy-start(bf16[768,768]{1,0:T(8,128)(2,1)S(1)} %pad_maximum_fusion.6.refs_0_.refs_13_) | copy-start | bytes 3538948
  68.8 29.1 %collective-permute-start.5 = (bf16[768,768]{1,0:T(8,128)(2,1)S(1)}, bf16[768,768]{1,0:T(8,128)(2,1)}, u32[]{:S(2)}, u32[]{:S(2)}) collective-permute-start(bf16[768,768]{1,0:T(8,128)(2,1)S(1)} %pad_maximum_fusion.6.refs_0_.refs_13_), channel_id=1, source_target_pairs={{0,4},{4,0},{8,12},{12,8},{1,5},{5,1},{9,13},{13,9},{2,6},{6,2},{1... | collective-permute-start | bytes 3538952 | tf_op jit(solution)/shard_map/ppermute | solution.py:322
  68.9 41.1 %collective-permute-start.6 = (bf16[768,768]{1,0:T(8,128)(2,1)S(1)}, bf16[768,768]{1,0:T(8,128)(2,1)}, u32[]{:S(2)}, u32[]{:S(2)}) collective-permute-start(bf16[768,768]{1,0:T(8,128)(2,1)S(1)} %pad_maximum_fusion.6.refs_0_.refs_13_), channel_id=1, source_target_pairs={{4,8},{8,4},{5,9},{9,5},{6,10},{10,6},{7,11},{11,7},{20,24},{24,20... | collective-permute-start | bytes 3538952 | tf_op jit(solution)/shard_map/ppermute | solution.py:322
  70.7 224.0 %copy-start.4 = (bf16[768,768]{1,0:T(8,128)(2,1)}, bf16[768,768]{1,0:T(8,128)(2,1)S(1)}, u32[]{:S(2)}) copy-start(bf16[768,768]{1,0:T(8,128)(2,1)S(1)} %pad_maximum_fusion.7.refs_0_.refs_17_) | copy-start | bytes 3538948
  70.7 39.3 %collective-permute-start.11 = (bf16[768,768]{1,0:T(8,128)(2,1)S(1)}, bf16[768,768]{1,0:T(8,128)(2,1)}, u32[]{:S(2)}, u32[]{:S(2)}) collective-permute-start(bf16[768,768]{1,0:T(8,128)(2,1)S(1)} %pad_maximum_fusion.7.refs_0_.refs_17_), channel_id=1, source_target_pairs={{4,8},{8,4},{5,9},{9,5},{6,10},{10,6},{7,11},{11,7},{20,24},{24,20... | collective-permute-start | bytes 3538952 | tf_op jit(solution)/shard_map/ppermute | solution.py:322
  72.5 280.8 %copy-start.5 = (bf16[768,768]{1,0:T(8,128)(2,1)}, bf16[768,768]{1,0:T(8,128)(2,1)S(1)}, u32[]{:S(2)}) copy-start(bf16[768,768]{1,0:T(8,128)(2,1)S(1)} %pad_maximum_fusion.8.refs_0_.refs_21_) | copy-start | bytes 3538948
  72.5 54.6 %collective-permute-start.10 = (bf16[768,768]{1,0:T(8,128)(2,1)S(1)}, bf16[768,768]{1,0:T(8,128)(2,1)}, u32[]{:S(2)}, u32[]{:S(2)}) collective-permute-start(bf16[768,768]{1,0:T(8,128)(2,1)S(1)} %pad_maximum_fusion.7.refs_0_.refs_17_), channel_id=1, source_target_pairs={{0,4},{4,0},{8,12},{12,8},{1,5},{5,1},{9,13},{13,9},{2,6},{6,2},{1... | collective-permute-start | bytes 3538952 | tf_op jit(solution)/shard_map/ppermute | solution.py:322
  97.9 50.6 %collective-permute-start.15 = (bf16[768,768]{1,0:T(8,128)(2,1)S(1)}, bf16[768,768]{1,0:T(8,128)(2,1)}, u32[]{:S(2)}, u32[]{:S(2)}) collective-permute-start(bf16[768,768]{1,0:T(8,128)(2,1)S(1)} %pad_maximum_fusion.8.refs_0_.refs_21_), channel_id=1, source_target_pairs={{0,4},{4,0},{8,12},{12,8},{1,5},{5,1},{9,13},{13,9},{2,6},{6,2},{1... | collective-permute-start | bytes 3538952 | tf_op jit(solution)/shard_map/ppermute | solution.py:322
  103.5 46.6 %collective-permute-start.8 = (bf16[768,768]{1,0:T(8,128)(2,1)}, bf16[768,768]{1,0:T(8,128)(2,1)}, u32[]{:S(2)}, u32[]{:S(2)}) collective-permute-start(bf16[768,768]{1,0:T(8,128)(2,1)} %collective-permute-done.5.refs_1_.refs_14_), channel_id=1, source_target_pairs={{4,8},{8,4},{5,9},{9,5},{6,10},{10,6},{7,11},{11,7},{20,24},{24,20... | collective-permute-start | bytes 3538952 | tf_op jit(solution)/shard_map/ppermute | solution.py:322
  110.0 166.3 %collective-permute-start.4 = (bf16[2,2,512,768]{3,2,1,0:T(8,128)(2,1)}, bf16[2,2,512,768]{3,2,1,0:T(8,128)(2,1)}, u32[]{:S(2)}, u32[]{:S(2)}) collective-permute-start(bf16[2,2,512,768]{3,2,1,0:T(8,128)(2,1)} %pad_maximum_fusion), channel_id=1, source_target_pairs={{0,1},{1,0},{2,3},{3,2},{4,5},{5,4},{6,7},{7,6},{8,9},{9,8},{10,11... | collective-permute-start | bytes 9437192 | tf_op jit(solution)/shard_map/ppermute | solution.py:294
  110.0 63.7 %collective-permute-start.7 = (bf16[768,768]{1,0:T(8,128)(2,1)}, bf16[768,768]{1,0:T(8,128)(2,1)}, u32[]{:S(2)}, u32[]{:S(2)}) collective-permute-start(bf16[768,768]{1,0:T(8,128)(2,1)} %collective-permute-done.6), channel_id=1, source_target_pairs={{0,4},{4,0},{8,12},{12,8},{1,5},{5,1},{9,13},{13,9},{2,6},{6,2},{1... | collective-permute-start | bytes 3538952 | tf_op jit(solution)/shard_map/ppermute | solution.py:322
  127.1 71.9 %collective-permute-start.12 = (bf16[768,768]{1,0:T(8,128)(2,1)}, bf16[768,768]{1,0:T(8,128)(2,1)}, u32[]{:S(2)}, u32[]{:S(2)}) collective-permute-start(bf16[768,768]{1,0:T(8,128)(2,1)} %collective-permute-done.11), channel_id=1, source_target_pairs={{0,4},{4,0},{8,12},{12,8},{1,5},{5,1},{9,13},{13,9},{2,6},{6,2},{1... | collective-permute-start | bytes 3538952 | tf_op jit(solution)/shard_map/ppermute | solution.py:322
  148.4 52.3 %collective-permute-start.13 = (bf16[768,768]{1,0:T(8,128)(2,1)}, bf16[768,768]{1,0:T(8,128)(2,1)}, u32[]{:S(2)}, u32[]{:S(2)}) collective-permute-start(bf16[768,768]{1,0:T(8,128)(2,1)} %collective-permute-done.10.refs_1_.refs_18_), channel_id=1, source_target_pairs={{4,8},{8,4},{5,9},{9,5},{6,10},{10,6},{7,11},{11,7},{20,24},{24,20... | collective-permute-start | bytes 3538952 | tf_op jit(solution)/shard_map/ppermute | solution.py:322
  150.1 74.2 %collective-permute-start.9 = (bf16[768,768]{1,0:T(8,128)(2,1)}, bf16[768,768]{1,0:T(8,128)(2,1)}, u32[]{:S(2)}, u32[]{:S(2)}) collective-permute-start(bf16[768,768]{1,0:T(8,128)(2,1)} %collective-permute-done.8), channel_id=1, source_target_pairs={{0,4},{4,0},{8,12},{12,8},{1,5},{5,1},{9,13},{13,9},{2,6},{6,2},{1... | collective-permute-start | bytes 3538952 | tf_op jit(solution)/shard_map/ppermute | solution.py:322
  173.7 75.8 %collective-permute-start.20 = (bf16[768,768]{1,0:T(8,128)(2,1)}, bf16[768,768]{1,0:T(8,128)(2,1)}, u32[]{:S(2)}, u32[]{:S(2)}) collective-permute-start(bf16[768,768]{1,0:T(8,128)(2,1)} %bitcast.235), channel_id=1, source_target_pairs={{0,4},{4,0},{8,12},{12,8},{1,5},{5,1},{9,13},{13,9},{2,6},{6,2},{1... | collective-permute-start | bytes 3538952 | tf_op jit(solution)/shard_map/ppermute | solution.py:322
  199.0 50.6 %collective-permute-start.16 = (bf16[768,768]{1,0:T(8,128)(2,1)S(1)}, bf16[768,768]{1,0:T(8,128)(2,1)}, u32[]{:S(2)}, u32[]{:S(2)}) collective-permute-start(bf16[768,768]{1,0:T(8,128)(2,1)S(1)} %pad_maximum_fusion.8.refs_0_.refs_21_), channel_id=1, source_target_pairs={{4,8},{8,4},{5,9},{9,5},{6,10},{10,6},{7,11},{11,7},{20,24},{24,20... | collective-permute-start | bytes 3538952 | tf_op jit(solution)/shard_map/ppermute | solution.py:322
  200.7 64.8 %collective-permute-start.18 = (bf16[768,768]{1,0:T(8,128)(2,1)}, bf16[768,768]{1,0:T(8,128)(2,1)}, u32[]{:S(2)}, u32[]{:S(2)}) collective-permute-start(bf16[768,768]{1,0:T(8,128)(2,1)} %collective-permute-done.15.refs_1_.refs_22_), channel_id=1, source_target_pairs={{4,8},{8,4},{5,9},{9,5},{6,10},{10,6},{7,11},{11,7},{20,24},{24,20... | collective-permute-start | bytes 3538952 | tf_op jit(solution)/shard_map/ppermute | solution.py:322
  224.3 50.6 %collective-permute-start.14 = (bf16[768,768]{1,0:T(8,128)(2,1)}, bf16[768,768]{1,0:T(8,128)(2,1)}, u32[]{:S(2)}, u32[]{:S(2)}) collective-permute-start(bf16[768,768]{1,0:T(8,128)(2,1)} %collective-permute-done.13), channel_id=1, source_target_pairs={{0,4},{4,0},{8,12},{12,8},{1,5},{5,1},{9,13},{13,9},{2,6},{6,2},{1... | collective-permute-start | bytes 3538952 | tf_op jit(solution)/shard_map/ppermute | solution.py:322
  224.4 128.9 %copy-start.14 = (s32[4]{0:T(128)}, s32[4]{0:T(128)S(1)}, u32[]{:S(2)}) copy-start(s32[4]{0:T(128)S(1)} %pad_add_fusion.source_ref) | copy-start | bytes 52
  226.5 76.6 %copy-start.6 = (bf16[768,768]{1,0:T(8,128)(2,1)}, bf16[768,768]{1,0:T(8,128)(2,1)S(1)}, u32[]{:S(2)}) copy-start(bf16[768,768]{1,0:T(8,128)(2,1)S(1)} %broadcast_select_fusion.13.refs_2_.refs_15_) | copy-start | bytes 3538948
  228.3 66.4 %copy-start.7 = (bf16[768,768]{1,0:T(8,128)(2,1)}, bf16[768,768]{1,0:T(8,128)(2,1)S(1)}, u32[]{:S(2)}) copy-start(bf16[768,768]{1,0:T(8,128)(2,1)S(1)} %broadcast_select_fusion.11.refs_2_.refs_19_) | copy-start | bytes 3538948
  230.2 72.9 %copy-start.8 = (bf16[768,768]{1,0:T(8,128)(2,1)}, bf16[768,768]{1,0:T(8,128)(2,1)S(1)}, u32[]{:S(2)}) copy-start(bf16[768,768]{1,0:T(8,128)(2,1)S(1)} %broadcast_select_fusion.12.refs_3_.refs_16_) | copy-start | bytes 3538948
  249.6 64.8 %collective-permute-start.22 = (bf16[768,768]{1,0:T(8,128)(2,1)}, bf16[768,768]{1,0:T(8,128)(2,1)}, u32[]{:S(2)}, u32[]{:S(2)}) collective-permute-start(bf16[768,768]{1,0:T(8,128)(2,1)} %collective-permute-done.21), channel_id=1, source_target_pairs={{0,4},{4,0},{8,12},{12,8},{1,5},{5,1},{9,13},{13,9},{2,6},{6,2},{1... | collective-permute-start | bytes 3538952 | tf_op jit(solution)/shard_map/ppermute | solution.py:322
  249.6 62.7 %collective-permute-start.23 = (bf16[768,768]{1,0:T(8,128)(2,1)}, bf16[768,768]{1,0:T(8,128)(2,1)}, u32[]{:S(2)}, u32[]{:S(2)}) collective-permute-start(bf16[768,768]{1,0:T(8,128)(2,1)} %collective-permute-done.20.refs_10_), channel_id=1, source_target_pairs={{4,8},{8,4},{5,9},{9,5},{6,10},{10,6},{7,11},{11,7},{20,24},{24,20... | collective-permute-start | bytes 3538952 | tf_op jit(solution)/shard_map/ppermute | solution.py:322
  265.5 59.9 %collective-permute-start.17 = (bf16[768,768]{1,0:T(8,128)(2,1)}, bf16[768,768]{1,0:T(8,128)(2,1)}, u32[]{:S(2)}, u32[]{:S(2)}) collective-permute-start(bf16[768,768]{1,0:T(8,128)(2,1)} %collective-permute-done.16), channel_id=1, source_target_pairs={{0,4},{4,0},{8,12},{12,8},{1,5},{5,1},{9,13},{13,9},{2,6},{6,2},{1... | collective-permute-start | bytes 3538952 | tf_op jit(solution)/shard_map/ppermute | solution.py:322
  274.8 75.8 %collective-permute-start.19 = (bf16[768,768]{1,0:T(8,128)(2,1)}, bf16[768,768]{1,0:T(8,128)(2,1)}, u32[]{:S(2)}, u32[]{:S(2)}) collective-permute-start(bf16[768,768]{1,0:T(8,128)(2,1)} %collective-permute-done.18), channel_id=1, source_target_pairs={{0,4},{4,0},{8,12},{12,8},{1,5},{5,1},{9,13},{13,9},{2,6},{6,2},{1... | collective-permute-start | bytes 3538952 | tf_op jit(solution)/shard_map/ppermute | solution.py:322
  312.3 61.3 %collective-permute-start.24 = (bf16[768,768]{1,0:T(8,128)(2,1)}, bf16[768,768]{1,0:T(8,128)(2,1)}, u32[]{:S(2)}, u32[]{:S(2)}) collective-permute-start(bf16[768,768]{1,0:T(8,128)(2,1)} %collective-permute-done.23), channel_id=1, source_target_pairs={{0,4},{4,0},{8,12},{12,8},{1,5},{5,1},{9,13},{13,9},{2,6},{6,2},{1... | collective-permute-start | bytes 3538952 | tf_op jit(solution)/shard_map/ppermute | solution.py:322
  379.3 3.6 collective-permute-start.25
  386.1 19.9 %collective-permute-start.26 = (bf16[512,768]{1,0:T(8,128)(2,1)}, bf16[512,768]{1,0:T(8,128)(2,1)}, u32[]{:S(2)}, u32[]{:S(2)}) collective-permute-start(bf16[512,768]{1,0:T(8,128)(2,1)} %fusion.27), channel_id=1, source_target_pairs={{0,2},{1,3},{2,0},{3,1},{4,6},{5,7},{6,4},{7,5},{8,10},{9,11},{10,... | collective-permute-start | bytes 2359304 | tf_op jit(solution)/shard_map/ppermute | solution.py:294
  408.5 13.6 %collective-permute-start.31 = (bf16[1,128,768]{1,2,0:T(8,128)(2,1)S(1)}, bf16[1,128,768]{1,2,0:T(8,128)(2,1)S(1)}, u32[]{:S(2)}, u32[]{:S(2)}) collective-permute-start(bf16[1,128,768]{1,2,0:T(8,128)(2,1)S(1)} %get-tuple-element.78), channel_id=1, source_target_pairs={{16,0},{20,4},{24,8},{28,12},{17,1},{21,5},{25,9},{29,13},{18,2},{... | collective-permute-start | bytes 589832 | tf_op jit(solution)/shard_map/ppermute | solution.py:279
  409.8 12.3 %collective-permute-start.34 = (bf16[1,128,768]{1,2,0:T(8,128)(2,1)S(1)}, bf16[1,128,768]{1,2,0:T(8,128)(2,1)S(1)}, u32[]{:S(2)}, u32[]{:S(2)}) collective-permute-start(bf16[1,128,768]{1,2,0:T(8,128)(2,1)S(1)} %get-tuple-element.79), channel_id=1, source_target_pairs={{16,12},{20,0},{24,4},{28,8},{17,13},{21,1},{25,5},{29,9},{18,14},... | collective-permute-start | bytes 589832 | tf_op jit(solution)/shard_map/ppermute | solution.py:279
  411.1 20.4 %collective-permute-start.33 = (bf16[1,128,768]{1,2,0:T(8,128)(2,1)S(1)}, bf16[1,128,768]{1,2,0:T(8,128)(2,1)S(1)}, u32[]{:S(2)}, u32[]{:S(2)}) collective-permute-start(bf16[1,128,768]{1,2,0:T(8,128)(2,1)S(1)} %get-tuple-element.80), channel_id=1, source_target_pairs={{16,8},{20,12},{24,0},{28,4},{17,9},{21,13},{25,1},{29,5},{18,10},... | collective-permute-start | bytes 589832 | tf_op jit(solution)/shard_map/ppermute | solution.py:279
  412.4 19.1 %collective-permute-start.32 = (bf16[1,128,768]{1,2,0:T(8,128)(2,1)S(1)}, bf16[1,128,768]{1,2,0:T(8,128)(2,1)S(1)}, u32[]{:S(2)}, u32[]{:S(2)}) collective-permute-start(bf16[1,128,768]{1,2,0:T(8,128)(2,1)S(1)} %get-tuple-element.81), channel_id=1, source_target_pairs={{16,4},{20,8},{24,12},{28,0},{17,5},{21,9},{25,13},{29,1},{18,6},{... | collective-permute-start | bytes 589832 | tf_op jit(solution)/shard_map/ppermute | solution.py:279
  416.3 35.3 %collective-permute-start.27 = (bf16[2,256,768]{2,1,0:T(8,128)(2,1)S(1)}, bf16[2,256,768]{2,1,0:T(8,128)(2,1)S(1)}, u32[]{:S(2)}, u32[]{:S(2)}) collective-permute-start(bf16[2,256,768]{2,1,0:T(8,128)(2,1)S(1)} %dynamic-slice_bitcast_fusion.8), channel_id=1, source_target_pairs={{0,1},{1,0},{2,3},{3,2},{4,5},{5,4},{6,7},{7,6},{8,9},{9,8},{10,11... | collective-permute-start | bytes 2359304 | tf_op jit(solution)/shard_map/ppermute | solution.py:294
  432.2 17.9 %collective-permute-start.35 = (bf16[512,768]{1,0:T(8,128)(2,1)S(1)}, bf16[512,768]{1,0:T(8,128)(2,1)S(1)}, u32[]{:S(2)}, u32[]{:S(2)}) collective-permute-start(bf16[512,768]{1,0:T(8,128)(2,1)S(1)} %fusion.19), channel_id=1, source_target_pairs={{0,2},{1,3},{2,0},{3,1},{4,6},{5,7},{6,4},{7,5},{8,10},{9,11},{10,... | collective-permute-start | bytes 2359304 | tf_op jit(solution)/shard_map/ppermute | solution.py:294
  436.0 18.3 %collective-permute-start.29 = (bf16[2,256,768]{2,1,0:T(8,128)(2,1)S(1)}, bf16[2,256,768]{2,1,0:T(8,128)(2,1)S(1)}, u32[]{:S(2)}, u32[]{:S(2)}) collective-permute-start(bf16[2,256,768]{2,1,0:T(8,128)(2,1)S(1)} %dynamic-slice_bitcast_fusion.7), channel_id=1, source_target_pairs={{0,1},{1,0},{2,3},{3,2},{4,5},{5,4},{6,7},{7,6},{8,9},{9,8},{10,11... | collective-permute-start | bytes 2359304 | tf_op jit(solution)/shard_map/ppermute | solution.py:294
  451.5 22.5 %collective-permute-start.36 = (bf16[2,512,768]{2,1,0:T(8,128)(2,1)}, bf16[2,512,768]{2,1,0:T(8,128)(2,1)}, u32[]{:S(2)}, u32[]{:S(2)}) collective-permute-start(bf16[2,512,768]{2,1,0:T(8,128)(2,1)} %pad_maximum_fusion.4), channel_id=1, source_target_pairs={{0,1},{1,0},{2,3},{3,2},{4,5},{5,4},{6,7},{7,6},{8,9},{9,8},{10,11... | collective-permute-start | bytes 4718600 | tf_op jit(solution)/shard_map/ppermute | solution.py:294
  453.2 12.2 %collective-permute-start.28 = (bf16[256,768]{1,0:T(8,128)(2,1)}, bf16[256,768]{1,0:T(8,128)(2,1)S(1)}, u32[]{:S(2)}, u32[]{:S(2)}) collective-permute-start(bf16[256,768]{1,0:T(8,128)(2,1)} %fusion.67), channel_id=1, source_target_pairs={{0,2},{1,3},{2,0},{3,1},{4,6},{5,7},{6,4},{7,5},{8,10},{9,11},{10,... | collective-permute-start | bytes 1179656 | tf_op jit(solution)/shard_map/ppermute | solution.py:294
  456.4 16.4 %collective-permute-start.30 = (bf16[256,768]{1,0:T(8,128)(2,1)}, bf16[256,768]{1,0:T(8,128)(2,1)}, u32[]{:S(2)}, u32[]{:S(2)}) collective-permute-start(bf16[256,768]{1,0:T(8,128)(2,1)} %fusion.68), channel_id=1, source_target_pairs={{0,2},{1,3},{2,0},{3,1},{4,6},{5,7},{6,4},{7,5},{8,10},{9,11},{10,... | collective-permute-start | bytes 1179656 | tf_op jit(solution)/shard_map/ppermute | solution.py:294
  480.0 20.6 %collective-permute-start.47 = (bf16[1,128,768]{1,2,0:T(8,128)(2,1)S(1)}, bf16[1,128,768]{1,2,0:T(8,128)(2,1)S(1)}, u32[]{:S(2)}, u32[]{:S(2)}) collective-permute-start(bf16[1,128,768]{1,2,0:T(8,128)(2,1)S(1)} %get-tuple-element.74), channel_id=1, source_target_pairs={{16,12},{20,0},{24,4},{28,8},{17,13},{21,1},{25,5},{29,9},{18,14},... | collective-permute-start | bytes 589832 | tf_op jit(solution)/shard_map/ppermute | solution.py:279
  481.3 21.9 %collective-permute-start.46 = (bf16[1,128,768]{1,2,0:T(8,128)(2,1)S(1)}, bf16[1,128,768]{1,2,0:T(8,128)(2,1)S(1)}, u32[]{:S(2)}, u32[]{:S(2)}) collective-permute-start(bf16[1,128,768]{1,2,0:T(8,128)(2,1)S(1)} %get-tuple-element.75), channel_id=1, source_target_pairs={{16,8},{20,12},{24,0},{28,4},{17,9},{21,13},{25,1},{29,5},{18,10},... | collective-permute-start | bytes 589832 | tf_op jit(solution)/shard_map/ppermute | solution.py:279
  482.6 20.6 %collective-permute-start.45 = (bf16[1,128,768]{1,2,0:T(8,128)(2,1)S(1)}, bf16[1,128,768]{1,2,0:T(8,128)(2,1)S(1)}, u32[]{:S(2)}, u32[]{:S(2)}) collective-permute-start(bf16[1,128,768]{1,2,0:T(8,128)(2,1)S(1)} %get-tuple-element.76), channel_id=1, source_target_pairs={{16,4},{20,8},{24,12},{28,0},{17,5},{21,9},{25,13},{29,1},{18,6},{... | collective-permute-start | bytes 589832 | tf_op jit(solution)/shard_map/ppermute | solution.py:279
  483.9 19.3 %collective-permute-start.44 = (bf16[1,128,768]{1,2,0:T(8,128)(2,1)S(1)}, bf16[1,128,768]{1,2,0:T(8,128)(2,1)S(1)}, u32[]{:S(2)}, u32[]{:S(2)}) collective-permute-start(bf16[1,128,768]{1,2,0:T(8,128)(2,1)S(1)} %get-tuple-element.77), channel_id=1, source_target_pairs={{16,0},{20,4},{24,8},{28,12},{17,1},{21,5},{25,9},{29,13},{18,2},{... | collective-permute-start | bytes 589832 | tf_op jit(solution)/shard_map/ppermute | solution.py:279
  503.8 18.5 %collective-permute-start.48 = (bf16[512,768]{1,0:T(8,128)(2,1)S(1)}, bf16[512,768]{1,0:T(8,128)(2,1)S(1)}, u32[]{:S(2)}, u32[]{:S(2)}) collective-permute-start(bf16[512,768]{1,0:T(8,128)(2,1)S(1)} %bitcast.280), channel_id=1, source_target_pairs={{0,2},{1,3},{2,0},{3,1},{4,6},{5,7},{6,4},{7,5},{8,10},{9,11},{10,... | collective-permute-start | bytes 2359304 | tf_op jit(solution)/shard_map/ppermute | solution.py:294
  521.6 2.4 collective-permute-start.39
  522.0 3.2 collective-permute-start.37
  522.6 21.5 %collective-permute-start.49 = (bf16[2,512,768]{2,1,0:T(8,128)(2,1)S(1)}, bf16[2,512,768]{2,1,0:T(8,128)(2,1)S(1)}, u32[]{:S(2)}, u32[]{:S(2)}) collective-permute-start(bf16[2,512,768]{2,1,0:T(8,128)(2,1)S(1)} %pad_maximum_fusion.5), channel_id=1, source_target_pairs={{0,1},{1,0},{2,3},{3,2},{4,5},{5,4},{6,7},{7,6},{8,9},{9,8},{10,11... | collective-permute-start | bytes 4718600 | tf_op jit(solution)/shard_map/ppermute | solution.py:294
  524.3 12.0 %collective-permute-start.40 = (bf16[256,768]{1,0:T(8,128)(2,1)S(1)}, bf16[256,768]{1,0:T(8,128)(2,1)S(1)}, u32[]{:S(2)}, u32[]{:S(2)}) collective-permute-start(bf16[256,768]{1,0:T(8,128)(2,1)S(1)} %fusion.70), channel_id=1, source_target_pairs={{0,2},{1,3},{2,0},{3,1},{4,6},{5,7},{6,4},{7,5},{8,10},{9,11},{10,... | collective-permute-start | bytes 1179656 | tf_op jit(solution)/shard_map/ppermute | solution.py:294
  525.5 18.4 %collective-permute-start.38 = (bf16[256,768]{1,0:T(8,128)(2,1)S(1)}, bf16[256,768]{1,0:T(8,128)(2,1)S(1)}, u32[]{:S(2)}, u32[]{:S(2)}) collective-permute-start(bf16[256,768]{1,0:T(8,128)(2,1)S(1)} %fusion.69), channel_id=1, source_target_pairs={{0,2},{1,3},{2,0},{3,1},{4,6},{5,7},{6,4},{7,5},{8,10},{9,11},{10,... | collective-permute-start | bytes 1179656 | tf_op jit(solution)/shard_map/ppermute | solution.py:294
  563.3 17.9 %collective-permute-start.50 = (bf16[2,256,768]{2,1,0:T(8,128)(2,1)S(1)}, bf16[2,256,768]{2,1,0:T(8,128)(2,1)S(1)}, u32[]{:S(2)}, u32[]{:S(2)}) collective-permute-start(bf16[2,256,768]{2,1,0:T(8,128)(2,1)S(1)} %dynamic-slice_bitcast_fusion.4), channel_id=1, source_target_pairs={{0,1},{1,0},{2,3},{3,2},{4,5},{5,4},{6,7},{7,6},{8,9},{9,8},{10,11... | collective-permute-start | bytes 2359304 | tf_op jit(solution)/shard_map/ppermute | solution.py:294
  580.0 2.5 collective-permute-start.52
  581.5 12.3 %collective-permute-start.51 = (bf16[256,768]{1,0:T(8,128)(2,1)S(1)}, bf16[256,768]{1,0:T(8,128)(2,1)S(1)}, u32[]{:S(2)}, u32[]{:S(2)}) collective-permute-start(bf16[256,768]{1,0:T(8,128)(2,1)S(1)} %fusion.71), channel_id=1, source_target_pairs={{0,2},{1,3},{2,0},{3,1},{4,6},{5,7},{6,4},{7,5},{8,10},{9,11},{10,... | collective-permute-start | bytes 1179656 | tf_op jit(solution)/shard_map/ppermute | solution.py:294
  582.9 18.2 %collective-permute-start.53 = (bf16[256,768]{1,0:T(8,128)(2,1)S(1)}, bf16[256,768]{1,0:T(8,128)(2,1)S(1)}, u32[]{:S(2)}, u32[]{:S(2)}) collective-permute-start(bf16[256,768]{1,0:T(8,128)(2,1)S(1)} %fusion.72), channel_id=1, source_target_pairs={{0,2},{1,3},{2,0},{3,1},{4,6},{5,7},{6,4},{7,5},{8,10},{9,11},{10,... | collective-permute-start | bytes 1179656 | tf_op jit(solution)/shard_map/ppermute | solution.py:294
  583.9 24.4 %collective-permute-start.43 = (bf16[1,128,768]{2,1,0:T(8,128)(2,1)S(1)}, bf16[1,128,768]{2,1,0:T(8,128)(2,1)S(1)}, u32[]{:S(2)}, u32[]{:S(2)}) collective-permute-start(bf16[1,128,768]{2,1,0:T(8,128)(2,1)S(1)} %get-tuple-element.67), channel_id=1, source_target_pairs={{0,12},{4,0},{8,4},{12,8},{1,13},{5,1},{9,5},{13,9},{2,14},{6,2},{... | collective-permute-start | bytes 589832 | tf_op jit(solution)/shard_map/ppermute | solution.py:279
  588.5 22.9 %collective-permute-start.42 = (bf16[1,128,768]{2,1,0:T(8,128)(2,1)S(1)}, bf16[1,128,768]{2,1,0:T(8,128)(2,1)S(1)}, u32[]{:S(2)}, u32[]{:S(2)}) collective-permute-start(bf16[1,128,768]{2,1,0:T(8,128)(2,1)S(1)} %get-tuple-element.68), channel_id=1, source_target_pairs={{0,8},{4,12},{8,0},{12,4},{1,9},{5,13},{9,1},{13,5},{2,10},{6,14},... | collective-permute-start | bytes 589832 | tf_op jit(solution)/shard_map/ppermute | solution.py:279
  590.5 21.0 %collective-permute-start.41 = (bf16[1,128,768]{2,1,0:T(8,128)(2,1)S(1)}, bf16[1,128,768]{2,1,0:T(8,128)(2,1)S(1)}, u32[]{:S(2)}, u32[]{:S(2)}) collective-permute-start(bf16[1,128,768]{2,1,0:T(8,128)(2,1)S(1)} %get-tuple-element.69), channel_id=1, source_target_pairs={{0,4},{4,8},{8,12},{12,0},{1,5},{5,9},{9,13},{13,1},{2,6},{6,10},{... | collective-permute-start | bytes 589832 | tf_op jit(solution)/shard_map/ppermute | solution.py:279
  601.8 10.3 %collective-permute-start.56 = (bf16[1,128,768]{2,1,0:T(8,128)(2,1)S(1)}, bf16[1,128,768]{2,1,0:T(8,128)(2,1)S(1)}, u32[]{:S(2)}, u32[]{:S(2)}) collective-permute-start(bf16[1,128,768]{2,1,0:T(8,128)(2,1)S(1)} %get-tuple-element.71), channel_id=1, source_target_pairs={{0,12},{4,0},{8,4},{12,8},{1,13},{5,1},{9,5},{13,9},{2,14},{6,2},{... | collective-permute-start | bytes 589832 | tf_op jit(solution)/shard_map/ppermute | solution.py:279
  606.3 16.7 %collective-permute-start.55 = (bf16[1,128,768]{2,1,0:T(8,128)(2,1)S(1)}, bf16[1,128,768]{2,1,0:T(8,128)(2,1)S(1)}, u32[]{:S(2)}, u32[]{:S(2)}) collective-permute-start(bf16[1,128,768]{2,1,0:T(8,128)(2,1)S(1)} %get-tuple-element.72), channel_id=1, source_target_pairs={{0,8},{4,12},{8,0},{12,4},{1,9},{5,13},{9,1},{13,5},{2,10},{6,14},... | collective-permute-start | bytes 589832 | tf_op jit(solution)/shard_map/ppermute | solution.py:279
  608.3 14.7 %collective-permute-start.54 = (bf16[1,128,768]{2,1,0:T(8,128)(2,1)S(1)}, bf16[1,128,768]{2,1,0:T(8,128)(2,1)S(1)}, u32[]{:S(2)}, u32[]{:S(2)}) collective-permute-start(bf16[1,128,768]{2,1,0:T(8,128)(2,1)S(1)} %get-tuple-element.73), channel_id=1, source_target_pairs={{0,4},{4,8},{8,12},{12,0},{1,5},{5,9},{9,13},{13,1},{2,6},{6,10},{... | collective-permute-start | bytes 589832 | tf_op jit(solution)/shard_map/ppermute | solution.py:279
  (39 other events, 439.5 us)

commit v3 on v2

--- a/solution.py
+++ b/solution.py
@@ -120,12 +120,12 @@
     for slot in range(slots):
         target = out_weight_ref.at[:, pl.ds(places[slot], depth)]
         get_first.append(start(out_weight_hbm[slot], target))
+    for copy in get_first:
+        copy.wait()
     get_raw = [
         start(raw_hbm[chunk].at[pl.ds(first_saved, rows)], raw_ref.at[chunk])
         for chunk in range(chunks)
     ]
-    for copy in get_first:
-        copy.wait()
     get_rest = []
     for slot in range(slots):
         for chunk in range(chunks):
@@ -290,30 +290,37 @@
     def place_rows(parts, enter):
         return reorder(jnp.concatenate(parts, axis=1), enter)
 
-    def swap(array_in, bit):
-        return lax.ppermute(array_in, "head", [(i, i ^ bit) for i in range(head_count)])
+    def swap(array_in, bit, section):
+        first = section * head_count
+        pairs = [(first + i, first + (i ^ bit)) for i in range(head_count)]
+        return lax.ppermute(array_in, ("section", "head"), pairs)
 
     my_core, my_side = my_head % 2, my_head // 2
 
-    def gather_share(own):
-        far = swap(own, 2)
+    def gather_share(own, tie=None):
+        far = swap(own, 2, 0)
+        if tie is not None:
+            far, _ = lax.optimization_barrier((far, tie))
         low_side = jnp.where(my_side == 0, own, far)
         high_side = jnp.where(my_side == 0, far, own)
         both = jnp.stack([low_side, high_side])
-        other = swap(both, 1)
+        other = swap(both, 1, 0)
         first, second = jnp.where(my_core == 0, both, other), jnp.where(my_core == 0, other, both)
         return jnp.concatenate([first[0], second[0], first[1], second[1]], axis=-1)
 
-    def core_sum(term):
+    def core_sum(term, section):
         shaped = term.reshape(2, 2, *term.shape[1:])
         keep = lax.dynamic_index_in_dim(shaped, my_core, 1, keepdims=False)
-        other = swap(lax.dynamic_index_in_dim(shaped, 1 - my_core, 1, keepdims=False), 1)
+        other = swap(lax.dynamic_index_in_dim(shaped, 1 - my_core, 1, keepdims=False), 1, section)
         pair = keep.astype(jnp.float32) + other.astype(jnp.float32)
         far = lax.dynamic_index_in_dim(pair, 1 - my_side, 0, keepdims=False).astype(jnp.bfloat16)
         return lax.dynamic_index_in_dim(pair, my_side, 0, keepdims=False), far
 
-    def side_sum(own, far):
-        return own + swap(far, 2).astype(jnp.float32)
+    def side_sum(own, far, section, tie):
+        arrived = swap(far, 2, section)
+        if tie is not None:
+            arrived, _ = lax.optimization_barrier((arrived, tie))
+        return own + arrived.astype(jnp.float32)
 
     def my_share(array_in):
         return lax.dynamic_slice_in_dim(array_in, my_head * share, share, array_in.ndim - 1)
@@ -373,7 +380,6 @@
             raws.append(run_raw(sources, low, pieces[-1]))
         out_pieces = [lax.all_gather(shards[-1], "frame", axis=1, tiled=True)]
     flags = [(lax.axis_index("section") == s).astype(jnp.int32).reshape(1) for s in range(2)]
-    halves = 2 if rows % (2 * patches) == 0 else 1
 
     def sublayer(flag, grad, first_grad, first, count):
         return run_back(
@@ -381,50 +387,42 @@
             raws, out_pieces, pieces, head_count, head_dim,
         )
 
-    def in_parts(flag, grad, first_grad, b, count, tie=None):
-        sums, first_term = [], None
-        for start in range(0, rows, count):
-            if tie is not None and start + count == rows:
-                flag, tie = lax.optimization_barrier((flag, tie))
-            term = sublayer(flag, grad, first_grad + start, b * rows + start, count)
-            first_term = term if first_term is None else first_term
-            sums.append(side_sum(*core_sum(term)))
-        return jnp.concatenate(sums, axis=0), first_term, tie
+    def term_of(section, grad, first_grad, b, tie):
+        flag = flags[section]
+        if tie is not None:
+            flag, _ = lax.optimization_barrier((flag, tie))
+        return sublayer(flag, grad, first_grad, b * rows, rows)
 
     def add(residual, summed):
         return (residual.astype(jnp.float32) + summed).astype(jnp.bfloat16)
 
     grad_space = upstream.reshape(batches * rows, feat)
     share_space = my_share(upstream.reshape(batches, rows, feat))
-    space_parts, sent, shares, fulls = [], [], [], []
-
-    def receive(arrived):
-        shares.append(place_rows(arrived, enter_time)[0])
-        fulls.append(gather_share(shares[-1]))
-
+    space_parts, sent = [], []
     for b in range(batches):
         tie = space_parts[-1] if b else None
-        count = rows // halves if b else rows
-        summed, _, tie = in_parts(flags[1], grad_space, b * rows, b, count, tie)
+        own, far = core_sum(term_of(1, grad_space, b * rows, b, tie), 1)
+        space_parts.append(add(share_space[b], side_sum(own, far, 1, None)))
+        sent.append(send_rows(space_parts[-1], leave_space, 1))
+    shares, fulls, terms, halves = [], [], [], []
+    for b in range(batches):
+        if b == 0:
+            shares.append(place_rows(sent[b], enter_time)[0])
+            fulls.append(gather_share(shares[-1]))
+        terms.append(term_of(0, fulls[b], 0, b, halves[-1][1] if b else None))
+        halves.append(core_sum(terms[-1], 0))
+        if b + 1 < batches:
+            arrived, _ = lax.optimization_barrier((sent[b + 1], fulls[b]))
+            shares.append(place_rows(arrived, enter_time)[0])
+            fulls.append(gather_share(shares[-1], terms[-1]))
+    time_parts, returned = [], []
+    for b in range(batches):
+        tie = terms[b + 1] if b + 1 < batches else None
+        part = add(shares[b], side_sum(*halves[b], 0, tie))
         if b:
-            space_parts[-1] = tie
-            receive(send_rows(tie, leave_space, 1))
-            summed, fulls[-1] = lax.optimization_barrier((summed, fulls[-1]))
-        space_parts.append(add(share_space[b], summed))
-    sent = send_rows(space_parts[-1], leave_space, 1)
-    time_parts, returned, first_term = [], [], None
-    for b in range(batches):
-        if b == batches - 1:
-            if b:
-                sent, first_term = lax.optimization_barrier((sent, first_term))
-            receive(sent)
-        tie = time_parts[-1] if b else None
-        summed, first_term, tie = in_parts(flags[0], fulls[b], 0, b, rows // halves, tie)
-        if b:
-            time_parts[-1] = tie
-            returned.append(send_rows(tie, leave_time, 0))
-        time_parts.append(add(shares[b], summed))
-    returned.append(send_rows(time_parts[-1], leave_time, 0))
+            part, _ = lax.optimization_barrier((part, returned[-1][0]))
+        time_parts.append(part)
+        returned.append(send_rows(time_parts[-1], leave_time, 0))
     time_parts = [place_rows(parts, enter_space)[0] for parts in returned]
     result = jnp.where(on_last, jnp.stack(space_parts), jnp.stack(time_parts))
     return result.reshape(1, batches, frames, patches, share)

time: 632 us -> 595 us (0.941)
  waiting for transfers between devices: 338 us -> 288 us
  starting transfers between devices: 112 us -> 143 us
  Pallas kernels: 89.5 us -> 80.1 us
    ppermute x20 -> x14, waiting for transfers between devices: 81.6 us -> 39.2 us  [swap(): return lax.ppermute(array_in, ('section', 'head'), pairs)]
    ppermute x20 -> x14, starting transfers between devices: 12.7 us -> 32.2 us  [swap(): return lax.ppermute(array_in, ('section', 'head'), pairs)]
    ppermute x17, waiting for transfers between devices: 77.4 us -> 64.6 us  [send_rows(): lax.ppermute(part, ('section', 'frame'), [(from_section * frame_count + s...]
    pallas_call x7 -> x4, Pallas kernels: 66.1 us -> 56.7 us  [run_back(): pl.pallas_call(functools.partial(back_kernel, chunks, slots, head_dim, fi...]
  transfers between devices with their start and end apart: 57 -> 51, of which waited for: 26 -> 26; matrix products, arithmetic and copies ran while one was open for 8% -> 9% of each run, Pallas kernels for 12% -> 8%
where the time goes in v3:
time: 595 us; the launch traced here: 593 us
  waiting for transfers between devices  288 us (48%)
  starting transfers between devices  143 us (24%)
  Pallas kernels  80.1 us (13%)
  other arithmetic  51.9 us (9%)
  local copies, waits for them, and re-layouts  20.7 us (3%)
  matrix products  8.81 us (1%)
    ppermute x20, waiting for transfers between devices, along(): return lax.ppermute(array_in, 'frame', pairs)  184 us
    ppermute x17, waiting for transfers between devices, send_rows(): lax.ppermute(part, ('section', 'frame'), [(from_section * frame_count + s...  64.6 us
    ppermute x20, starting transfers between devices, along(): return lax.ppermute(array_in, 'frame', pairs)  61.6 us
    pallas_call x4, Pallas kernels, run_back(): pl.pallas_call(functools.partial(back_kernel, chunks, slots, head_dim, fi...  56.7 us
    ppermute x17, starting transfers between devices, send_rows(): lax.ppermute(part, ('section', 'frame'), [(from_section * frame_count + s...  48.7 us
    ppermute x14, waiting for transfers between devices, swap(): return lax.ppermute(array_in, ('section', 'head'), pairs)  39.2 us
    ppermute x14, starting transfers between devices, swap(): return lax.ppermute(array_in, ('section', 'head'), pairs)  32.2 us
    pallas_call x3, Pallas kernels, run_raw(): pl.pallas_call(raw_kernel, grid_spec=pltpu.PrefetchScalarGridSpec(num_sca...  23.4 us
  transfers between devices with their start and end apart: 51, of which 26 were waited for; matrix products, arithmetic and copies ran while one was open for 9% of the time, Pallas kernels for 8%

profile of v3, /device:TPU:0, one launch (start us, length us, event | category | flops | bytes accessed | tf_op | source)
XLA Modules:
  0.0 593.0 jit_solution(1826476227582880104)
XLA Ops:
  0.0 2.4 fusion.14
  2.6 5.1 collective-permute-start
  7.7 4.5 collective-permute-start.1
  12.2 3.3 collective-permute-start.2
  15.6 4.1 collective-permute-done
  19.8 16.0 %collective-permute-done.1 = bf16[2,128,768]{2,1,0:T(8,128)(2,1)S(1)} collective-permute-done((bf16[2,128,768]{2,1,0:T(8,128)(2,1)S(1)}, bf16[2,128,768]{2,1,0:T(8,128)(2,1)S(1)}, u32[]{:S(2)}, u32[]{:S(2)}) %collective-permute-start.1) | collective-permute-done | bytes 393248 | tf_op jit(solution)/shard_map/ppermute | solution.py:279
  36.8 3.4 collective-permute-start.3
  40.5 8.9 %collective-permute-start.10 = (bf16[768,768]{1,0:T(8,128)(2,1)S(1)}, bf16[768,768]{1,0:T(8,128)(2,1)}, u32[]{:S(2)}, u32[]{:S(2)}) collective-permute-start(bf16[768,768]{1,0:T(8,128)(2,1)S(1)} %pad_maximum_fusion.6.refs_0_.refs_17_), channel_id=1, source_target_pairs={{0,4},{4,0},{8,12},{12,8},{1,5},{5,1},{9,13},{13,9},{2,6},{6,2},{1... | collective-permute-start | bytes 3538952 | tf_op jit(solution)/shard_map/ppermute | solution.py:329
  51.2 2.4 collective-permute-start.5
  55.4 20.9 %collective-permute-done.10.refs_1_.refs_18_ = bf16[768,768]{1,0:T(8,128)(2,1)} collective-permute-done((bf16[768,768]{1,0:T(8,128)(2,1)S(1)}, bf16[768,768]{1,0:T(8,128)(2,1)}, u32[]{:S(2)}, u32[]{:S(2)}) %collective-permute-start.10) | collective-permute-done | bytes 1179680 | tf_op jit(solution)/shard_map/ppermute | solution.py:329
  76.3 2.1 collective-permute-start.20
  78.4 2.0 collective-permute-start.15
  83.3 2.1 select_bitcast_fusion.1
  85.4 2.1 pad_maximum_fusion
  88.1 13.5 %collective-permute-done.5.refs_1_.refs_14_ = bf16[768,768]{1,0:T(8,128)(2,1)} collective-permute-done((bf16[768,768]{1,0:T(8,128)(2,1)S(1)}, bf16[768,768]{1,0:T(8,128)(2,1)}, u32[]{:S(2)}, u32[]{:S(2)}) %collective-permute-start.5) | collective-permute-done | bytes 1179680 | tf_op jit(solution)/shard_map/ppermute | solution.py:329
  103.5 2.2 collective-permute-start.12
  105.7 21.2 %collective-permute-done.20.refs_10_ = bf16[768,768]{1,0:T(8,128)(2,1)} collective-permute-done((bf16[768,768]{1,0:T(8,128)(2,1)}, bf16[768,768]{1,0:T(8,128)(2,1)}, u32[]{:S(2)}, u32[]{:S(2)}) %collective-permute-start.20) | collective-permute-done | bytes 1179680 | tf_op jit(solution)/shard_map/ppermute | solution.py:329
  128.6 23.6 %collective-permute-done.15.refs_1_.refs_22_ = bf16[768,768]{1,0:T(8,128)(2,1)} collective-permute-done((bf16[768,768]{1,0:T(8,128)(2,1)S(1)}, bf16[768,768]{1,0:T(8,128)(2,1)}, u32[]{:S(2)}, u32[]{:S(2)}) %collective-permute-start.15) | collective-permute-done | bytes 1179680 | tf_op jit(solution)/shard_map/ppermute | solution.py:329
  152.2 2.1 collective-permute-start.7
  155.6 21.8 %collective-permute-done.12 = bf16[768,768]{1,0:T(8,128)(2,1)} collective-permute-done((bf16[768,768]{1,0:T(8,128)(2,1)}, bf16[768,768]{1,0:T(8,128)(2,1)}, u32[]{:S(2)}, u32[]{:S(2)}) %collective-permute-start.12) | collective-permute-done | bytes 1179680 | tf_op jit(solution)/shard_map/ppermute | solution.py:329
  180.9 21.8 %collective-permute-done.7 = bf16[768,768]{1,0:T(8,128)(2,1)} collective-permute-done((bf16[768,768]{1,0:T(8,128)(2,1)}, bf16[768,768]{1,0:T(8,128)(2,1)}, u32[]{:S(2)}, u32[]{:S(2)}) %collective-permute-start.7) | collective-permute-done | bytes 1179680 | tf_op jit(solution)/shard_map/ppermute | solution.py:329
  204.4 22.7 %collective-permute-done.14 = bf16[768,768]{1,0:T(8,128)(2,1)} collective-permute-done((bf16[768,768]{1,0:T(8,128)(2,1)}, bf16[768,768]{1,0:T(8,128)(2,1)}, u32[]{:S(2)}, u32[]{:S(2)}) %collective-permute-start.14) | collective-permute-done | bytes 1179680 | tf_op jit(solution)/shard_map/ppermute | solution.py:329
  238.4 22.6 %collective-permute-start.22 = (bf16[768,768]{1,0:T(8,128)(2,1)}, bf16[768,768]{1,0:T(8,128)(2,1)}, u32[]{:S(2)}, u32[]{:S(2)}) collective-permute-start(bf16[768,768]{1,0:T(8,128)(2,1)} %collective-permute-done.21), channel_id=1, source_target_pairs={{0,4},{4,0},{8,12},{12,8},{1,5},{5,1},{9,13},{13,9},{2,6},{6,2},{1... | collective-permute-start | bytes 3538952 | tf_op jit(solution)/shard_map/ppermute | solution.py:329
  262.4 2.5 broadcast_select_fusion.1
  267.8 7.3 %multiply_reduce_fusion = f32[2,4,128]{2,1,0:T(4,128)S(1)} fusion(bf16[1,2,4,128,3072]{4,3,2,1,0:T(8,128)(2,1)S(1)} %bitcast.195, bf16[1,2,4,128,768]{4,3,2,1,0:T(8,128)(2,1)S(1)} %bitcast.200, bf16[1,2,4,128,768]{4,3,2,1,0:T(8,128)(2,1)S(1)} %bitcast.198, bf16[1,2,4,128,768]{4,3,2,1,0:T(8,128)(2,1)S(1)} %bitcast.202, ...), kind=kLoop, calls=%fused_computation.1 | loop fusion | flops 37747712 | bytes 12587009 | tf_op jit(solution)/shard_map/reduce_sum | solution.py:365
  275.2 5.6 multiply_convert_fusion
  280.8 8.4 %raw_products.4.refs_7_ = f32[1024,768]{1,0:T(8,128)S(1)} custom-call(s32[4]{0:T(128)S(1)} %pad_add_fusion.source_ref, bf16[1024,3072]{1,0:T(8,128)(2,1)S(1)} %get-tuple-element.25.low_ref, bf16[768,768]{1,0:T(8,128)(2,1)S(1)} %pad_maximum_fusion.6.refs_0_.refs_17_, bf16[768,768]{1,0:T(8,128)(2,1)} %collective-permute-done.10.refs_1_.refs_18_, ...), custom_call_target="tpu_custom_call" | custom-call | flops 4831838208 | bytes 14155776 | tf_op jit(solution)/shard_map/raw_products/pallas_call | solution.py:68
  290.9 7.5 %raw_products.3.refs_6_ = f32[1024,768]{1,0:T(8,128)S(1)} custom-call(s32[4]{0:T(128)S(1)} %pad_add_fusion.source_ref, bf16[1024,3072]{1,0:T(8,128)(2,1)S(1)} %get-tuple-element.25.low_ref, bf16[768,768]{1,0:T(8,128)(2,1)S(1)} %pad_maximum_fusion.5.refs_0_.refs_13_, bf16[768,768]{1,0:T(8,128)(2,1)} %collective-permute-done.5.refs_1_.refs_14_, ...), custom_call_target="tpu_custom_call" | custom-call | flops 4831838208 | bytes 14155776 | tf_op jit(solution)/shard_map/raw_products/pallas_call | solution.py:68
  298.4 2.0 collective-permute-start.24
  301.9 5.0 collective-permute-done.22
  306.9 2.5 broadcast_select_fusion.7.refs_11_
  309.3 22.8 %collective-permute-done.19 = bf16[768,768]{1,0:T(8,128)(2,1)} collective-permute-done((bf16[768,768]{1,0:T(8,128)(2,1)}, bf16[768,768]{1,0:T(8,128)(2,1)}, u32[]{:S(2)}, u32[]{:S(2)}) %collective-permute-start.19) | collective-permute-done | bytes 1179680 | tf_op jit(solution)/shard_map/ppermute | solution.py:329
  334.7 2.8 copy-done.1
  337.5 7.5 %raw_products.5.refs_8_ = f32[1024,768]{1,0:T(8,128)S(1)} custom-call(s32[4]{0:T(128)S(1)} %pad_add_fusion.source_ref, bf16[1024,3072]{1,0:T(8,128)(2,1)S(1)} %copy-done.1, bf16[768,768]{1,0:T(8,128)(2,1)S(1)} %pad_maximum_fusion.7.refs_0_.refs_21_, bf16[768,768]{1,0:T(8,128)(2,1)} %collective-permute-done.15.refs_1_.refs_22_, ...), custom_call_target="tpu_custom_call" | custom-call | flops 4831838208 | bytes 14155776 | tf_op jit(solution)/shard_map/raw_products/pallas_call | solution.py:68
  345.0 10.5 %collective-permute-done.24 = bf16[768,768]{1,0:T(8,128)(2,1)} collective-permute-done((bf16[768,768]{1,0:T(8,128)(2,1)}, bf16[768,768]{1,0:T(8,128)(2,1)}, u32[]{:S(2)}, u32[]{:S(2)}) %collective-permute-start.24) | collective-permute-done | bytes 1179680 | tf_op jit(solution)/shard_map/ppermute | solution.py:329
  355.6 2.4 broadcast_select_fusion.6.refs_12_
  358.0 11.5 %sublayer_back.4 = bf16[4,512,768]{2,1,0:T(8,128)(2,1)} custom-call(s32[1]{0:T(128)} %bitcast.2.flag_ref, s32[4]{0:T(128)} %copy-done.11, f32[128,128]{1,0:T(8,128)} %convert_select_fusion.refs_0_, f32[2,128]{1,0:T(2,128)} %pad_maximum_fusion.8.refs_1_, f32[1024,1]{1,0:T(8,128)} %copy.12.refs_2_, f32[1,3072]{1,0:T(1,128)} %refs_3_.7, ...), custom_call_target="tpu_custom_call" | custom-call | flops 19327352832 | bytes 28311552 | tf_op jit(solution)/shard_map/sublayer_back/pallas_call | solution.py:206
  372.8 2.2 convert_add_fusion.3
  389.2 2.7 collective-permute-done.29
  391.9 5.9 collective-permute-done.30
  397.8 7.0 %collective-permute-done.31 = bf16[1,128,768]{1,2,0:T(8,128)(2,1)S(1)} collective-permute-done((bf16[1,128,768]{1,2,0:T(8,128)(2,1)S(1)}, bf16[1,128,768]{1,2,0:T(8,128)(2,1)S(1)}, u32[]{:S(2)}, u32[]{:S(2)}) %collective-permute-start.31) | collective-permute-done | bytes 196640 | tf_op jit(solution)/shard_map/ppermute | solution.py:279
  405.4 3.4 collective-permute-start.33
  408.9 17.8 %collective-permute-done.33 = bf16[512,768]{1,0:T(8,128)(2,1)S(1)} collective-permute-done((bf16[512,768]{1,0:T(8,128)(2,1)S(1)}, bf16[512,768]{1,0:T(8,128)(2,1)S(1)}, u32[]{:S(2)}, u32[]{:S(2)}) %collective-permute-start.33) | collective-permute-done | bytes 786464 | tf_op jit(solution)/shard_map/ppermute | solution.py:296
  428.5 2.0 collective-permute-start.34
  445.0 8.9 %collective-permute-done.37 = bf16[1,128,768]{1,2,0:T(8,128)(2,1)S(1)} collective-permute-done((bf16[1,128,768]{1,2,0:T(8,128)(2,1)S(1)}, bf16[1,128,768]{1,2,0:T(8,128)(2,1)S(1)}, u32[]{:S(2)}, u32[]{:S(2)}) %collective-permute-start.37) | collective-permute-done | bytes 196640 | tf_op jit(solution)/shard_map/ppermute | solution.py:279
  453.9 5.4 collective-permute-done.38
  459.4 7.4 %collective-permute-done.39 = bf16[1,128,768]{1,2,0:T(8,128)(2,1)S(1)} collective-permute-done((bf16[1,128,768]{1,2,0:T(8,128)(2,1)S(1)}, bf16[1,128,768]{1,2,0:T(8,128)(2,1)S(1)}, u32[]{:S(2)}, u32[]{:S(2)}) %collective-permute-start.39) | collective-permute-done | bytes 196640 | tf_op jit(solution)/shard_map/ppermute | solution.py:279
  467.4 3.4 collective-permute-start.41
  470.9 22.0 %sublayer_back.6 = bf16[4,512,768]{2,1,0:T(8,128)(2,1)} custom-call(s32[1]{0:T(128)} %bitcast.53.flag_ref, s32[4]{0:T(128)} %copy-done.11, f32[128,128]{1,0:T(8,128)} %convert_select_fusion.refs_0_, f32[2,128]{1,0:T(2,128)} %pad_maximum_fusion.8.refs_1_, f32[1024,1]{1,0:T(8,128)} %copy.12.refs_2_, f32[1,3072]{1,0:T(1,128)} %refs_3_.7, ...), custom_call_target="tpu_custom_call" | custom-call | flops 19327352832 | bytes 28311552 | tf_op jit(solution)/shard_map/sublayer_back/pallas_call | solution.py:206
  496.7 2.7 collective-permute-start.42
  500.2 2.1 collective-permute-done.42
  504.7 21.6 %sublayer_back.7 = bf16[4,512,768]{2,1,0:T(8,128)(2,1)} custom-call(s32[1]{0:T(128)} %bitcast.53.flag_ref, s32[4]{0:T(128)} %copy-done.11, f32[128,128]{1,0:T(8,128)} %convert_select_fusion.refs_0_, f32[2,128]{1,0:T(2,128)} %pad_maximum_fusion.8.refs_1_, f32[1024,1]{1,0:T(8,128)} %copy.12.refs_2_, f32[1,3072]{1,0:T(1,128)} %refs_3_.7, ...), custom_call_target="tpu_custom_call" | custom-call | flops 19327352832 | bytes 28311552 | tf_op jit(solution)/shard_map/sublayer_back/pallas_call | solution.py:206
  528.1 2.3 collective-permute-start.46
  530.3 2.4 collective-permute-start.36
  533.8 3.0 collective-permute-start.47
  536.9 15.8 %collective-permute-done.36 = bf16[512,768]{1,0:T(8,128)(2,1)S(1)} collective-permute-done((bf16[512,768]{1,0:T(8,128)(2,1)S(1)}, bf16[512,768]{1,0:T(8,128)(2,1)S(1)}, u32[]{:S(2)}, u32[]{:S(2)}) %collective-permute-start.36) | collective-permute-done | bytes 786464 | tf_op jit(solution)/shard_map/ppermute | solution.py:296
  553.4 6.6 %collective-permute-start.43 = (bf16[1,128,768]{2,1,0:T(8,128)(2,1)S(1)}, bf16[1,128,768]{2,1,0:T(8,128)(2,1)S(1)}, u32[]{:S(2)}, u32[]{:S(2)}) collective-permute-start(bf16[1,128,768]{2,1,0:T(8,128)(2,1)S(1)} %get-tuple-element.64), channel_id=1, source_target_pairs={{0,4},{4,8},{8,12},{12,0},{1,5},{5,9},{9,13},{13,1},{2,6},{6,10},{... | collective-permute-start | bytes 589832 | tf_op jit(solution)/shard_map/ppermute | solution.py:279
  560.0 2.3 collective-permute-start.44
  562.3 3.9 collective-permute-start.45
  566.2 2.4 collective-permute-done.47
  569.7 6.6 %collective-permute-start.48 = (bf16[1,128,768]{2,1,0:T(8,128)(2,1)S(1)}, bf16[1,128,768]{2,1,0:T(8,128)(2,1)S(1)}, u32[]{:S(2)}, u32[]{:S(2)}) collective-permute-start(bf16[1,128,768]{2,1,0:T(8,128)(2,1)S(1)} %get-tuple-element.71), channel_id=1, source_target_pairs={{0,4},{4,8},{8,12},{12,0},{1,5},{5,9},{9,13},{13,1},{2,6},{6,10},{... | collective-permute-start | bytes 589832 | tf_op jit(solution)/shard_map/ppermute | solution.py:279
  576.3 2.3 collective-permute-start.49
  578.6 3.9 collective-permute-start.50
  583.2 5.8 collective-permute-done.49
  (195 shorter events, 90.4 us)
Async XLA Ops:
  2.6 17.2 %collective-permute-start = (bf16[2,128,768]{2,1,0:T(8,128)(2,1)S(1)}, bf16[2,128,768]{2,1,0:T(8,128)(2,1)S(1)}, u32[]{:S(2)}, u32[]{:S(2)}) collective-permute-start(bf16[2,128,768]{2,1,0:T(8,128)(2,1)S(1)} %get-tuple-element.54), channel_id=1, source_target_pairs={{0,4},{4,8},{8,12},{12,0},{1,5},{5,9},{9,13},{13,1},{2,6},{6,10},{... | collective-permute-start | bytes 1179656 | tf_op jit(solution)/shard_map/ppermute | solution.py:279
  7.7 28.1 %collective-permute-start.1 = (bf16[2,128,768]{2,1,0:T(8,128)(2,1)S(1)}, bf16[2,128,768]{2,1,0:T(8,128)(2,1)S(1)}, u32[]{:S(2)}, u32[]{:S(2)}) collective-permute-start(bf16[2,128,768]{2,1,0:T(8,128)(2,1)S(1)} %get-tuple-element.53), channel_id=1, source_target_pairs={{0,8},{4,12},{8,0},{12,4},{1,9},{5,13},{9,1},{13,5},{2,10},{6,14},... | collective-permute-start | bytes 1179656 | tf_op jit(solution)/shard_map/ppermute | solution.py:279
  12.2 23.6 %collective-permute-start.2 = (bf16[2,128,768]{2,1,0:T(8,128)(2,1)S(1)}, bf16[2,128,768]{2,1,0:T(8,128)(2,1)S(1)}, u32[]{:S(2)}, u32[]{:S(2)}) collective-permute-start(bf16[2,128,768]{2,1,0:T(8,128)(2,1)S(1)} %get-tuple-element.52), channel_id=1, source_target_pairs={{0,12},{4,0},{8,4},{12,8},{1,13},{5,1},{9,5},{13,9},{2,14},{6,2},{... | collective-permute-start | bytes 1179656 | tf_op jit(solution)/shard_map/ppermute | solution.py:279
  36.8 43.6 %collective-permute-start.3 = (bf16[2,512,768]{2,1,0:T(8,128)(2,1)S(1)}, bf16[2,512,768]{2,1,0:T(8,128)(2,1)S(1)}, u32[]{:S(2)}, u32[]{:S(2)}) collective-permute-start(bf16[2,512,768]{2,1,0:T(8,128)(2,1)S(1)} %fusion.17), channel_id=1, source_target_pairs={{0,2},{1,3},{2,0},{3,1},{4,6},{5,7},{6,4},{7,5},{8,10},{9,11},{10,... | collective-permute-start | bytes 4718600 | tf_op jit(solution)/shard_map/ppermute | solution.py:296
  40.5 240.3 %copy-start.2 = (bf16[768,768]{1,0:T(8,128)(2,1)}, bf16[768,768]{1,0:T(8,128)(2,1)S(1)}, u32[]{:S(2)}) copy-start(bf16[768,768]{1,0:T(8,128)(2,1)S(1)} %pad_maximum_fusion.6.refs_0_.refs_17_) | copy-start | bytes 3538948
  40.5 35.9 %collective-permute-start.10 = (bf16[768,768]{1,0:T(8,128)(2,1)S(1)}, bf16[768,768]{1,0:T(8,128)(2,1)}, u32[]{:S(2)}, u32[]{:S(2)}) collective-permute-start(bf16[768,768]{1,0:T(8,128)(2,1)S(1)} %pad_maximum_fusion.6.refs_0_.refs_17_), channel_id=1, source_target_pairs={{0,4},{4,0},{8,12},{12,8},{1,5},{5,1},{9,13},{13,9},{2,6},{6,2},{1... | collective-permute-start | bytes 3538952 | tf_op jit(solution)/shard_map/ppermute | solution.py:329
  49.4 29.0 %collective-permute-start.11 = (bf16[768,768]{1,0:T(8,128)(2,1)S(1)}, bf16[768,768]{1,0:T(8,128)(2,1)}, u32[]{:S(2)}, u32[]{:S(2)}) collective-permute-start(bf16[768,768]{1,0:T(8,128)(2,1)S(1)} %pad_maximum_fusion.6.refs_0_.refs_17_), channel_id=1, source_target_pairs={{4,8},{8,4},{5,9},{9,5},{6,10},{10,6},{7,11},{11,7},{20,24},{24,20... | collective-permute-start | bytes 3538952 | tf_op jit(solution)/shard_map/ppermute | solution.py:329
  51.2 238.0 %copy-start.3 = (bf16[768,768]{1,0:T(8,128)(2,1)}, bf16[768,768]{1,0:T(8,128)(2,1)S(1)}, u32[]{:S(2)}) copy-start(bf16[768,768]{1,0:T(8,128)(2,1)S(1)} %pad_maximum_fusion.5.refs_0_.refs_13_) | copy-start | bytes 3538948
  51.2 50.4 %collective-permute-start.5 = (bf16[768,768]{1,0:T(8,128)(2,1)S(1)}, bf16[768,768]{1,0:T(8,128)(2,1)}, u32[]{:S(2)}, u32[]{:S(2)}) collective-permute-start(bf16[768,768]{1,0:T(8,128)(2,1)S(1)} %pad_maximum_fusion.5.refs_0_.refs_13_), channel_id=1, source_target_pairs={{0,4},{4,0},{8,12},{12,8},{1,5},{5,1},{9,13},{13,9},{2,6},{6,2},{1... | collective-permute-start | bytes 3538952 | tf_op jit(solution)/shard_map/ppermute | solution.py:329
  53.6 49.9 %collective-permute-start.6 = (bf16[768,768]{1,0:T(8,128)(2,1)S(1)}, bf16[768,768]{1,0:T(8,128)(2,1)}, u32[]{:S(2)}, u32[]{:S(2)}) collective-permute-start(bf16[768,768]{1,0:T(8,128)(2,1)S(1)} %pad_maximum_fusion.5.refs_0_.refs_13_), channel_id=1, source_target_pairs={{4,8},{8,4},{5,9},{9,5},{6,10},{10,6},{7,11},{11,7},{20,24},{24,20... | collective-permute-start | bytes 3538952 | tf_op jit(solution)/shard_map/ppermute | solution.py:329
  55.4 279.3 %copy-start.4 = (bf16[768,768]{1,0:T(8,128)(2,1)}, bf16[768,768]{1,0:T(8,128)(2,1)S(1)}, u32[]{:S(2)}) copy-start(bf16[768,768]{1,0:T(8,128)(2,1)S(1)} %pad_maximum_fusion.7.refs_0_.refs_21_) | copy-start | bytes 3538948
  76.3 50.6 %collective-permute-start.20 = (bf16[768,768]{1,0:T(8,128)(2,1)}, bf16[768,768]{1,0:T(8,128)(2,1)}, u32[]{:S(2)}, u32[]{:S(2)}) collective-permute-start(bf16[768,768]{1,0:T(8,128)(2,1)} %bitcast.32.refs_9_), channel_id=1, source_target_pairs={{0,4},{4,0},{8,12},{12,8},{1,5},{5,1},{9,13},{13,9},{2,6},{6,2},{1... | collective-permute-start | bytes 3538952 | tf_op jit(solution)/shard_map/ppermute | solution.py:329
  78.4 73.8 %collective-permute-start.15 = (bf16[768,768]{1,0:T(8,128)(2,1)S(1)}, bf16[768,768]{1,0:T(8,128)(2,1)}, u32[]{:S(2)}, u32[]{:S(2)}) collective-permute-start(bf16[768,768]{1,0:T(8,128)(2,1)S(1)} %pad_maximum_fusion.7.refs_0_.refs_21_), channel_id=1, source_target_pairs={{0,4},{4,0},{8,12},{12,8},{1,5},{5,1},{9,13},{13,9},{2,6},{6,2},{1... | collective-permute-start | bytes 3538952 | tf_op jit(solution)/shard_map/ppermute | solution.py:329
  81.6 72.7 %collective-permute-start.13 = (bf16[768,768]{1,0:T(8,128)(2,1)}, bf16[768,768]{1,0:T(8,128)(2,1)}, u32[]{:S(2)}, u32[]{:S(2)}) collective-permute-start(bf16[768,768]{1,0:T(8,128)(2,1)} %collective-permute-done.10.refs_1_.refs_18_), channel_id=1, source_target_pairs={{4,8},{8,4},{5,9},{9,5},{6,10},{10,6},{7,11},{11,7},{20,24},{24,20... | collective-permute-start | bytes 3538952 | tf_op jit(solution)/shard_map/ppermute | solution.py:329
  101.6 160.8 %collective-permute-start.4 = (bf16[2,2,512,768]{3,2,1,0:T(8,128)(2,1)}, bf16[2,2,512,768]{3,2,1,0:T(8,128)(2,1)}, u32[]{:S(2)}, u32[]{:S(2)}) collective-permute-start(bf16[2,2,512,768]{3,2,1,0:T(8,128)(2,1)} %pad_maximum_fusion), channel_id=1, source_target_pairs={{0,1},{1,0},{2,3},{3,2},{4,5},{5,4},{6,7},{7,6},{8,9},{9,8},{10,11... | collective-permute-start | bytes 9437192 | tf_op jit(solution)/shard_map/ppermute | solution.py:296
  103.5 73.9 %collective-permute-start.12 = (bf16[768,768]{1,0:T(8,128)(2,1)}, bf16[768,768]{1,0:T(8,128)(2,1)}, u32[]{:S(2)}, u32[]{:S(2)}) collective-permute-start(bf16[768,768]{1,0:T(8,128)(2,1)} %collective-permute-done.11), channel_id=1, source_target_pairs={{0,4},{4,0},{8,12},{12,8},{1,5},{5,1},{9,13},{13,9},{2,6},{6,2},{1... | collective-permute-start | bytes 3538952 | tf_op jit(solution)/shard_map/ppermute | solution.py:329
  126.9 52.3 %collective-permute-start.8 = (bf16[768,768]{1,0:T(8,128)(2,1)}, bf16[768,768]{1,0:T(8,128)(2,1)}, u32[]{:S(2)}, u32[]{:S(2)}) collective-permute-start(bf16[768,768]{1,0:T(8,128)(2,1)} %collective-permute-done.5.refs_1_.refs_14_), channel_id=1, source_target_pairs={{4,8},{8,4},{5,9},{9,5},{6,10},{10,6},{7,11},{11,7},{20,24},{24,20... | collective-permute-start | bytes 3538952 | tf_op jit(solution)/shard_map/ppermute | solution.py:329
  152.2 50.6 %collective-permute-start.7 = (bf16[768,768]{1,0:T(8,128)(2,1)}, bf16[768,768]{1,0:T(8,128)(2,1)}, u32[]{:S(2)}, u32[]{:S(2)}) collective-permute-start(bf16[768,768]{1,0:T(8,128)(2,1)} %collective-permute-done.6), channel_id=1, source_target_pairs={{0,4},{4,0},{8,12},{12,8},{1,5},{5,1},{9,13},{13,9},{2,6},{6,2},{1... | collective-permute-start | bytes 3538952 | tf_op jit(solution)/shard_map/ppermute | solution.py:329
  154.2 72.8 %collective-permute-start.14 = (bf16[768,768]{1,0:T(8,128)(2,1)}, bf16[768,768]{1,0:T(8,128)(2,1)}, u32[]{:S(2)}, u32[]{:S(2)}) collective-permute-start(bf16[768,768]{1,0:T(8,128)(2,1)} %collective-permute-done.13), channel_id=1, source_target_pairs={{0,4},{4,0},{8,12},{12,8},{1,5},{5,1},{9,13},{13,9},{2,6},{6,2},{1... | collective-permute-start | bytes 3538952 | tf_op jit(solution)/shard_map/ppermute | solution.py:329
  177.5 57.3 %collective-permute-start.16 = (bf16[768,768]{1,0:T(8,128)(2,1)S(1)}, bf16[768,768]{1,0:T(8,128)(2,1)}, u32[]{:S(2)}, u32[]{:S(2)}) collective-permute-start(bf16[768,768]{1,0:T(8,128)(2,1)S(1)} %pad_maximum_fusion.7.refs_0_.refs_21_), channel_id=1, source_target_pairs={{4,8},{8,4},{5,9},{9,5},{6,10},{10,6},{7,11},{11,7},{20,24},{24,20... | collective-permute-start | bytes 3538952 | tf_op jit(solution)/shard_map/ppermute | solution.py:329
  179.2 57.6 %collective-permute-start.21 = (bf16[768,768]{1,0:T(8,128)(2,1)}, bf16[768,768]{1,0:T(8,128)(2,1)}, u32[]{:S(2)}, u32[]{:S(2)}) collective-permute-start(bf16[768,768]{1,0:T(8,128)(2,1)} %bitcast.32.refs_9_), channel_id=1, source_target_pairs={{4,8},{8,4},{5,9},{9,5},{6,10},{10,6},{7,11},{11,7},{20,24},{24,20... | collective-permute-start | bytes 3538952 | tf_op jit(solution)/shard_map/ppermute | solution.py:329
  202.7 35.6 %collective-permute-start.18 = (bf16[768,768]{1,0:T(8,128)(2,1)}, bf16[768,768]{1,0:T(8,128)(2,1)}, u32[]{:S(2)}, u32[]{:S(2)}) collective-permute-start(bf16[768,768]{1,0:T(8,128)(2,1)} %collective-permute-done.15.refs_1_.refs_22_), channel_id=1, source_target_pairs={{4,8},{8,4},{5,9},{9,5},{6,10},{10,6},{7,11},{11,7},{20,24},{24,20... | collective-permute-start | bytes 3538952 | tf_op jit(solution)/shard_map/ppermute | solution.py:329
  227.1 33.9 %collective-permute-start.9 = (bf16[768,768]{1,0:T(8,128)(2,1)}, bf16[768,768]{1,0:T(8,128)(2,1)}, u32[]{:S(2)}, u32[]{:S(2)}) collective-permute-start(bf16[768,768]{1,0:T(8,128)(2,1)} %collective-permute-done.8), channel_id=1, source_target_pairs={{0,4},{4,0},{8,12},{12,8},{1,5},{5,1},{9,13},{13,9},{2,6},{6,2},{1... | collective-permute-start | bytes 3538952 | tf_op jit(solution)/shard_map/ppermute | solution.py:329
  228.9 105.8 %copy-start.11 = (s32[4]{0:T(128)}, s32[4]{0:T(128)S(1)}, u32[]{:S(2)}) copy-start(s32[4]{0:T(128)S(1)} %pad_add_fusion.source_ref) | copy-start | bytes 52
  231.0 49.8 %copy-start.5 = (bf16[768,768]{1,0:T(8,128)(2,1)}, bf16[768,768]{1,0:T(8,128)(2,1)S(1)}, u32[]{:S(2)}) copy-start(bf16[768,768]{1,0:T(8,128)(2,1)S(1)} %broadcast_select_fusion.11.refs_2_.refs_19_) | copy-start | bytes 3538948
  232.9 56.4 %copy-start.6 = (bf16[768,768]{1,0:T(8,128)(2,1)}, bf16[768,768]{1,0:T(8,128)(2,1)S(1)}, u32[]{:S(2)}) copy-start(bf16[768,768]{1,0:T(8,128)(2,1)S(1)} %broadcast_select_fusion.13.refs_2_.refs_15_) | copy-start | bytes 3538948
  234.7 46.1 %copy-start.7 = (bf16[768,768]{1,0:T(8,128)(2,1)}, bf16[768,768]{1,0:T(8,128)(2,1)S(1)}, u32[]{:S(2)}) copy-start(bf16[768,768]{1,0:T(8,128)(2,1)S(1)} %broadcast_select_fusion.10.refs_3_.refs_20_) | copy-start | bytes 3538948
  234.7 27.7 %copy-start.16 = (bf16[1,2,512,768]{3,2,1,0:T(8,128)(2,1)S(1)}, bf16[1,2,512,768]{3,2,1,0:T(8,128)(2,1)}, u32[]{:S(2)}) copy-start(bf16[1,2,512,768]{3,2,1,0:T(8,128)(2,1)} %copy-done.15) | copy-start | bytes 4718596
  234.7 27.7 %copy-start.18 = (bf16[1,2,512,768]{3,2,1,0:T(8,128)(2,1)S(1)}, bf16[1,2,512,768]{3,2,1,0:T(8,128)(2,1)}, u32[]{:S(2)}) copy-start(bf16[1,2,512,768]{3,2,1,0:T(8,128)(2,1)} %copy-done.17) | copy-start | bytes 4718596
  234.8 63.7 %collective-permute-start.23 = (bf16[768,768]{1,0:T(8,128)(2,1)}, bf16[768,768]{1,0:T(8,128)(2,1)}, u32[]{:S(2)}, u32[]{:S(2)}) collective-permute-start(bf16[768,768]{1,0:T(8,128)(2,1)} %collective-permute-done.20.refs_10_), channel_id=1, source_target_pairs={{4,8},{8,4},{5,9},{9,5},{6,10},{10,6},{7,11},{11,7},{20,24},{24,20... | collective-permute-start | bytes 3538952 | tf_op jit(solution)/shard_map/ppermute | solution.py:329
  236.8 63.7 %collective-permute-start.17 = (bf16[768,768]{1,0:T(8,128)(2,1)}, bf16[768,768]{1,0:T(8,128)(2,1)}, u32[]{:S(2)}, u32[]{:S(2)}) collective-permute-start(bf16[768,768]{1,0:T(8,128)(2,1)} %collective-permute-done.16), channel_id=1, source_target_pairs={{0,4},{4,0},{8,12},{12,8},{1,5},{5,1},{9,13},{13,9},{2,6},{6,2},{1... | collective-permute-start | bytes 3538952 | tf_op jit(solution)/shard_map/ppermute | solution.py:329
  238.4 68.5 %collective-permute-start.22 = (bf16[768,768]{1,0:T(8,128)(2,1)}, bf16[768,768]{1,0:T(8,128)(2,1)}, u32[]{:S(2)}, u32[]{:S(2)}) collective-permute-start(bf16[768,768]{1,0:T(8,128)(2,1)} %collective-permute-done.21), channel_id=1, source_target_pairs={{0,4},{4,0},{8,12},{12,8},{1,5},{5,1},{9,13},{13,9},{2,6},{6,2},{1... | collective-permute-start | bytes 3538952 | tf_op jit(solution)/shard_map/ppermute | solution.py:329
  261.0 71.2 %collective-permute-start.19 = (bf16[768,768]{1,0:T(8,128)(2,1)}, bf16[768,768]{1,0:T(8,128)(2,1)}, u32[]{:S(2)}, u32[]{:S(2)}) collective-permute-start(bf16[768,768]{1,0:T(8,128)(2,1)} %collective-permute-done.18), channel_id=1, source_target_pairs={{0,4},{4,0},{8,12},{12,8},{1,5},{5,1},{9,13},{13,9},{2,6},{6,2},{1... | collective-permute-start | bytes 3538952 | tf_op jit(solution)/shard_map/ppermute | solution.py:329
  262.4 26.8 %copy-start.8 = (bf16[768,768]{1,0:T(8,128)(2,1)}, bf16[768,768]{1,0:T(8,128)(2,1)S(1)}, u32[]{:S(2)}) copy-start(bf16[768,768]{1,0:T(8,128)(2,1)S(1)} %broadcast_select_fusion.12.refs_3_.refs_16_) | copy-start | bytes 3538948
  298.4 57.1 %collective-permute-start.24 = (bf16[768,768]{1,0:T(8,128)(2,1)}, bf16[768,768]{1,0:T(8,128)(2,1)}, u32[]{:S(2)}, u32[]{:S(2)}) collective-permute-start(bf16[768,768]{1,0:T(8,128)(2,1)} %collective-permute-done.23), channel_id=1, source_target_pairs={{0,4},{4,0},{8,12},{12,8},{1,5},{5,1},{9,13},{13,9},{2,6},{6,2},{1... | collective-permute-start | bytes 3538952 | tf_op jit(solution)/shard_map/ppermute | solution.py:329
  301.9 32.8 %copy-start.9 = (bf16[768,768]{1,0:T(8,128)(2,1)}, bf16[768,768]{1,0:T(8,128)(2,1)S(1)}, u32[]{:S(2)}) copy-start(bf16[768,768]{1,0:T(8,128)(2,1)S(1)} %broadcast_select_fusion.9.refs_2_.refs_23_) | copy-start | bytes 3538948
  371.0 1.8 collective-permute-start.25
  376.0 1.5 collective-permute-start.26
  380.1 11.8 %collective-permute-start.29 = (bf16[1,128,768]{1,2,0:T(8,128)(2,1)S(1)}, bf16[1,128,768]{1,2,0:T(8,128)(2,1)S(1)}, u32[]{:S(2)}, u32[]{:S(2)}) collective-permute-start(bf16[1,128,768]{1,2,0:T(8,128)(2,1)S(1)} %get-tuple-element.76), channel_id=1, source_target_pairs={{16,0},{20,4},{24,8},{28,12},{17,1},{21,5},{25,9},{29,13},{18,2},{... | collective-permute-start | bytes 589832 | tf_op jit(solution)/shard_map/ppermute | solution.py:279
  381.4 16.4 %collective-permute-start.30 = (bf16[1,128,768]{1,2,0:T(8,128)(2,1)S(1)}, bf16[1,128,768]{1,2,0:T(8,128)(2,1)S(1)}, u32[]{:S(2)}, u32[]{:S(2)}) collective-permute-start(bf16[1,128,768]{1,2,0:T(8,128)(2,1)S(1)} %get-tuple-element.79), channel_id=1, source_target_pairs={{16,4},{20,8},{24,12},{28,0},{17,5},{21,9},{25,13},{29,1},{18,6},{... | collective-permute-start | bytes 589832 | tf_op jit(solution)/shard_map/ppermute | solution.py:279
  382.7 22.1 %collective-permute-start.31 = (bf16[1,128,768]{1,2,0:T(8,128)(2,1)S(1)}, bf16[1,128,768]{1,2,0:T(8,128)(2,1)S(1)}, u32[]{:S(2)}, u32[]{:S(2)}) collective-permute-start(bf16[1,128,768]{1,2,0:T(8,128)(2,1)S(1)} %get-tuple-element.78), channel_id=1, source_target_pairs={{16,8},{20,12},{24,0},{28,4},{17,9},{21,13},{25,1},{29,5},{18,10},... | collective-permute-start | bytes 589832 | tf_op jit(solution)/shard_map/ppermute | solution.py:279
  384.0 20.8 %collective-permute-start.32 = (bf16[1,128,768]{1,2,0:T(8,128)(2,1)S(1)}, bf16[1,128,768]{1,2,0:T(8,128)(2,1)S(1)}, u32[]{:S(2)}, u32[]{:S(2)}) collective-permute-start(bf16[1,128,768]{1,2,0:T(8,128)(2,1)S(1)} %get-tuple-element.77), channel_id=1, source_target_pairs={{16,12},{20,0},{24,4},{28,8},{17,13},{21,1},{25,5},{29,9},{18,14},... | collective-permute-start | bytes 589832 | tf_op jit(solution)/shard_map/ppermute | solution.py:279
  388.4 42.2 %collective-permute-start.27 = (bf16[2,512,768]{2,1,0:T(8,128)(2,1)S(1)}, bf16[2,512,768]{2,1,0:T(8,128)(2,1)S(1)}, u32[]{:S(2)}, u32[]{:S(2)}) collective-permute-start(bf16[2,512,768]{2,1,0:T(8,128)(2,1)S(1)} %dynamic-slice_bitcast_fusion.2), channel_id=1, source_target_pairs={{16,17},{17,16},{18,19},{19,18},{20,21},{21,20},{22,23},{23,22},{2... | collective-permute-start | bytes 4718600 | tf_op jit(solution)/shard_map/ppermute | solution.py:296
  405.4 21.4 %copy-start.28 = (bf16[512,768]{1,0:T(8,128)(2,1)}, bf16[512,768]{1,0:T(8,128)(2,1)S(1)}, u32[]{:S(2)}) copy-start(bf16[512,768]{1,0:T(8,128)(2,1)S(1)} %fusion.21) | copy-start | bytes 2359300
  405.4 21.3 %collective-permute-start.33 = (bf16[512,768]{1,0:T(8,128)(2,1)S(1)}, bf16[512,768]{1,0:T(8,128)(2,1)S(1)}, u32[]{:S(2)}, u32[]{:S(2)}) collective-permute-start(bf16[512,768]{1,0:T(8,128)(2,1)S(1)} %fusion.21), channel_id=1, source_target_pairs={{0,2},{1,3},{2,0},{3,1},{4,6},{5,7},{6,4},{7,5},{8,10},{9,11},{10,... | collective-permute-start | bytes 2359304 | tf_op jit(solution)/shard_map/ppermute | solution.py:296
  428.5 12.7 %collective-permute-start.34 = (bf16[2,512,768]{2,1,0:T(8,128)(2,1)}, bf16[2,512,768]{2,1,0:T(8,128)(2,1)}, u32[]{:S(2)}, u32[]{:S(2)}) collective-permute-start(bf16[2,512,768]{2,1,0:T(8,128)(2,1)} %pad_maximum_fusion.3), channel_id=1, source_target_pairs={{0,1},{1,0},{2,3},{3,2},{4,5},{5,4},{6,7},{7,6},{8,9},{9,8},{10,11... | collective-permute-start | bytes 4718600 | tf_op jit(solution)/shard_map/ppermute | solution.py:296
  431.9 1.6 collective-permute-start.28
  436.0 17.9 %collective-permute-start.37 = (bf16[1,128,768]{1,2,0:T(8,128)(2,1)S(1)}, bf16[1,128,768]{1,2,0:T(8,128)(2,1)S(1)}, u32[]{:S(2)}, u32[]{:S(2)}) collective-permute-start(bf16[1,128,768]{1,2,0:T(8,128)(2,1)S(1)} %get-tuple-element.75), channel_id=1, source_target_pairs={{16,0},{20,4},{24,8},{28,12},{17,1},{21,5},{25,9},{29,13},{18,2},{... | collective-permute-start | bytes 589832 | tf_op jit(solution)/shard_map/ppermute | solution.py:279
  437.3 22.1 %collective-permute-start.38 = (bf16[1,128,768]{1,2,0:T(8,128)(2,1)S(1)}, bf16[1,128,768]{1,2,0:T(8,128)(2,1)S(1)}, u32[]{:S(2)}, u32[]{:S(2)}) collective-permute-start(bf16[1,128,768]{1,2,0:T(8,128)(2,1)S(1)} %get-tuple-element.74), channel_id=1, source_target_pairs={{16,4},{20,8},{24,12},{28,0},{17,5},{21,9},{25,13},{29,1},{18,6},{... | collective-permute-start | bytes 589832 | tf_op jit(solution)/shard_map/ppermute | solution.py:279
  438.6 28.2 %collective-permute-start.39 = (bf16[1,128,768]{1,2,0:T(8,128)(2,1)S(1)}, bf16[1,128,768]{1,2,0:T(8,128)(2,1)S(1)}, u32[]{:S(2)}, u32[]{:S(2)}) collective-permute-start(bf16[1,128,768]{1,2,0:T(8,128)(2,1)S(1)} %get-tuple-element.73), channel_id=1, source_target_pairs={{16,8},{20,12},{24,0},{28,4},{17,9},{21,13},{25,1},{29,5},{18,10},... | collective-permute-start | bytes 589832 | tf_op jit(solution)/shard_map/ppermute | solution.py:279
  439.9 26.9 %collective-permute-start.40 = (bf16[1,128,768]{1,2,0:T(8,128)(2,1)S(1)}, bf16[1,128,768]{1,2,0:T(8,128)(2,1)S(1)}, u32[]{:S(2)}, u32[]{:S(2)}) collective-permute-start(bf16[1,128,768]{1,2,0:T(8,128)(2,1)S(1)} %get-tuple-element.72), channel_id=1, source_target_pairs={{16,12},{20,0},{24,4},{28,8},{17,13},{21,1},{25,5},{29,9},{18,14},... | collective-permute-start | bytes 589832 | tf_op jit(solution)/shard_map/ppermute | solution.py:279
  467.4 28.9 %collective-permute-start.41 = (bf16[512,768]{1,0:T(8,128)(2,1)S(1)}, bf16[512,768]{1,0:T(8,128)(2,1)S(1)}, u32[]{:S(2)}, u32[]{:S(2)}) collective-permute-start(bf16[512,768]{1,0:T(8,128)(2,1)S(1)} %fusion.23), channel_id=1, source_target_pairs={{0,2},{1,3},{2,0},{3,1},{4,6},{5,7},{6,4},{7,5},{8,10},{9,11},{10,... | collective-permute-start | bytes 2359304 | tf_op jit(solution)/shard_map/ppermute | solution.py:296
  494.4 5.3 collective-permute-start.35
  496.7 5.7 collective-permute-start.42
  528.1 5.3 collective-permute-start.46
  530.3 22.3 %collective-permute-start.36 = (bf16[512,768]{1,0:T(8,128)(2,1)S(1)}, bf16[512,768]{1,0:T(8,128)(2,1)S(1)}, u32[]{:S(2)}, u32[]{:S(2)}) collective-permute-start(bf16[512,768]{1,0:T(8,128)(2,1)S(1)} %fusion.32), channel_id=1, source_target_pairs={{0,2},{1,3},{2,0},{3,1},{4,6},{5,7},{6,4},{7,5},{8,10},{9,11},{10,... | collective-permute-start | bytes 2359304 | tf_op jit(solution)/shard_map/ppermute | solution.py:296
  533.7 18.9 %copy-start.29 = (bf16[512,768]{1,0:T(8,128)(2,1)S(1)}, bf16[512,768]{1,0:T(8,128)(2,1)}, u32[]{:S(2)}) copy-start(bf16[512,768]{1,0:T(8,128)(2,1)} %copy-done.28) | copy-start | bytes 2359300
  533.8 34.9 %collective-permute-start.47 = (bf16[512,768]{1,0:T(8,128)(2,1)S(1)}, bf16[512,768]{1,0:T(8,128)(2,1)S(1)}, u32[]{:S(2)}, u32[]{:S(2)}) collective-permute-start(bf16[512,768]{1,0:T(8,128)(2,1)S(1)} %fusion.33), channel_id=1, source_target_pairs={{0,2},{1,3},{2,0},{3,1},{4,6},{5,7},{6,4},{7,5},{8,10},{9,11},{10,... | collective-permute-start | bytes 2359304 | tf_op jit(solution)/shard_map/ppermute | solution.py:296
  553.4 25.2 %collective-permute-start.43 = (bf16[1,128,768]{2,1,0:T(8,128)(2,1)S(1)}, bf16[1,128,768]{2,1,0:T(8,128)(2,1)S(1)}, u32[]{:S(2)}, u32[]{:S(2)}) collective-permute-start(bf16[1,128,768]{2,1,0:T(8,128)(2,1)S(1)} %get-tuple-element.64), channel_id=1, source_target_pairs={{0,4},{4,8},{8,12},{12,0},{1,5},{5,9},{9,13},{13,1},{2,6},{6,10},{... | collective-permute-start | bytes 589832 | tf_op jit(solution)/shard_map/ppermute | solution.py:279
  560.0 22.5 %collective-permute-start.44 = (bf16[1,128,768]{2,1,0:T(8,128)(2,1)S(1)}, bf16[1,128,768]{2,1,0:T(8,128)(2,1)S(1)}, u32[]{:S(2)}, u32[]{:S(2)}) collective-permute-start(bf16[1,128,768]{2,1,0:T(8,128)(2,1)S(1)} %get-tuple-element.66), channel_id=1, source_target_pairs={{0,8},{4,12},{8,0},{12,4},{1,9},{5,13},{9,1},{13,5},{2,10},{6,14},... | collective-permute-start | bytes 589832 | tf_op jit(solution)/shard_map/ppermute | solution.py:279
  562.3 20.2 %collective-permute-start.45 = (bf16[1,128,768]{2,1,0:T(8,128)(2,1)S(1)}, bf16[1,128,768]{2,1,0:T(8,128)(2,1)S(1)}, u32[]{:S(2)}, u32[]{:S(2)}) collective-permute-start(bf16[1,128,768]{2,1,0:T(8,128)(2,1)S(1)} %get-tuple-element.65), channel_id=1, source_target_pairs={{0,12},{4,0},{8,4},{12,8},{1,13},{5,1},{9,5},{13,9},{2,14},{6,2},{... | collective-permute-start | bytes 589832 | tf_op jit(solution)/shard_map/ppermute | solution.py:279
  569.7 13.5 %collective-permute-start.48 = (bf16[1,128,768]{2,1,0:T(8,128)(2,1)S(1)}, bf16[1,128,768]{2,1,0:T(8,128)(2,1)S(1)}, u32[]{:S(2)}, u32[]{:S(2)}) collective-permute-start(bf16[1,128,768]{2,1,0:T(8,128)(2,1)S(1)} %get-tuple-element.71), channel_id=1, source_target_pairs={{0,4},{4,8},{8,12},{12,0},{1,5},{5,9},{9,13},{13,1},{2,6},{6,10},{... | collective-permute-start | bytes 589832 | tf_op jit(solution)/shard_map/ppermute | solution.py:279
  576.3 12.7 %collective-permute-start.49 = (bf16[1,128,768]{2,1,0:T(8,128)(2,1)S(1)}, bf16[1,128,768]{2,1,0:T(8,128)(2,1)S(1)}, u32[]{:S(2)}, u32[]{:S(2)}) collective-permute-start(bf16[1,128,768]{2,1,0:T(8,128)(2,1)S(1)} %get-tuple-element.70), channel_id=1, source_target_pairs={{0,8},{4,12},{8,0},{12,4},{1,9},{5,13},{9,1},{13,5},{2,10},{6,14},... | collective-permute-start | bytes 589832 | tf_op jit(solution)/shard_map/ppermute | solution.py:279
  578.6 11.7 %collective-permute-start.50 = (bf16[1,128,768]{2,1,0:T(8,128)(2,1)S(1)}, bf16[1,128,768]{2,1,0:T(8,128)(2,1)S(1)}, u32[]{:S(2)}, u32[]{:S(2)}) collective-permute-start(bf16[1,128,768]{2,1,0:T(8,128)(2,1)S(1)} %get-tuple-element.69), channel_id=1, source_target_pairs={{0,12},{4,0},{8,4},{12,8},{1,13},{5,1},{9,5},{13,9},{2,14},{6,2},{... | collective-permute-start | bytes 589832 | tf_op jit(solution)/shard_map/ppermute | solution.py:279
  (25 other events, 124.7 us)

commit v4 on v3

--- a/solution.py
+++ b/solution.py
@@ -404,24 +404,17 @@
         own, far = core_sum(term_of(1, grad_space, b * rows, b, tie), 1)
         space_parts.append(add(share_space[b], side_sum(own, far, 1, None)))
         sent.append(send_rows(space_parts[-1], leave_space, 1))
-    shares, fulls, terms, halves = [], [], [], []
+    shares, fulls, time_parts, returned = [], [], [], []
+    term = far = None
     for b in range(batches):
-        if b == 0:
-            shares.append(place_rows(sent[b], enter_time)[0])
-            fulls.append(gather_share(shares[-1]))
-        terms.append(term_of(0, fulls[b], 0, b, halves[-1][1] if b else None))
-        halves.append(core_sum(terms[-1], 0))
-        if b + 1 < batches:
-            arrived, _ = lax.optimization_barrier((sent[b + 1], fulls[b]))
-            shares.append(place_rows(arrived, enter_time)[0])
-            fulls.append(gather_share(shares[-1], terms[-1]))
-    time_parts, returned = [], []
-    for b in range(batches):
-        tie = terms[b + 1] if b + 1 < batches else None
-        part = add(shares[b], side_sum(*halves[b], 0, tie))
+        arrived = sent[b]
         if b:
-            part, _ = lax.optimization_barrier((part, returned[-1][0]))
-        time_parts.append(part)
+            arrived, _ = lax.optimization_barrier((arrived, term))
+        shares.append(place_rows(arrived, enter_time)[0])
+        fulls.append(gather_share(shares[-1]))
+        term = term_of(0, fulls[b], 0, b, None)
+        own, far = core_sum(term, 0)
+        time_parts.append(add(shares[b], side_sum(own, far, 0, None)))
         returned.append(send_rows(time_parts[-1], leave_time, 0))
     time_parts = [place_rows(parts, enter_space)[0] for parts in returned]
     result = jnp.where(on_last, jnp.stack(space_parts), jnp.stack(time_parts))

time: 595 us -> 593 us (level)
  starting transfers between devices: 143 us -> 130 us
  waiting for transfers between devices: 288 us -> 298 us
    ppermute x14, waiting for transfers between devices: 39.2 us -> 57.3 us  [swap(): return lax.ppermute(array_in, ('section', 'head'), pairs)]
    ppermute x20, starting transfers between devices: 61.6 us -> 55 us  [along(): return lax.ppermute(array_in, 'frame', pairs)]
  transfers between devices with their start and end apart: 51 -> 51, of which waited for: 26 -> 21; matrix products, arithmetic and copies ran while one was open for 9% -> 9% of each run, Pallas kernels for 8% -> 12%
where the time goes in v4:
time: 593 us; the launch traced here: 591 us
  waiting for transfers between devices  298 us (50%)
  starting transfers between devices  130 us (22%)
  Pallas kernels  80.1 us (14%)
  other arithmetic  52.8 us (9%)
  local copies, waits for them, and re-layouts  19.1 us (3%)
  matrix products  8.86 us (1%)
    ppermute x20, waiting for transfers between devices, along(): return lax.ppermute(array_in, 'frame', pairs)  181 us
    ppermute x17, waiting for transfers between devices, send_rows(): lax.ppermute(part, ('section', 'frame'), [(from_section * frame_count + s...  59.8 us
    ppermute x14, waiting for transfers between devices, swap(): return lax.ppermute(array_in, ('section', 'head'), pairs)  57.3 us
    pallas_call x4, Pallas kernels, run_back(): pl.pallas_call(functools.partial(back_kernel, chunks, slots, head_dim, fi...  56.7 us
    ppermute x20, starting transfers between devices, along(): return lax.ppermute(array_in, 'frame', pairs)  55 us
    ppermute x17, starting transfers between devices, send_rows(): lax.ppermute(part, ('section', 'frame'), [(from_section * frame_count + s...  42.9 us
    ppermute x14, starting transfers between devices, swap(): return lax.ppermute(array_in, ('section', 'head'), pairs)  32.4 us
    pallas_call x3, Pallas kernels, run_raw(): pl.pallas_call(raw_kernel, grid_spec=pltpu.PrefetchScalarGridSpec(num_sca...  23.4 us
  transfers between devices with their start and end apart: 51, of which 21 were waited for; matrix products, arithmetic and copies ran while one was open for 9% of the time, Pallas kernels for 12%

profile of v4, /device:TPU:0, one launch (start us, length us, event | category | flops | bytes accessed | tf_op | source)
XLA Modules:
  0.0 591.0 jit_solution(7357662161740463846)
XLA Ops:
  0.0 2.4 fusion.14
  2.6 7.1 %collective-permute-start.2 = (bf16[2,128,768]{2,1,0:T(8,128)(2,1)S(1)}, bf16[2,128,768]{2,1,0:T(8,128)(2,1)S(1)}, u32[]{:S(2)}, u32[]{:S(2)}) collective-permute-start(bf16[2,128,768]{2,1,0:T(8,128)(2,1)S(1)} %get-tuple-element.44), channel_id=1, source_target_pairs={{0,12},{4,0},{8,4},{12,8},{1,13},{5,1},{9,5},{13,9},{2,14},{6,2},{... | collective-permute-start | bytes 1179656 | tf_op jit(solution)/shard_map/ppermute | solution.py:279
  9.7 1.9 collective-permute-start.1
  11.6 2.9 collective-permute-start
  14.7 4.5 collective-permute-done.2
  19.3 23.9 %collective-permute-done.1 = bf16[2,128,768]{2,1,0:T(8,128)(2,1)S(1)} collective-permute-done((bf16[2,128,768]{2,1,0:T(8,128)(2,1)S(1)}, bf16[2,128,768]{2,1,0:T(8,128)(2,1)S(1)}, u32[]{:S(2)}, u32[]{:S(2)}) %collective-permute-start.1) | collective-permute-done | bytes 393248 | tf_op jit(solution)/shard_map/ppermute | solution.py:279
  44.3 3.4 collective-permute-start.3
  51.4 2.8 collective-permute-start.10
  55.9 21.0 %collective-permute-done.5.refs_1_.refs_14_ = bf16[768,768]{1,0:T(8,128)(2,1)} collective-permute-done((bf16[768,768]{1,0:T(8,128)(2,1)S(1)}, bf16[768,768]{1,0:T(8,128)(2,1)}, u32[]{:S(2)}, u32[]{:S(2)}) %collective-permute-start.5) | collective-permute-done | bytes 1179680 | tf_op jit(solution)/shard_map/ppermute | solution.py:329
  83.2 2.1 select_bitcast_fusion.1
  85.3 2.1 pad_maximum_fusion
  88.0 14.2 %collective-permute-done.10.refs_1_.refs_18_ = bf16[768,768]{1,0:T(8,128)(2,1)} collective-permute-done((bf16[768,768]{1,0:T(8,128)(2,1)S(1)}, bf16[768,768]{1,0:T(8,128)(2,1)}, u32[]{:S(2)}, u32[]{:S(2)}) %collective-permute-start.10) | collective-permute-done | bytes 1179680 | tf_op jit(solution)/shard_map/ppermute | solution.py:329
  102.2 1.9 collective-permute-start.4
  104.2 2.0 collective-permute-start.7
  106.2 21.4 %collective-permute-done.15.refs_1_.refs_22_ = bf16[768,768]{1,0:T(8,128)(2,1)} collective-permute-done((bf16[768,768]{1,0:T(8,128)(2,1)S(1)}, bf16[768,768]{1,0:T(8,128)(2,1)}, u32[]{:S(2)}, u32[]{:S(2)}) %collective-permute-start.15) | collective-permute-done | bytes 1179680 | tf_op jit(solution)/shard_map/ppermute | solution.py:329
  130.8 25.9 %collective-permute-start.9 = (bf16[768,768]{1,0:T(8,128)(2,1)}, bf16[768,768]{1,0:T(8,128)(2,1)}, u32[]{:S(2)}, u32[]{:S(2)}) collective-permute-start(bf16[768,768]{1,0:T(8,128)(2,1)} %collective-permute-done.8), channel_id=1, source_target_pairs={{0,4},{4,0},{8,12},{12,8},{1,5},{5,1},{9,13},{13,9},{2,6},{6,2},{1... | collective-permute-start | bytes 3538952 | tf_op jit(solution)/shard_map/ppermute | solution.py:329
  157.3 20.7 %collective-permute-done.12 = bf16[768,768]{1,0:T(8,128)(2,1)} collective-permute-done((bf16[768,768]{1,0:T(8,128)(2,1)}, bf16[768,768]{1,0:T(8,128)(2,1)}, u32[]{:S(2)}, u32[]{:S(2)}) %collective-permute-start.12) | collective-permute-done | bytes 1179680 | tf_op jit(solution)/shard_map/ppermute | solution.py:329
  181.5 21.9 %collective-permute-done.9 = bf16[768,768]{1,0:T(8,128)(2,1)} collective-permute-done((bf16[768,768]{1,0:T(8,128)(2,1)}, bf16[768,768]{1,0:T(8,128)(2,1)}, u32[]{:S(2)}, u32[]{:S(2)}) %collective-permute-start.9) | collective-permute-done | bytes 1179680 | tf_op jit(solution)/shard_map/ppermute | solution.py:329
  207.1 1.8 broadcast_select_fusion.11.refs_2_.refs_19_
  209.0 1.8 broadcast_select_fusion.12.refs_3_.refs_16_
  210.9 17.8 %collective-permute-done.20.refs_10_ = bf16[768,768]{1,0:T(8,128)(2,1)} collective-permute-done((bf16[768,768]{1,0:T(8,128)(2,1)}, bf16[768,768]{1,0:T(8,128)(2,1)}, u32[]{:S(2)}, u32[]{:S(2)}) %collective-permute-start.20) | collective-permute-done | bytes 1179680 | tf_op jit(solution)/shard_map/ppermute | solution.py:329
  230.7 1.9 collective-permute-start.23
  232.6 21.3 %collective-permute-done.14 = bf16[768,768]{1,0:T(8,128)(2,1)} collective-permute-done((bf16[768,768]{1,0:T(8,128)(2,1)}, bf16[768,768]{1,0:T(8,128)(2,1)}, u32[]{:S(2)}, u32[]{:S(2)}) %collective-permute-start.14) | collective-permute-done | bytes 1179680 | tf_op jit(solution)/shard_map/ppermute | solution.py:329
  257.0 2.5 broadcast_select_fusion.1
  262.4 7.3 %multiply_reduce_fusion = f32[2,4,128]{2,1,0:T(4,128)S(1)} fusion(bf16[1,2,4,128,3072]{4,3,2,1,0:T(8,128)(2,1)S(1)} %bitcast.195, bf16[1,2,4,128,768]{4,3,2,1,0:T(8,128)(2,1)S(1)} %bitcast.200, bf16[1,2,4,128,768]{4,3,2,1,0:T(8,128)(2,1)S(1)} %bitcast.198, bf16[1,2,4,128,768]{4,3,2,1,0:T(8,128)(2,1)S(1)} %bitcast.202, ...), kind=kLoop, calls=%fused_computation.1 | loop fusion | flops 37747712 | bytes 12587009 | tf_op jit(solution)/shard_map/reduce_sum | solution.py:365
  269.7 5.6 multiply_convert_fusion
  275.3 8.4 %raw_products.3.refs_6_ = f32[1024,768]{1,0:T(8,128)S(1)} custom-call(s32[4]{0:T(128)S(1)} %pad_add_fusion.source_ref, bf16[1024,3072]{1,0:T(8,128)(2,1)S(1)} %get-tuple-element.17.low_ref, bf16[768,768]{1,0:T(8,128)(2,1)S(1)} %pad_maximum_fusion.5.refs_0_.refs_13_, bf16[768,768]{1,0:T(8,128)(2,1)} %collective-permute-done.5.refs_1_.refs_14_, ...), custom_call_target="tpu_custom_call" | custom-call | flops 4831838208 | bytes 14155776 | tf_op jit(solution)/shard_map/raw_products/pallas_call | solution.py:68
  285.4 7.5 %raw_products.4.refs_7_ = f32[1024,768]{1,0:T(8,128)S(1)} custom-call(s32[4]{0:T(128)S(1)} %pad_add_fusion.source_ref, bf16[1024,3072]{1,0:T(8,128)(2,1)S(1)} %get-tuple-element.17.low_ref, bf16[768,768]{1,0:T(8,128)(2,1)S(1)} %pad_maximum_fusion.6.refs_0_.refs_17_, bf16[768,768]{1,0:T(8,128)(2,1)} %collective-permute-done.10.refs_1_.refs_18_, ...), custom_call_target="tpu_custom_call" | custom-call | flops 4831838208 | bytes 14155776 | tf_op jit(solution)/shard_map/raw_products/pallas_call | solution.py:68
  293.4 2.0 broadcast_select_fusion.9.refs_2_.refs_23_
  295.4 9.1 %collective-permute-done.22 = bf16[768,768]{1,0:T(8,128)(2,1)} collective-permute-done((bf16[768,768]{1,0:T(8,128)(2,1)}, bf16[768,768]{1,0:T(8,128)(2,1)}, u32[]{:S(2)}, u32[]{:S(2)}) %collective-permute-start.22) | collective-permute-done | bytes 1179680 | tf_op jit(solution)/shard_map/ppermute | solution.py:329
  304.5 2.4 broadcast_select_fusion.7.refs_11_
  306.9 22.8 %collective-permute-done.19 = bf16[768,768]{1,0:T(8,128)(2,1)} collective-permute-done((bf16[768,768]{1,0:T(8,128)(2,1)}, bf16[768,768]{1,0:T(8,128)(2,1)}, u32[]{:S(2)}, u32[]{:S(2)}) %collective-permute-start.19) | collective-permute-done | bytes 1179680 | tf_op jit(solution)/shard_map/ppermute | solution.py:329
  332.4 2.8 copy-done.1
  335.1 7.5 %raw_products.5.refs_8_ = f32[1024,768]{1,0:T(8,128)S(1)} custom-call(s32[4]{0:T(128)S(1)} %pad_add_fusion.source_ref, bf16[1024,3072]{1,0:T(8,128)(2,1)S(1)} %copy-done.1, bf16[768,768]{1,0:T(8,128)(2,1)S(1)} %pad_maximum_fusion.7.refs_0_.refs_21_, bf16[768,768]{1,0:T(8,128)(2,1)} %collective-permute-done.15.refs_1_.refs_22_, ...), custom_call_target="tpu_custom_call" | custom-call | flops 4831838208 | bytes 14155776 | tf_op jit(solution)/shard_map/raw_products/pallas_call | solution.py:68
  342.7 11.0 %collective-permute-done.24 = bf16[768,768]{1,0:T(8,128)(2,1)} collective-permute-done((bf16[768,768]{1,0:T(8,128)(2,1)}, bf16[768,768]{1,0:T(8,128)(2,1)}, u32[]{:S(2)}, u32[]{:S(2)}) %collective-permute-start.24) | collective-permute-done | bytes 1179680 | tf_op jit(solution)/shard_map/ppermute | solution.py:329
  353.6 2.4 broadcast_select_fusion.6.refs_12_
  356.1 11.5 %sublayer_back.4 = bf16[4,512,768]{2,1,0:T(8,128)(2,1)} custom-call(s32[1]{0:T(128)} %bitcast.2.flag_ref, s32[4]{0:T(128)} %copy-done.11, f32[128,128]{1,0:T(8,128)} %convert_select_fusion.refs_0_, f32[2,128]{1,0:T(2,128)} %pad_maximum_fusion.8.refs_1_, f32[1024,1]{1,0:T(8,128)} %copy.12.refs_2_, f32[1,3072]{1,0:T(1,128)} %refs_3_.7, ...), custom_call_target="tpu_custom_call" | custom-call | flops 19327352832 | bytes 28311552 | tf_op jit(solution)/shard_map/sublayer_back/pallas_call | solution.py:206
  370.9 2.2 convert_add_fusion.3
  387.2 5.3 collective-permute-done.32
  392.5 13.4 %collective-permute-done.31 = bf16[1,128,768]{1,2,0:T(8,128)(2,1)S(1)} collective-permute-done((bf16[1,128,768]{1,2,0:T(8,128)(2,1)S(1)}, bf16[1,128,768]{1,2,0:T(8,128)(2,1)S(1)}, u32[]{:S(2)}, u32[]{:S(2)}) %collective-permute-start.31) | collective-permute-done | bytes 196640 | tf_op jit(solution)/shard_map/ppermute | solution.py:279
  406.6 3.4 collective-permute-start.33
  410.1 16.6 %collective-permute-done.33 = bf16[512,768]{1,0:T(8,128)(2,1)S(1)} collective-permute-done((bf16[512,768]{1,0:T(8,128)(2,1)S(1)}, bf16[512,768]{1,0:T(8,128)(2,1)S(1)}, u32[]{:S(2)}, u32[]{:S(2)}) %collective-permute-start.33) | collective-permute-done | bytes 786464 | tf_op jit(solution)/shard_map/ppermute | solution.py:296
  428.5 2.0 collective-permute-start.34
  443.0 2.0 pad_maximum_fusion.1.refs_4_
  445.0 22.0 %sublayer_back.6 = bf16[4,512,768]{2,1,0:T(8,128)(2,1)} custom-call(s32[1]{0:T(128)} %bitcast.53.flag_ref, s32[4]{0:T(128)} %copy-done.11, f32[128,128]{1,0:T(8,128)} %convert_select_fusion.refs_0_, f32[2,128]{1,0:T(2,128)} %pad_maximum_fusion.8.refs_1_, f32[1024,1]{1,0:T(8,128)} %copy.12.refs_2_, f32[1,3072]{1,0:T(1,128)} %refs_3_.7, ...), custom_call_target="tpu_custom_call" | custom-call | flops 19327352832 | bytes 28311552 | tf_op jit(solution)/shard_map/sublayer_back/pallas_call | solution.py:206
  467.7 3.4 collective-permute-start.44
  471.1 18.4 %collective-permute-done.44 = bf16[512,768]{1,0:T(8,128)(2,1)S(1)} collective-permute-done((bf16[512,768]{1,0:T(8,128)(2,1)S(1)}, bf16[512,768]{1,0:T(8,128)(2,1)S(1)}, u32[]{:S(2)}, u32[]{:S(2)}) %collective-permute-start.44) | collective-permute-done | bytes 786464 | tf_op jit(solution)/shard_map/ppermute | solution.py:296
  489.8 2.2 collective-permute-start.45
  493.2 2.4 collective-permute-start.35
  496.1 1.9 pad_maximum_fusion.2.refs_4_
  498.0 21.7 %sublayer_back.7 = bf16[4,512,768]{2,1,0:T(8,128)(2,1)} custom-call(s32[1]{0:T(128)} %bitcast.53.flag_ref, s32[4]{0:T(128)} %copy-done.11, f32[128,128]{1,0:T(8,128)} %convert_select_fusion.refs_0_, f32[2,128]{1,0:T(2,128)} %pad_maximum_fusion.8.refs_1_, f32[1024,1]{1,0:T(8,128)} %copy.12.refs_2_, f32[1,3072]{1,0:T(1,128)} %refs_3_.7, ...), custom_call_target="tpu_custom_call" | custom-call | flops 19327352832 | bytes 28311552 | tf_op jit(solution)/shard_map/sublayer_back/pallas_call | solution.py:206
  521.2 1.9 collective-permute-start.46
  523.2 1.9 convert_add_fusion.1
  525.2 3.4 collective-permute-start.36
  529.1 2.5 collective-permute-start.47
  531.7 15.7 %collective-permute-done.36 = bf16[512,768]{1,0:T(8,128)(2,1)S(1)} collective-permute-done((bf16[512,768]{1,0:T(8,128)(2,1)S(1)}, bf16[512,768]{1,0:T(8,128)(2,1)S(1)}, u32[]{:S(2)}, u32[]{:S(2)}) %collective-permute-start.36) | collective-permute-done | bytes 786464 | tf_op jit(solution)/shard_map/ppermute | solution.py:296
  548.2 4.1 collective-permute-start.39
  552.4 4.2 collective-permute-start.38
  556.6 2.0 collective-permute-start.37
  558.6 5.3 collective-permute-done.47
  564.6 4.1 collective-permute-start.50
  568.8 4.2 collective-permute-start.49
  573.0 2.0 collective-permute-start.48
  576.0 12.3 %collective-permute-done.49 = bf16[1,128,768]{2,1,0:T(8,128)(2,1)S(1)} collective-permute-done((bf16[1,128,768]{2,1,0:T(8,128)(2,1)S(1)}, bf16[1,128,768]{2,1,0:T(8,128)(2,1)S(1)}, u32[]{:S(2)}, u32[]{:S(2)}) %collective-permute-start.49) | collective-permute-done | bytes 196640 | tf_op jit(solution)/shard_map/ppermute | solution.py:279
  (194 shorter events, 79.1 us)
Async XLA Ops:
  2.6 16.7 %collective-permute-start.2 = (bf16[2,128,768]{2,1,0:T(8,128)(2,1)S(1)}, bf16[2,128,768]{2,1,0:T(8,128)(2,1)S(1)}, u32[]{:S(2)}, u32[]{:S(2)}) collective-permute-start(bf16[2,128,768]{2,1,0:T(8,128)(2,1)S(1)} %get-tuple-element.44), channel_id=1, source_target_pairs={{0,12},{4,0},{8,4},{12,8},{1,13},{5,1},{9,5},{13,9},{2,14},{6,2},{... | collective-permute-start | bytes 1179656 | tf_op jit(solution)/shard_map/ppermute | solution.py:279
  9.7 33.5 %collective-permute-start.1 = (bf16[2,128,768]{2,1,0:T(8,128)(2,1)S(1)}, bf16[2,128,768]{2,1,0:T(8,128)(2,1)S(1)}, u32[]{:S(2)}, u32[]{:S(2)}) collective-permute-start(bf16[2,128,768]{2,1,0:T(8,128)(2,1)S(1)} %get-tuple-element.45), channel_id=1, source_target_pairs={{0,8},{4,12},{8,0},{12,4},{1,9},{5,13},{9,1},{13,5},{2,10},{6,14},... | collective-permute-start | bytes 1179656 | tf_op jit(solution)/shard_map/ppermute | solution.py:279
  11.6 31.6 %collective-permute-start = (bf16[2,128,768]{2,1,0:T(8,128)(2,1)S(1)}, bf16[2,128,768]{2,1,0:T(8,128)(2,1)S(1)}, u32[]{:S(2)}, u32[]{:S(2)}) collective-permute-start(bf16[2,128,768]{2,1,0:T(8,128)(2,1)S(1)} %get-tuple-element.46), channel_id=1, source_target_pairs={{0,4},{4,8},{8,12},{12,0},{1,5},{5,9},{9,13},{13,1},{2,6},{6,10},{... | collective-permute-start | bytes 1179656 | tf_op jit(solution)/shard_map/ppermute | solution.py:279
  44.3 37.3 %collective-permute-start.3 = (bf16[2,512,768]{2,1,0:T(8,128)(2,1)S(1)}, bf16[2,512,768]{2,1,0:T(8,128)(2,1)}, u32[]{:S(2)}, u32[]{:S(2)}) collective-permute-start(bf16[2,512,768]{2,1,0:T(8,128)(2,1)S(1)} %fusion.17), channel_id=1, source_target_pairs={{0,2},{1,3},{2,0},{3,1},{4,6},{5,7},{6,4},{7,5},{8,10},{9,11},{10,... | collective-permute-start | bytes 4718600 | tf_op jit(solution)/shard_map/ppermute | solution.py:296
  47.9 227.4 %copy-start.2 = (bf16[768,768]{1,0:T(8,128)(2,1)}, bf16[768,768]{1,0:T(8,128)(2,1)S(1)}, u32[]{:S(2)}) copy-start(bf16[768,768]{1,0:T(8,128)(2,1)S(1)} %pad_maximum_fusion.5.refs_0_.refs_13_) | copy-start | bytes 3538948
  47.9 29.1 %collective-permute-start.5 = (bf16[768,768]{1,0:T(8,128)(2,1)S(1)}, bf16[768,768]{1,0:T(8,128)(2,1)}, u32[]{:S(2)}, u32[]{:S(2)}) collective-permute-start(bf16[768,768]{1,0:T(8,128)(2,1)S(1)} %pad_maximum_fusion.5.refs_0_.refs_13_), channel_id=1, source_target_pairs={{0,4},{4,0},{8,12},{12,8},{1,5},{5,1},{9,13},{13,9},{2,6},{6,2},{1... | collective-permute-start | bytes 3538952 | tf_op jit(solution)/shard_map/ppermute | solution.py:329
  49.6 29.0 %collective-permute-start.6 = (bf16[768,768]{1,0:T(8,128)(2,1)S(1)}, bf16[768,768]{1,0:T(8,128)(2,1)}, u32[]{:S(2)}, u32[]{:S(2)}) collective-permute-start(bf16[768,768]{1,0:T(8,128)(2,1)S(1)} %pad_maximum_fusion.5.refs_0_.refs_13_), channel_id=1, source_target_pairs={{4,8},{8,4},{5,9},{9,5},{6,10},{10,6},{7,11},{11,7},{20,24},{24,20... | collective-permute-start | bytes 3538952 | tf_op jit(solution)/shard_map/ppermute | solution.py:329
  51.4 232.3 %copy-start.3 = (bf16[768,768]{1,0:T(8,128)(2,1)}, bf16[768,768]{1,0:T(8,128)(2,1)S(1)}, u32[]{:S(2)}) copy-start(bf16[768,768]{1,0:T(8,128)(2,1)S(1)} %pad_maximum_fusion.6.refs_0_.refs_17_) | copy-start | bytes 3538948
  51.4 50.9 %collective-permute-start.10 = (bf16[768,768]{1,0:T(8,128)(2,1)S(1)}, bf16[768,768]{1,0:T(8,128)(2,1)}, u32[]{:S(2)}, u32[]{:S(2)}) collective-permute-start(bf16[768,768]{1,0:T(8,128)(2,1)S(1)} %pad_maximum_fusion.6.refs_0_.refs_17_), channel_id=1, source_target_pairs={{0,4},{4,0},{8,12},{12,8},{1,5},{5,1},{9,13},{13,9},{2,6},{6,2},{1... | collective-permute-start | bytes 3538952 | tf_op jit(solution)/shard_map/ppermute | solution.py:329
  54.2 50.0 %collective-permute-start.11 = (bf16[768,768]{1,0:T(8,128)(2,1)S(1)}, bf16[768,768]{1,0:T(8,128)(2,1)}, u32[]{:S(2)}, u32[]{:S(2)}) collective-permute-start(bf16[768,768]{1,0:T(8,128)(2,1)S(1)} %pad_maximum_fusion.6.refs_0_.refs_17_), channel_id=1, source_target_pairs={{4,8},{8,4},{5,9},{9,5},{6,10},{10,6},{7,11},{11,7},{20,24},{24,20... | collective-permute-start | bytes 3538952 | tf_op jit(solution)/shard_map/ppermute | solution.py:329
  55.9 276.4 %copy-start.4 = (bf16[768,768]{1,0:T(8,128)(2,1)}, bf16[768,768]{1,0:T(8,128)(2,1)S(1)}, u32[]{:S(2)}) copy-start(bf16[768,768]{1,0:T(8,128)(2,1)S(1)} %pad_maximum_fusion.7.refs_0_.refs_21_) | copy-start | bytes 3538948
  77.0 50.6 %collective-permute-start.15 = (bf16[768,768]{1,0:T(8,128)(2,1)S(1)}, bf16[768,768]{1,0:T(8,128)(2,1)}, u32[]{:S(2)}, u32[]{:S(2)}) collective-permute-start(bf16[768,768]{1,0:T(8,128)(2,1)S(1)} %pad_maximum_fusion.7.refs_0_.refs_21_), channel_id=1, source_target_pairs={{0,4},{4,0},{8,12},{12,8},{1,5},{5,1},{9,13},{13,9},{2,6},{6,2},{1... | collective-permute-start | bytes 3538952 | tf_op jit(solution)/shard_map/ppermute | solution.py:329
  78.6 50.6 %collective-permute-start.16 = (bf16[768,768]{1,0:T(8,128)(2,1)S(1)}, bf16[768,768]{1,0:T(8,128)(2,1)}, u32[]{:S(2)}, u32[]{:S(2)}) collective-permute-start(bf16[768,768]{1,0:T(8,128)(2,1)S(1)} %pad_maximum_fusion.7.refs_0_.refs_21_), channel_id=1, source_target_pairs={{4,8},{8,4},{5,9},{9,5},{6,10},{10,6},{7,11},{11,7},{20,24},{24,20... | collective-permute-start | bytes 3538952 | tf_op jit(solution)/shard_map/ppermute | solution.py:329
  81.5 49.3 %collective-permute-start.8 = (bf16[768,768]{1,0:T(8,128)(2,1)}, bf16[768,768]{1,0:T(8,128)(2,1)}, u32[]{:S(2)}, u32[]{:S(2)}) collective-permute-start(bf16[768,768]{1,0:T(8,128)(2,1)} %collective-permute-done.5.refs_1_.refs_14_), channel_id=1, source_target_pairs={{4,8},{8,4},{5,9},{9,5},{6,10},{10,6},{7,11},{11,7},{20,24},{24,20... | collective-permute-start | bytes 3538952 | tf_op jit(solution)/shard_map/ppermute | solution.py:329
  85.3 71.4 %copy-start.35 = (f32[1,2,128]{2,1,0:T(2,128)S(1)}, f32[1,2,128]{2,1,0:T(2,128)}, u32[]{:S(2)}) copy-start(f32[1,2,128]{2,1,0:T(2,128)} %param.11) | copy-start | bytes 3076
  102.2 154.7 %collective-permute-start.4 = (bf16[2,2,512,768]{3,2,1,0:T(8,128)(2,1)}, bf16[2,2,512,768]{3,2,1,0:T(8,128)(2,1)}, u32[]{:S(2)}, u32[]{:S(2)}) collective-permute-start(bf16[2,2,512,768]{3,2,1,0:T(8,128)(2,1)} %pad_maximum_fusion), channel_id=1, source_target_pairs={{0,1},{1,0},{2,3},{3,2},{4,5},{5,4},{6,7},{7,6},{8,9},{9,8},{10,11... | collective-permute-start | bytes 9437192 | tf_op jit(solution)/shard_map/ppermute | solution.py:296
  104.2 53.2 %collective-permute-start.7 = (bf16[768,768]{1,0:T(8,128)(2,1)}, bf16[768,768]{1,0:T(8,128)(2,1)}, u32[]{:S(2)}, u32[]{:S(2)}) collective-permute-start(bf16[768,768]{1,0:T(8,128)(2,1)} %collective-permute-done.6), channel_id=1, source_target_pairs={{0,4},{4,0},{8,12},{12,8},{1,5},{5,1},{9,13},{13,9},{2,6},{6,2},{1... | collective-permute-start | bytes 3538952 | tf_op jit(solution)/shard_map/ppermute | solution.py:329
  127.5 50.6 %collective-permute-start.12 = (bf16[768,768]{1,0:T(8,128)(2,1)}, bf16[768,768]{1,0:T(8,128)(2,1)}, u32[]{:S(2)}, u32[]{:S(2)}) collective-permute-start(bf16[768,768]{1,0:T(8,128)(2,1)} %collective-permute-done.11), channel_id=1, source_target_pairs={{0,4},{4,0},{8,12},{12,8},{1,5},{5,1},{9,13},{13,9},{2,6},{6,2},{1... | collective-permute-start | bytes 3538952 | tf_op jit(solution)/shard_map/ppermute | solution.py:329
  129.1 50.7 %collective-permute-start.13 = (bf16[768,768]{1,0:T(8,128)(2,1)}, bf16[768,768]{1,0:T(8,128)(2,1)}, u32[]{:S(2)}, u32[]{:S(2)}) collective-permute-start(bf16[768,768]{1,0:T(8,128)(2,1)} %collective-permute-done.10.refs_1_.refs_18_), channel_id=1, source_target_pairs={{4,8},{8,4},{5,9},{9,5},{6,10},{10,6},{7,11},{11,7},{20,24},{24,20... | collective-permute-start | bytes 3538952 | tf_op jit(solution)/shard_map/ppermute | solution.py:329
  130.8 72.5 %collective-permute-start.9 = (bf16[768,768]{1,0:T(8,128)(2,1)}, bf16[768,768]{1,0:T(8,128)(2,1)}, u32[]{:S(2)}, u32[]{:S(2)}) collective-permute-start(bf16[768,768]{1,0:T(8,128)(2,1)} %collective-permute-done.8), channel_id=1, source_target_pairs={{0,4},{4,0},{8,12},{12,8},{1,5},{5,1},{9,13},{13,9},{2,6},{6,2},{1... | collective-permute-start | bytes 3538952 | tf_op jit(solution)/shard_map/ppermute | solution.py:329
  157.3 71.3 %collective-permute-start.20 = (bf16[768,768]{1,0:T(8,128)(2,1)}, bf16[768,768]{1,0:T(8,128)(2,1)}, u32[]{:S(2)}, u32[]{:S(2)}) collective-permute-start(bf16[768,768]{1,0:T(8,128)(2,1)} %bitcast.226), channel_id=1, source_target_pairs={{0,4},{4,0},{8,12},{12,8},{1,5},{5,1},{9,13},{13,9},{2,6},{6,2},{1... | collective-permute-start | bytes 3538952 | tf_op jit(solution)/shard_map/ppermute | solution.py:329
  178.1 52.1 %collective-permute-start.21 = (bf16[768,768]{1,0:T(8,128)(2,1)}, bf16[768,768]{1,0:T(8,128)(2,1)}, u32[]{:S(2)}, u32[]{:S(2)}) collective-permute-start(bf16[768,768]{1,0:T(8,128)(2,1)} %bitcast.227), channel_id=1, source_target_pairs={{4,8},{8,4},{5,9},{9,5},{6,10},{10,6},{7,11},{11,7},{20,24},{24,20... | collective-permute-start | bytes 3538952 | tf_op jit(solution)/shard_map/ppermute | solution.py:329
  179.8 50.9 %collective-permute-start.18 = (bf16[768,768]{1,0:T(8,128)(2,1)}, bf16[768,768]{1,0:T(8,128)(2,1)}, u32[]{:S(2)}, u32[]{:S(2)}) collective-permute-start(bf16[768,768]{1,0:T(8,128)(2,1)} %collective-permute-done.15.refs_1_.refs_22_), channel_id=1, source_target_pairs={{4,8},{8,4},{5,9},{9,5},{6,10},{10,6},{7,11},{11,7},{20,24},{24,20... | collective-permute-start | bytes 3538952 | tf_op jit(solution)/shard_map/ppermute | solution.py:329
  203.4 50.6 %collective-permute-start.14 = (bf16[768,768]{1,0:T(8,128)(2,1)}, bf16[768,768]{1,0:T(8,128)(2,1)}, u32[]{:S(2)}, u32[]{:S(2)}) collective-permute-start(bf16[768,768]{1,0:T(8,128)(2,1)} %collective-permute-done.13), channel_id=1, source_target_pairs={{0,4},{4,0},{8,12},{12,8},{1,5},{5,1},{9,13},{13,9},{2,6},{6,2},{1... | collective-permute-start | bytes 3538952 | tf_op jit(solution)/shard_map/ppermute | solution.py:329
  205.0 127.3 %copy-start.11 = (s32[4]{0:T(128)}, s32[4]{0:T(128)S(1)}, u32[]{:S(2)}) copy-start(s32[4]{0:T(128)S(1)} %pad_add_fusion.source_ref) | copy-start | bytes 52
  207.1 68.2 %copy-start.5 = (bf16[768,768]{1,0:T(8,128)(2,1)}, bf16[768,768]{1,0:T(8,128)(2,1)S(1)}, u32[]{:S(2)}) copy-start(bf16[768,768]{1,0:T(8,128)(2,1)S(1)} %broadcast_select_fusion.13.refs_2_.refs_15_) | copy-start | bytes 3538948
  209.0 74.8 %copy-start.6 = (bf16[768,768]{1,0:T(8,128)(2,1)}, bf16[768,768]{1,0:T(8,128)(2,1)S(1)}, u32[]{:S(2)}) copy-start(bf16[768,768]{1,0:T(8,128)(2,1)S(1)} %broadcast_select_fusion.11.refs_2_.refs_19_) | copy-start | bytes 3538948
  210.8 64.5 %copy-start.7 = (bf16[768,768]{1,0:T(8,128)(2,1)}, bf16[768,768]{1,0:T(8,128)(2,1)S(1)}, u32[]{:S(2)}) copy-start(bf16[768,768]{1,0:T(8,128)(2,1)S(1)} %broadcast_select_fusion.12.refs_3_.refs_16_) | copy-start | bytes 3538948
  210.8 46.1 %copy-start.16 = (bf16[1,2,512,768]{3,2,1,0:T(8,128)(2,1)S(1)}, bf16[1,2,512,768]{3,2,1,0:T(8,128)(2,1)}, u32[]{:S(2)}) copy-start(bf16[1,2,512,768]{3,2,1,0:T(8,128)(2,1)} %copy-done.15) | copy-start | bytes 4718596
  210.8 46.1 %copy-start.18 = (bf16[1,2,512,768]{3,2,1,0:T(8,128)(2,1)S(1)}, bf16[1,2,512,768]{3,2,1,0:T(8,128)(2,1)}, u32[]{:S(2)}) copy-start(bf16[1,2,512,768]{3,2,1,0:T(8,128)(2,1)} %copy-done.17) | copy-start | bytes 4718596
  228.6 64.7 %collective-permute-start.17 = (bf16[768,768]{1,0:T(8,128)(2,1)}, bf16[768,768]{1,0:T(8,128)(2,1)}, u32[]{:S(2)}, u32[]{:S(2)}) collective-permute-start(bf16[768,768]{1,0:T(8,128)(2,1)} %collective-permute-done.16), channel_id=1, source_target_pairs={{0,4},{4,0},{8,12},{12,8},{1,5},{5,1},{9,13},{13,9},{2,6},{6,2},{1... | collective-permute-start | bytes 3538952 | tf_op jit(solution)/shard_map/ppermute | solution.py:329
  230.2 74.2 %collective-permute-start.22 = (bf16[768,768]{1,0:T(8,128)(2,1)}, bf16[768,768]{1,0:T(8,128)(2,1)}, u32[]{:S(2)}, u32[]{:S(2)}) collective-permute-start(bf16[768,768]{1,0:T(8,128)(2,1)} %collective-permute-done.21), channel_id=1, source_target_pairs={{0,4},{4,0},{8,12},{12,8},{1,5},{5,1},{9,13},{13,9},{2,6},{6,2},{1... | collective-permute-start | bytes 3538952 | tf_op jit(solution)/shard_map/ppermute | solution.py:329
  230.7 62.2 %collective-permute-start.23 = (bf16[768,768]{1,0:T(8,128)(2,1)}, bf16[768,768]{1,0:T(8,128)(2,1)}, u32[]{:S(2)}, u32[]{:S(2)}) collective-permute-start(bf16[768,768]{1,0:T(8,128)(2,1)} %collective-permute-done.20.refs_10_), channel_id=1, source_target_pairs={{4,8},{8,4},{5,9},{9,5},{6,10},{10,6},{7,11},{11,7},{20,24},{24,20... | collective-permute-start | bytes 3538952 | tf_op jit(solution)/shard_map/ppermute | solution.py:329
  253.9 75.8 %collective-permute-start.19 = (bf16[768,768]{1,0:T(8,128)(2,1)}, bf16[768,768]{1,0:T(8,128)(2,1)}, u32[]{:S(2)}, u32[]{:S(2)}) collective-permute-start(bf16[768,768]{1,0:T(8,128)(2,1)} %collective-permute-done.18), channel_id=1, source_target_pairs={{0,4},{4,0},{8,12},{12,8},{1,5},{5,1},{9,13},{13,9},{2,6},{6,2},{1... | collective-permute-start | bytes 3538952 | tf_op jit(solution)/shard_map/ppermute | solution.py:329
  256.9 26.8 %copy-start.8 = (bf16[768,768]{1,0:T(8,128)(2,1)}, bf16[768,768]{1,0:T(8,128)(2,1)S(1)}, u32[]{:S(2)}) copy-start(bf16[768,768]{1,0:T(8,128)(2,1)S(1)} %broadcast_select_fusion.10.refs_3_.refs_20_) | copy-start | bytes 3538948
  292.9 60.7 %collective-permute-start.24 = (bf16[768,768]{1,0:T(8,128)(2,1)}, bf16[768,768]{1,0:T(8,128)(2,1)}, u32[]{:S(2)}, u32[]{:S(2)}) collective-permute-start(bf16[768,768]{1,0:T(8,128)(2,1)} %collective-permute-done.23), channel_id=1, source_target_pairs={{0,4},{4,0},{8,12},{12,8},{1,5},{5,1},{9,13},{13,9},{2,6},{6,2},{1... | collective-permute-start | bytes 3538952 | tf_op jit(solution)/shard_map/ppermute | solution.py:329
  295.4 37.0 %copy-start.9 = (bf16[768,768]{1,0:T(8,128)(2,1)}, bf16[768,768]{1,0:T(8,128)(2,1)S(1)}, u32[]{:S(2)}) copy-start(bf16[768,768]{1,0:T(8,128)(2,1)S(1)} %broadcast_select_fusion.9.refs_2_.refs_23_) | copy-start | bytes 3538948
  369.1 1.8 collective-permute-start.25
  374.1 1.5 collective-permute-start.26
  378.1 14.4 %collective-permute-start.32 = (bf16[1,128,768]{1,2,0:T(8,128)(2,1)S(1)}, bf16[1,128,768]{1,2,0:T(8,128)(2,1)S(1)}, u32[]{:S(2)}, u32[]{:S(2)}) collective-permute-start(bf16[1,128,768]{1,2,0:T(8,128)(2,1)S(1)} %get-tuple-element.65), channel_id=1, source_target_pairs={{16,12},{20,0},{24,4},{28,8},{17,13},{21,1},{25,5},{29,9},{18,14},... | collective-permute-start | bytes 589832 | tf_op jit(solution)/shard_map/ppermute | solution.py:279
  379.4 26.5 %collective-permute-start.31 = (bf16[1,128,768]{1,2,0:T(8,128)(2,1)S(1)}, bf16[1,128,768]{1,2,0:T(8,128)(2,1)S(1)}, u32[]{:S(2)}, u32[]{:S(2)}) collective-permute-start(bf16[1,128,768]{1,2,0:T(8,128)(2,1)S(1)} %get-tuple-element.66), channel_id=1, source_target_pairs={{16,8},{20,12},{24,0},{28,4},{17,9},{21,13},{25,1},{29,5},{18,10},... | collective-permute-start | bytes 589832 | tf_op jit(solution)/shard_map/ppermute | solution.py:279
  380.7 25.2 %collective-permute-start.30 = (bf16[1,128,768]{1,2,0:T(8,128)(2,1)S(1)}, bf16[1,128,768]{1,2,0:T(8,128)(2,1)S(1)}, u32[]{:S(2)}, u32[]{:S(2)}) collective-permute-start(bf16[1,128,768]{1,2,0:T(8,128)(2,1)S(1)} %get-tuple-element.67), channel_id=1, source_target_pairs={{16,4},{20,8},{24,12},{28,0},{17,5},{21,9},{25,13},{29,1},{18,6},{... | collective-permute-start | bytes 589832 | tf_op jit(solution)/shard_map/ppermute | solution.py:279
  382.0 23.9 %collective-permute-start.29 = (bf16[1,128,768]{1,2,0:T(8,128)(2,1)S(1)}, bf16[1,128,768]{1,2,0:T(8,128)(2,1)S(1)}, u32[]{:S(2)}, u32[]{:S(2)}) collective-permute-start(bf16[1,128,768]{1,2,0:T(8,128)(2,1)S(1)} %get-tuple-element.64), channel_id=1, source_target_pairs={{16,0},{20,4},{24,8},{28,12},{17,1},{21,5},{25,9},{29,13},{18,2},{... | collective-permute-start | bytes 589832 | tf_op jit(solution)/shard_map/ppermute | solution.py:279
  386.4 44.1 %collective-permute-start.27 = (bf16[2,512,768]{2,1,0:T(8,128)(2,1)S(1)}, bf16[2,512,768]{2,1,0:T(8,128)(2,1)S(1)}, u32[]{:S(2)}, u32[]{:S(2)}) collective-permute-start(bf16[2,512,768]{2,1,0:T(8,128)(2,1)S(1)} %dynamic-slice_bitcast_fusion.2), channel_id=1, source_target_pairs={{16,17},{17,16},{18,19},{19,18},{20,21},{21,20},{22,23},{23,22},{2... | collective-permute-start | bytes 4718600 | tf_op jit(solution)/shard_map/ppermute | solution.py:296
  406.6 20.1 %copy-start.28 = (bf16[512,768]{1,0:T(8,128)(2,1)}, bf16[512,768]{1,0:T(8,128)(2,1)S(1)}, u32[]{:S(2)}) copy-start(bf16[512,768]{1,0:T(8,128)(2,1)S(1)} %fusion.21) | copy-start | bytes 2359300
  406.6 20.0 %collective-permute-start.33 = (bf16[512,768]{1,0:T(8,128)(2,1)S(1)}, bf16[512,768]{1,0:T(8,128)(2,1)S(1)}, u32[]{:S(2)}, u32[]{:S(2)}) collective-permute-start(bf16[512,768]{1,0:T(8,128)(2,1)S(1)} %fusion.21), channel_id=1, source_target_pairs={{0,2},{1,3},{2,0},{3,1},{4,6},{5,7},{6,4},{7,5},{8,10},{9,11},{10,... | collective-permute-start | bytes 2359304 | tf_op jit(solution)/shard_map/ppermute | solution.py:296
  428.5 12.7 %collective-permute-start.34 = (bf16[2,512,768]{2,1,0:T(8,128)(2,1)}, bf16[2,512,768]{2,1,0:T(8,128)(2,1)}, u32[]{:S(2)}, u32[]{:S(2)}) collective-permute-start(bf16[2,512,768]{2,1,0:T(8,128)(2,1)} %pad_maximum_fusion.3), channel_id=1, source_target_pairs={{0,1},{1,0},{2,3},{3,2},{4,5},{5,4},{6,7},{7,6},{8,9},{9,8},{10,11... | collective-permute-start | bytes 4718600 | tf_op jit(solution)/shard_map/ppermute | solution.py:296
  431.8 1.6 collective-permute-start.28
  436.0 31.0 %collective-permute-start.40 = (bf16[1,128,768]{1,2,0:T(8,128)(2,1)S(1)}, bf16[1,128,768]{1,2,0:T(8,128)(2,1)S(1)}, u32[]{:S(2)}, u32[]{:S(2)}) collective-permute-start(bf16[1,128,768]{1,2,0:T(8,128)(2,1)S(1)} %get-tuple-element.71), channel_id=1, source_target_pairs={{16,0},{20,4},{24,8},{28,12},{17,1},{21,5},{25,9},{29,13},{18,2},{... | collective-permute-start | bytes 589832 | tf_op jit(solution)/shard_map/ppermute | solution.py:279
  437.3 29.7 %collective-permute-start.41 = (bf16[1,128,768]{1,2,0:T(8,128)(2,1)S(1)}, bf16[1,128,768]{1,2,0:T(8,128)(2,1)S(1)}, u32[]{:S(2)}, u32[]{:S(2)}) collective-permute-start(bf16[1,128,768]{1,2,0:T(8,128)(2,1)S(1)} %get-tuple-element.70), channel_id=1, source_target_pairs={{16,4},{20,8},{24,12},{28,0},{17,5},{21,9},{25,13},{29,1},{18,6},{... | collective-permute-start | bytes 589832 | tf_op jit(solution)/shard_map/ppermute | solution.py:279
  438.6 28.5 %collective-permute-start.42 = (bf16[1,128,768]{1,2,0:T(8,128)(2,1)S(1)}, bf16[1,128,768]{1,2,0:T(8,128)(2,1)S(1)}, u32[]{:S(2)}, u32[]{:S(2)}) collective-permute-start(bf16[1,128,768]{1,2,0:T(8,128)(2,1)S(1)} %get-tuple-element.69), channel_id=1, source_target_pairs={{16,8},{20,12},{24,0},{28,4},{17,9},{21,13},{25,1},{29,5},{18,10},... | collective-permute-start | bytes 589832 | tf_op jit(solution)/shard_map/ppermute | solution.py:279
  439.9 27.2 %collective-permute-start.43 = (bf16[1,128,768]{1,2,0:T(8,128)(2,1)S(1)}, bf16[1,128,768]{1,2,0:T(8,128)(2,1)S(1)}, u32[]{:S(2)}, u32[]{:S(2)}) collective-permute-start(bf16[1,128,768]{1,2,0:T(8,128)(2,1)S(1)} %get-tuple-element.68), channel_id=1, source_target_pairs={{16,12},{20,0},{24,4},{28,8},{17,13},{21,1},{25,5},{29,9},{18,14},... | collective-permute-start | bytes 589832 | tf_op jit(solution)/shard_map/ppermute | solution.py:279
  467.7 21.8 %collective-permute-start.44 = (bf16[512,768]{1,0:T(8,128)(2,1)S(1)}, bf16[512,768]{1,0:T(8,128)(2,1)S(1)}, u32[]{:S(2)}, u32[]{:S(2)}) collective-permute-start(bf16[512,768]{1,0:T(8,128)(2,1)S(1)} %fusion.24), channel_id=1, source_target_pairs={{0,2},{1,3},{2,0},{3,1},{4,6},{5,7},{6,4},{7,5},{8,10},{9,11},{10,... | collective-permute-start | bytes 2359304 | tf_op jit(solution)/shard_map/ppermute | solution.py:296
  489.8 5.9 collective-permute-start.45
  493.2 29.9 %collective-permute-start.35 = (bf16[2,512,768]{2,1,0:T(8,128)(2,1)}, bf16[2,512,768]{2,1,0:T(8,128)(2,1)}, u32[]{:S(2)}, u32[]{:S(2)}) collective-permute-start(bf16[2,512,768]{2,1,0:T(8,128)(2,1)} %dynamic-slice_bitcast_fusion.1), channel_id=1, source_target_pairs={{0,1},{1,0},{2,3},{3,2},{4,5},{5,4},{6,7},{7,6},{8,9},{9,8},{10,11... | collective-permute-start | bytes 4718600 | tf_op jit(solution)/shard_map/ppermute | solution.py:296
  521.2 7.4 %collective-permute-start.46 = (bf16[2,512,768]{2,1,0:T(8,128)(2,1)S(1)}, bf16[2,512,768]{2,1,0:T(8,128)(2,1)S(1)}, u32[]{:S(2)}, u32[]{:S(2)}) collective-permute-start(bf16[2,512,768]{2,1,0:T(8,128)(2,1)S(1)} %dynamic-slice_bitcast_fusion), channel_id=1, source_target_pairs={{0,1},{1,0},{2,3},{3,2},{4,5},{5,4},{6,7},{7,6},{8,9},{9,8},{10,11... | collective-permute-start | bytes 4718600 | tf_op jit(solution)/shard_map/ppermute | solution.py:296
  525.2 22.2 %collective-permute-start.36 = (bf16[512,768]{1,0:T(8,128)(2,1)S(1)}, bf16[512,768]{1,0:T(8,128)(2,1)S(1)}, u32[]{:S(2)}, u32[]{:S(2)}) collective-permute-start(bf16[512,768]{1,0:T(8,128)(2,1)S(1)} %fusion.32), channel_id=1, source_target_pairs={{0,2},{1,3},{2,0},{3,1},{4,6},{5,7},{6,4},{7,5},{8,10},{9,11},{10,... | collective-permute-start | bytes 2359304 | tf_op jit(solution)/shard_map/ppermute | solution.py:296
  529.1 34.8 %collective-permute-start.47 = (bf16[512,768]{1,0:T(8,128)(2,1)S(1)}, bf16[512,768]{1,0:T(8,128)(2,1)S(1)}, u32[]{:S(2)}, u32[]{:S(2)}) collective-permute-start(bf16[512,768]{1,0:T(8,128)(2,1)S(1)} %fusion.33), channel_id=1, source_target_pairs={{0,2},{1,3},{2,0},{3,1},{4,6},{5,7},{6,4},{7,5},{8,10},{9,11},{10,... | collective-permute-start | bytes 2359304 | tf_op jit(solution)/shard_map/ppermute | solution.py:296
  548.2 24.8 %collective-permute-start.39 = (bf16[1,128,768]{2,1,0:T(8,128)(2,1)S(1)}, bf16[1,128,768]{2,1,0:T(8,128)(2,1)S(1)}, u32[]{:S(2)}, u32[]{:S(2)}) collective-permute-start(bf16[1,128,768]{2,1,0:T(8,128)(2,1)S(1)} %get-tuple-element.57), channel_id=1, source_target_pairs={{0,12},{4,0},{8,4},{12,8},{1,13},{5,1},{9,5},{13,9},{2,14},{6,2},{... | collective-permute-start | bytes 589832 | tf_op jit(solution)/shard_map/ppermute | solution.py:279
  552.4 22.6 %collective-permute-start.38 = (bf16[1,128,768]{2,1,0:T(8,128)(2,1)S(1)}, bf16[1,128,768]{2,1,0:T(8,128)(2,1)S(1)}, u32[]{:S(2)}, u32[]{:S(2)}) collective-permute-start(bf16[1,128,768]{2,1,0:T(8,128)(2,1)S(1)} %get-tuple-element.58), channel_id=1, source_target_pairs={{0,8},{4,12},{8,0},{12,4},{1,9},{5,13},{9,1},{13,5},{2,10},{6,14},... | collective-permute-start | bytes 589832 | tf_op jit(solution)/shard_map/ppermute | solution.py:279
  556.6 18.4 %collective-permute-start.37 = (bf16[1,128,768]{2,1,0:T(8,128)(2,1)S(1)}, bf16[1,128,768]{2,1,0:T(8,128)(2,1)S(1)}, u32[]{:S(2)}, u32[]{:S(2)}) collective-permute-start(bf16[1,128,768]{2,1,0:T(8,128)(2,1)S(1)} %get-tuple-element.59), channel_id=1, source_target_pairs={{0,4},{4,8},{8,12},{12,0},{1,5},{5,9},{9,13},{13,1},{2,6},{6,10},{... | collective-permute-start | bytes 589832 | tf_op jit(solution)/shard_map/ppermute | solution.py:279
  564.6 11.4 %collective-permute-start.50 = (bf16[1,128,768]{2,1,0:T(8,128)(2,1)S(1)}, bf16[1,128,768]{2,1,0:T(8,128)(2,1)S(1)}, u32[]{:S(2)}, u32[]{:S(2)}) collective-permute-start(bf16[1,128,768]{2,1,0:T(8,128)(2,1)S(1)} %get-tuple-element.61), channel_id=1, source_target_pairs={{0,12},{4,0},{8,4},{12,8},{1,13},{5,1},{9,5},{13,9},{2,14},{6,2},{... | collective-permute-start | bytes 589832 | tf_op jit(solution)/shard_map/ppermute | solution.py:279
  568.8 19.5 %collective-permute-start.49 = (bf16[1,128,768]{2,1,0:T(8,128)(2,1)S(1)}, bf16[1,128,768]{2,1,0:T(8,128)(2,1)S(1)}, u32[]{:S(2)}, u32[]{:S(2)}) collective-permute-start(bf16[1,128,768]{2,1,0:T(8,128)(2,1)S(1)} %get-tuple-element.62), channel_id=1, source_target_pairs={{0,8},{4,12},{8,0},{12,4},{1,9},{5,13},{9,1},{13,5},{2,10},{6,14},... | collective-permute-start | bytes 589832 | tf_op jit(solution)/shard_map/ppermute | solution.py:279
  573.0 15.2 %collective-permute-start.48 = (bf16[1,128,768]{2,1,0:T(8,128)(2,1)S(1)}, bf16[1,128,768]{2,1,0:T(8,128)(2,1)S(1)}, u32[]{:S(2)}, u32[]{:S(2)}) collective-permute-start(bf16[1,128,768]{2,1,0:T(8,128)(2,1)S(1)} %get-tuple-element.63), channel_id=1, source_target_pairs={{0,4},{4,8},{8,12},{12,0},{1,5},{5,9},{9,13},{13,1},{2,6},{6,10},{... | collective-permute-start | bytes 589832 | tf_op jit(solution)/shard_map/ppermute | solution.py:279
  (25 other events, 145.2 us)
